TPU v7x, 32 devices: a whole 2x2x4 slice. The times are simulated.
32 devices in a mesh: utt: 2 (over y), seq: 16 (over z, x, core).
Axes of the slice: x: 2, y: 2, z: 4, core: 2. Of those that a mesh axis runs over, the one named last changes fastest.
Arguments:
- frames: bfloat16 [4, 1024, 1024], P('utt', 'seq'), may hold values from -8 to 8
- codes: int32 [4, 1024, 3], P('utt', 'seq'), may hold values from 0 to 1023
- lengths: int32 [4], P('utt'), may hold values from 256 to 1024, as said below
- frame_mask: int32 [4, 1024], P('utt', 'seq'), may hold values 0 or 1
- table: bfloat16 [3072, 1024], replicated, may hold values from -6 to 6
- glob_norm_one: float32 [1024], replicated, may hold values from 0.1 to 1.9
- glob_w_query: bfloat16 [1024, 1024], replicated, may hold values from -0.1875 to 0.1875
- glob_w_key: bfloat16 [1024, 1024], replicated, may hold values from -0.1875 to 0.1875
- glob_w_value: bfloat16 [1024, 1024], replicated, may hold values from -0.1875 to 0.1875
- glob_w_output: bfloat16 [1024, 1024], replicated, may hold values from -0.75 to 0.75
- glob_norm_two: float32 [1024], replicated, may hold values from 0.1 to 1.9
- glob_w_up: bfloat16 [1024, 4096], replicated, may hold values from -0.1875 to 0.1875
- glob_b_up: float32 [4096], replicated, may hold values from -3 to 3
- glob_w_down: bfloat16 [4096, 1024], replicated, may hold values from -0.09375 to 0.09375
- glob_b_down: float32 [1024], replicated, may hold values from -1.75 to 1.75
- local_norm_one: float32 [1024], replicated, may hold values from 0.1 to 1.9
- local_w_query: bfloat16 [1024, 1024], replicated, may hold values from -0.1875 to 0.1875
- local_w_key: bfloat16 [1024, 1024], replicated, may hold values from -0.1875 to 0.1875
- local_w_value: bfloat16 [1024, 1024], replicated, may hold values from -0.1875 to 0.1875
- local_w_output: bfloat16 [1024, 1024], replicated, may hold values from -0.25 to 0.25
- local_norm_two: float32 [1024], replicated, may hold values from 0.1 to 1.9
- local_w_up: bfloat16 [1024, 4096], replicated, may hold values from -0.1875 to 0.1875
- local_b_up: float32 [4096], replicated, may hold values from -3 to 3
- local_w_down: bfloat16 [4096, 1024], replicated, may hold values from -0.09375 to 0.09375
- local_b_down: float32 [1024], replicated, may hold values from -1.75 to 1.75
- cotan_global: bfloat16 [4, 1024, 1024], P('utt', 'seq'), may hold values from -8 to 8
- cotan_local: bfloat16 [4, 1024, 4, 1024], P('utt', 'seq'), may hold values from -8 to 8
Outputs:
- global_out: bfloat16 [4, 1024, 1024], P('utt', 'seq')
- local_out: bfloat16 [4, 1024, 4, 1024], P('utt', 'seq')
- grad_frames: float32 [4, 1024, 1024], P('utt', 'seq')
- grad_table: float32 [3072, 1024], P('seq')
- grad_glob_norm_one: float32 [1024], P('seq')
- grad_glob_w_query: float32 [1024, 1024], P('seq')
- grad_glob_w_key: float32 [1024, 1024], P('seq')
- grad_glob_w_value: float32 [1024, 1024], P('seq')
- grad_glob_w_output: float32 [1024, 1024], P('seq')
- grad_glob_norm_two: float32 [1024], P('seq')
- grad_glob_w_up: float32 [1024, 4096], P('seq')
- grad_glob_b_up: float32 [4096], P('seq')
- grad_glob_w_down: float32 [4096, 1024], P('seq')
- grad_glob_b_down: float32 [1024], P('seq')
- grad_local_norm_one: float32 [1024], P('seq')
- grad_local_w_query: float32 [1024, 1024], P('seq')
- grad_local_w_key: float32 [1024, 1024], P('seq')
- grad_local_w_value: float32 [1024, 1024], P('seq')
- grad_local_w_output: float32 [1024, 1024], P('seq')
- grad_local_norm_two: float32 [1024], P('seq')
- grad_local_w_up: float32 [1024, 4096], P('seq')
- grad_local_b_up: float32 [4096], P('seq')
- grad_local_w_down: float32 [4096, 1024], P('seq')
- grad_local_b_down: float32 [1024], P('seq')
Inputs may be any that keep to these rules, and one draw needn't show every extreme that they name: `lengths`: in each aligned group of 2 utterances (those of one index of utt) exactly one, drawn from the seed, has 1024 valid frames; the others have 1024 // 4 or more.
All inputs are finite; a program needn't handle non-finite values. No bound on the sum of `frame_mask` on one device may be relied on, other than what follows from the above.
Results may differ from a plain program's by a relative error of at most 0.025.
Values may be sent and summed in bfloat16 or wider, within the bound.
A program may use at most 384 MiB of HBM per device.

v0:
```python
import jax
import jax.numpy as jnp
from jax import lax
from jax.sharding import PartitionSpec as P

H = 16
HD = 64
CB = 3
VOCAB = 1024


EPSILON = 1e-05
NEGATIVE = -1e30


def normalize(values, gain_vec):
    return (
        values * lax.rsqrt(jnp.mean(values * values, axis=-1, keepdims=True) + EPSILON) * gain_vec
    )


def gelu_fn(values):
    return jax.nn.gelu(values, approximate=True)


def softmax_rows(scores):
    row_peak = jnp.max(scores, axis=-1, keepdims=True)
    raised = jnp.exp(scores - row_peak)
    return raised / jnp.sum(raised, axis=-1, keepdims=True)


def project(left_side, weight):
    return jnp.dot(left_side, weight, preferred_element_type=jnp.float32)


def project_back(gradient, weight):
    return lax.dot_general(
        gradient, weight, (((1,), (1,)), ((), ())), preferred_element_type=jnp.float32
    )


def weight_grad(left_side, gradient):
    return lax.dot_general(
        left_side, gradient, (((0,), (0,)), ((), ())), preferred_element_type=jnp.float32
    )


def head_split(matrix):
    return matrix.reshape(matrix.shape[0], matrix.shape[1], H, HD)


def block_inputs(inputs, params):
    normed = normalize(inputs, params[0]).astype(jnp.bfloat16)
    queries = project(normed, params[1]).astype(jnp.bfloat16)
    key_rows = project(normed, params[2]).astype(jnp.bfloat16)
    value_rows = project(normed, params[3]).astype(jnp.bfloat16)
    return (normed, queries, key_rows, value_rows)


def block_outputs(inputs, mixed_rows, params):
    middle = inputs + project(mixed_rows, params[4])
    middle_norm = normalize(middle, params[5]).astype(jnp.bfloat16)
    pre_active = project(middle_norm, params[6]) + params[7]
    active = gelu_fn(pre_active).astype(jnp.bfloat16)
    result = middle + project(active, params[8]) + params[9]
    return (result, (middle, middle_norm, pre_active, active))


def block_back(inputs, front_parts, mixed_rows, kept_parts, params, grad_out, attention_back):
    normed, queries, key_rows, value_rows = front_parts
    middle, middle_norm, pre_active, active = kept_parts
    grad_branch = grad_out.astype(jnp.bfloat16)
    grad_b_down = jnp.sum(grad_branch.astype(jnp.float32), axis=0)
    grad_w_down = weight_grad(active, grad_branch)
    grad_active = project_back(grad_branch, params[8])
    grad_pre = jax.vjp(gelu_fn, pre_active)[1](grad_active)[0].astype(jnp.bfloat16)
    grad_b_up = jnp.sum(grad_pre.astype(jnp.float32), axis=0)
    grad_w_up = weight_grad(middle_norm, grad_pre)
    middle_back = jax.vjp(normalize, middle, params[5])[1]
    grad_middle, grad_norm_two = middle_back(project_back(grad_pre, params[6]))
    grad_middle = grad_middle + grad_out
    grad_attn = grad_middle.astype(jnp.bfloat16)
    grad_w_output = weight_grad(mixed_rows, grad_attn)
    grad_mixed = project_back(grad_attn, params[4]).astype(jnp.bfloat16)
    grad_query, grad_key, grad_value = attention_back(grad_mixed)
    grad_normed = (
        project_back(grad_query, params[1])
        + project_back(grad_key, params[2])
        + project_back(grad_value, params[3])
    )
    input_back = jax.vjp(normalize, inputs, params[0])[1]
    grad_inputs, grad_norm_one = input_back(grad_normed)
    weight_grads = (
        grad_norm_one,
        weight_grad(normed, grad_query),
        weight_grad(normed, grad_key),
        weight_grad(normed, grad_value),
        grad_w_output,
        grad_norm_two,
        grad_w_up,
        grad_b_up,
        grad_w_down,
        grad_b_down,
    )
    return (grad_inputs + grad_middle, weight_grads)


def permitted(row_ids, col_ids, usable_cols):
    causal = col_ids[None, :] <= row_ids[:, None]
    itself = col_ids[None, :] == row_ids[:, None]
    return (causal[None] & ((usable_cols[:, None, :] > 0) | itself[None]))[:, None]


def probs_from(query_heads, key_heads, allowed, log_total):
    scores = jnp.einsum(
        "uqhd,ukhd->uhqk", query_heads, key_heads, preferred_element_type=jnp.float32
    ) * HD ** (-0.5)
    return jnp.where(allowed, jnp.exp(scores - log_total[..., None]), 0.0)


def score_grads(probs, grad_heads, value_heads, delta_rows):
    grad_probs = jnp.einsum(
        "uqhd,ukhd->uhqk", grad_heads, value_heads, preferred_element_type=jnp.float32
    )
    return (probs * (grad_probs - delta_rows[..., None])).astype(jnp.bfloat16)


def on_device(
    frames,
    codes,
    lengths,
    frame_mask,
    table,
    glob_norm_one,
    glob_w_query,
    glob_w_key,
    glob_w_value,
    glob_w_output,
    glob_norm_two,
    glob_w_up,
    glob_b_up,
    glob_w_down,
    glob_b_down,
    local_norm_one,
    local_w_query,
    local_w_key,
    local_w_value,
    local_w_output,
    local_norm_two,
    local_w_up,
    local_b_up,
    local_w_down,
    local_b_down,
    cotan_global,
    cotan_local,
):
    utter_count, frame_count, model_width = frames.shape
    row_count = utter_count * frame_count
    local_len = CB + 1
    positions = lax.axis_index("seq") * frame_count + jnp.arange(frame_count, dtype=jnp.int32)
    valid = positions[None, :] < lengths[:, None]
    usable = frame_mask.astype(jnp.bfloat16)
    glob_params = (
        glob_norm_one,
        glob_w_query,
        glob_w_key,
        glob_w_value,
        glob_w_output,
        glob_norm_two,
        glob_w_up,
        glob_b_up,
        glob_w_down,
        glob_b_down,
    )
    local_params = (
        local_norm_one,
        local_w_query,
        local_w_key,
        local_w_value,
        local_w_output,
        local_norm_two,
        local_w_up,
        local_b_up,
        local_w_down,
        local_b_down,
    )
    global_in = frames.astype(jnp.float32).reshape(row_count, model_width)
    glob_front = block_inputs(global_in, glob_params)
    query_block = glob_front[1].reshape(utter_count, frame_count, model_width)
    key_block = glob_front[2].reshape(utter_count, frame_count, model_width)
    value_block = glob_front[3].reshape(utter_count, frame_count, model_width)
    query_heads = head_split(query_block)
    run_max = jnp.full((utter_count, H, frame_count), NEGATIVE, jnp.float32)
    part_keys = lax.all_gather(key_block, "seq", axis=1, tiled=True)
    part_values = lax.all_gather(value_block, "seq", axis=1, tiled=True)
    part_usable = lax.all_gather(usable, "seq", axis=1, tiled=True)
    span = part_keys.shape[1]
    allowed = permitted(positions, jnp.arange(span, dtype=jnp.int32), part_usable)
    scores = jnp.einsum(
        "uqhd,ukhd->uhqk", query_heads, head_split(part_keys), preferred_element_type=jnp.float32
    ) * HD ** (-0.5)
    scores = jnp.where(allowed, scores, NEGATIVE)
    new_max = jnp.maximum(run_max, jnp.max(scores, axis=-1))
    weights = jnp.where(allowed, jnp.exp(scores - new_max[..., None]), 0.0)
    new_sum = jnp.sum(weights, axis=-1)
    new_accum = jnp.einsum(
        "uhqk,ukhd->uqhd",
        weights.astype(jnp.bfloat16),
        head_split(part_values),
        preferred_element_type=jnp.float32,
    )
    log_total = new_max + jnp.log(new_sum)
    attn_heads = new_accum / new_sum.transpose(0, 2, 1)[..., None]
    glob_mixed = attn_heads.reshape(row_count, model_width).astype(jnp.bfloat16)
    glob_result, glob_kept = block_outputs(global_in, glob_mixed, glob_params)
    global_rows = jnp.where(valid.reshape(row_count, 1), glob_result, 0.0).astype(jnp.bfloat16)
    table_ids = codes + VOCAB * jnp.arange(CB, dtype=jnp.int32)[None, None, :]
    embedded = jnp.take(table, table_ids.reshape(-1), axis=0).reshape(
        utter_count, frame_count, CB, model_width
    )
    local_in = jnp.concatenate(
        [global_rows.reshape(utter_count, frame_count, 1, model_width), embedded], axis=2
    )
    local_in = local_in.astype(jnp.float32).reshape(row_count * local_len, model_width)
    local_front = block_inputs(local_in, local_params)
    local_q = local_front[1].reshape(row_count, local_len, H, HD)
    local_k = local_front[2].reshape(row_count, local_len, H, HD)
    local_v = local_front[3].reshape(row_count, local_len, H, HD)
    lower = (
        jnp.arange(local_len, dtype=jnp.int32)[:, None]
        >= jnp.arange(local_len, dtype=jnp.int32)[None, :]
    )
    local_scores = jnp.einsum(
        "nihd,njhd->nhij", local_q, local_k, preferred_element_type=jnp.float32
    ) * HD ** (-0.5)
    local_probs = softmax_rows(jnp.where(lower, local_scores, NEGATIVE))
    local_mixed = jnp.einsum(
        "nhij,njhd->nihd",
        local_probs.astype(jnp.bfloat16),
        local_v,
        preferred_element_type=jnp.float32,
    )
    local_mixed = local_mixed.reshape(row_count * local_len, model_width).astype(jnp.bfloat16)
    local_result, local_kept = block_outputs(local_in, local_mixed, local_params)
    local_valid = jnp.repeat(valid.reshape(-1), local_len)[:, None]
    local_rows = jnp.where(local_valid, local_result, 0.0).astype(jnp.bfloat16)

    def local_back(grad_mixed):
        grad_heads = grad_mixed.reshape(row_count, local_len, H, HD)
        grad_probs = jnp.einsum(
            "nihd,njhd->nhij", grad_heads, local_v, preferred_element_type=jnp.float32
        )
        grads_s = (
            local_probs * (grad_probs - jnp.sum(local_probs * grad_probs, axis=-1, keepdims=True))
        ).astype(jnp.bfloat16)
        grad_query = jnp.einsum(
            "nhij,njhd->nihd", grads_s, local_k, preferred_element_type=jnp.float32
        ) * HD ** (-0.5)
        grad_key = jnp.einsum(
            "nhij,nihd->njhd", grads_s, local_q, preferred_element_type=jnp.float32
        ) * HD ** (-0.5)
        grad_value = jnp.einsum(
            "nhij,nihd->njhd",
            local_probs.astype(jnp.bfloat16),
            grad_heads,
            preferred_element_type=jnp.float32,
        )
        return (
            grad_query.reshape(-1, model_width).astype(jnp.bfloat16),
            grad_key.reshape(-1, model_width).astype(jnp.bfloat16),
            grad_value.reshape(-1, model_width).astype(jnp.bfloat16),
        )

    local_cotan = jnp.where(
        local_valid, cotan_local.astype(jnp.float32).reshape(-1, model_width), 0.0
    )
    grad_local_in, local_grads = block_back(
        local_in, local_front, local_mixed, local_kept, local_params, local_cotan, local_back
    )
    grad_local_in = grad_local_in.reshape(utter_count, frame_count, local_len, model_width)
    grad_tab = jax.ops.segment_sum(
        grad_local_in[:, :, 1:].reshape(-1, model_width),
        table_ids.reshape(-1),
        num_segments=CB * VOCAB,
    )
    glob_cotan = jnp.where(
        valid[:, :, None], cotan_global.astype(jnp.float32) + grad_local_in[:, :, 0], 0.0
    )
    glob_cotan = glob_cotan.reshape(row_count, model_width)

    def global_back(grad_mixed):
        grad_block = grad_mixed.reshape(utter_count, frame_count, model_width)
        grad_heads = head_split(grad_block)
        delta_rows = jnp.sum(grad_heads.astype(jnp.float32) * attn_heads, axis=-1).transpose(
            0, 2, 1
        )
        all_keys, all_values, all_usable = (
            lax.all_gather(key_block, "seq", axis=1, tiled=True),
            lax.all_gather(value_block, "seq", axis=1, tiled=True),
            lax.all_gather(usable, "seq", axis=1, tiled=True),
        )
        every_col = jnp.arange(all_keys.shape[1], dtype=jnp.int32)
        probs = probs_from(
            query_heads,
            head_split(all_keys),
            permitted(positions, every_col, all_usable),
            log_total,
        )
        grads_s = score_grads(probs, grad_heads, head_split(all_values), delta_rows)
        grad_query = jnp.einsum(
            "uhqk,ukhd->uqhd", grads_s, head_split(all_keys), preferred_element_type=jnp.float32
        ) * HD ** (-0.5)
        span = frame_count * lax.axis_size("seq")
        col_ids = jnp.arange(span, dtype=jnp.int32)
        part_probs = probs_from(
            query_heads, head_split(all_keys), permitted(positions, col_ids, all_usable), log_total
        )
        part_grads = score_grads(part_probs, grad_heads, head_split(all_values), delta_rows)
        term_keys = jnp.einsum(
            "uhqk,uqhd->ukhd", part_grads, query_heads, preferred_element_type=jnp.float32
        ) * HD ** (-0.5)
        term_values = jnp.einsum(
            "uhqk,uqhd->ukhd",
            part_probs.astype(jnp.bfloat16),
            grad_heads,
            preferred_element_type=jnp.float32,
        )
        joined = jnp.concatenate(
            [
                term_keys.reshape(utter_count, span, model_width),
                term_values.reshape(utter_count, span, model_width),
            ],
            axis=-1,
        )
        summed = (
            lax.psum_scatter(
                joined.transpose(1, 0, 2).astype(jnp.bfloat16),
                "seq",
                scatter_dimension=0,
                tiled=True,
            )
            .astype(jnp.float32)
            .transpose(1, 0, 2)
        )
        grad_key = summed[:, :, :model_width]
        grad_value = summed[:, :, model_width:]
        return (
            grad_query.reshape(row_count, model_width).astype(jnp.bfloat16),
            grad_key.reshape(row_count, model_width).astype(jnp.bfloat16),
            grad_value.reshape(row_count, model_width).astype(jnp.bfloat16),
        )

    grad_inputs, glob_grads = block_back(
        global_in, glob_front, glob_mixed, glob_kept, glob_params, glob_cotan, global_back
    )
    partial_sum = (
        lax.psum_scatter(
            grad_tab.astype(jnp.bfloat16), "seq", scatter_dimension=0, tiled=True
        ).astype(jnp.float32),
        lax.psum_scatter(
            glob_grads[0].astype(jnp.bfloat16), "seq", scatter_dimension=0, tiled=True
        ).astype(jnp.float32),
        lax.psum_scatter(
            glob_grads[1].astype(jnp.bfloat16), "seq", scatter_dimension=0, tiled=True
        ).astype(jnp.float32),
        lax.psum_scatter(
            glob_grads[2].astype(jnp.bfloat16), "seq", scatter_dimension=0, tiled=True
        ).astype(jnp.float32),
        lax.psum_scatter(
            glob_grads[3].astype(jnp.bfloat16), "seq", scatter_dimension=0, tiled=True
        ).astype(jnp.float32),
        lax.psum_scatter(
            glob_grads[4].astype(jnp.bfloat16), "seq", scatter_dimension=0, tiled=True
        ).astype(jnp.float32),
        lax.psum_scatter(
            glob_grads[5].astype(jnp.bfloat16), "seq", scatter_dimension=0, tiled=True
        ).astype(jnp.float32),
        lax.psum_scatter(
            glob_grads[6].astype(jnp.bfloat16), "seq", scatter_dimension=0, tiled=True
        ).astype(jnp.float32),
        lax.psum_scatter(
            glob_grads[7].astype(jnp.bfloat16), "seq", scatter_dimension=0, tiled=True
        ).astype(jnp.float32),
        lax.psum_scatter(
            glob_grads[8].astype(jnp.bfloat16), "seq", scatter_dimension=0, tiled=True
        ).astype(jnp.float32),
        lax.psum_scatter(
            glob_grads[9].astype(jnp.bfloat16), "seq", scatter_dimension=0, tiled=True
        ).astype(jnp.float32),
        lax.psum_scatter(
            local_grads[0].astype(jnp.bfloat16), "seq", scatter_dimension=0, tiled=True
        ).astype(jnp.float32),
        lax.psum_scatter(
            local_grads[1].astype(jnp.bfloat16), "seq", scatter_dimension=0, tiled=True
        ).astype(jnp.float32),
        lax.psum_scatter(
            local_grads[2].astype(jnp.bfloat16), "seq", scatter_dimension=0, tiled=True
        ).astype(jnp.float32),
        lax.psum_scatter(
            local_grads[3].astype(jnp.bfloat16), "seq", scatter_dimension=0, tiled=True
        ).astype(jnp.float32),
        lax.psum_scatter(
            local_grads[4].astype(jnp.bfloat16), "seq", scatter_dimension=0, tiled=True
        ).astype(jnp.float32),
        lax.psum_scatter(
            local_grads[5].astype(jnp.bfloat16), "seq", scatter_dimension=0, tiled=True
        ).astype(jnp.float32),
        lax.psum_scatter(
            local_grads[6].astype(jnp.bfloat16), "seq", scatter_dimension=0, tiled=True
        ).astype(jnp.float32),
        lax.psum_scatter(
            local_grads[7].astype(jnp.bfloat16), "seq", scatter_dimension=0, tiled=True
        ).astype(jnp.float32),
        lax.psum_scatter(
            local_grads[8].astype(jnp.bfloat16), "seq", scatter_dimension=0, tiled=True
        ).astype(jnp.float32),
        lax.psum_scatter(
            local_grads[9].astype(jnp.bfloat16), "seq", scatter_dimension=0, tiled=True
        ).astype(jnp.float32),
    )
    reduced = (
        lax.psum(partial_sum[0].astype(jnp.bfloat16), "utt").astype(jnp.float32),
        lax.psum(partial_sum[1].astype(jnp.bfloat16), "utt").astype(jnp.float32),
        lax.psum(partial_sum[2].astype(jnp.bfloat16), "utt").astype(jnp.float32),
        lax.psum(partial_sum[3].astype(jnp.bfloat16), "utt").astype(jnp.float32),
        lax.psum(partial_sum[4].astype(jnp.bfloat16), "utt").astype(jnp.float32),
        lax.psum(partial_sum[5].astype(jnp.bfloat16), "utt").astype(jnp.float32),
        lax.psum(partial_sum[6].astype(jnp.bfloat16), "utt").astype(jnp.float32),
        lax.psum(partial_sum[7].astype(jnp.bfloat16), "utt").astype(jnp.float32),
        lax.psum(partial_sum[8].astype(jnp.bfloat16), "utt").astype(jnp.float32),
        lax.psum(partial_sum[9].astype(jnp.bfloat16), "utt").astype(jnp.float32),
        lax.psum(partial_sum[10].astype(jnp.bfloat16), "utt").astype(jnp.float32),
        lax.psum(partial_sum[11].astype(jnp.bfloat16), "utt").astype(jnp.float32),
        lax.psum(partial_sum[12].astype(jnp.bfloat16), "utt").astype(jnp.float32),
        lax.psum(partial_sum[13].astype(jnp.bfloat16), "utt").astype(jnp.float32),
        lax.psum(partial_sum[14].astype(jnp.bfloat16), "utt").astype(jnp.float32),
        lax.psum(partial_sum[15].astype(jnp.bfloat16), "utt").astype(jnp.float32),
        lax.psum(partial_sum[16].astype(jnp.bfloat16), "utt").astype(jnp.float32),
        lax.psum(partial_sum[17].astype(jnp.bfloat16), "utt").astype(jnp.float32),
        lax.psum(partial_sum[18].astype(jnp.bfloat16), "utt").astype(jnp.float32),
        lax.psum(partial_sum[19].astype(jnp.bfloat16), "utt").astype(jnp.float32),
        lax.psum(partial_sum[20].astype(jnp.bfloat16), "utt").astype(jnp.float32),
    )
    return (
        global_rows.reshape(utter_count, frame_count, model_width),
        local_rows.reshape(utter_count, frame_count, local_len, model_width),
        grad_inputs.reshape(utter_count, frame_count, model_width),
        reduced[0],
        reduced[1],
        reduced[2],
        reduced[3],
        reduced[4],
        reduced[5],
        reduced[6],
        reduced[7],
        reduced[8],
        reduced[9],
        reduced[10],
        reduced[11],
        reduced[12],
        reduced[13],
        reduced[14],
        reduced[15],
        reduced[16],
        reduced[17],
        reduced[18],
        reduced[19],
        reduced[20],
    )


def solution(mesh):
    return jax.shard_map(
        on_device,
        mesh=mesh,
        in_specs=(
            P("utt", "seq", None),
            P("utt", "seq", None),
            P("utt"),
            P("utt", "seq"),
            P(),
            P(),
            P(),
            P(),
            P(),
            P(),
            P(),
            P(),
            P(),
            P(),
            P(),
            P(),
            P(),
            P(),
            P(),
            P(),
            P(),
            P(),
            P(),
            P(),
            P(),
            P("utt", "seq", None),
            P("utt", "seq", None, None),
        ),
        out_specs=(
            P("utt", "seq", None),
            P("utt", "seq", None, None),
            P("utt", "seq", None),
            P("seq", None),
            P("seq"),
            P("seq", None),
            P("seq", None),
            P("seq", None),
            P("seq", None),
            P("seq"),
            P("seq", None),
            P("seq"),
            P("seq", None),
            P("seq"),
            P("seq"),
            P("seq", None),
            P("seq", None),
            P("seq", None),
            P("seq", None),
            P("seq"),
            P("seq", None),
            P("seq"),
            P("seq", None),
            P("seq"),
        ),
        check_vma=False,
    )
```

profile of v0, /device:TPU:0, one launch (start us, length us, event | category | flops | bytes accessed | tf_op | source)
XLA Modules:
  0.0 1636.3 jit_solution(18134386944083135268)
XLA Ops:
  17.0 23.0 %all-gather = bf16[16,64,2]{1,2,0:T(2,128)(2,1)S(1)} all-gather(bf16[1,64,2]{1,2,0:T(2,128)(2,1)S(1)} %convert_bitcast_fusion.3), channel_id=1, replica_groups=mesh['utt'=2,'seq'=16] {'seq'}, dimensions={0}, use_global_device_ids=true | all-gather | bytes 4352 | tf_op jit(solution)/shard_map/all_gather | solution.py:196
  44.4 6.4 gather_fusion
  59.0 8.6 all-gather.6.cloned.1.call-done
  67.6 6.3 copy.104
  83.6 35.8 %all-gather.4.cloned.1.call-done = bf16[2,1024,1024]{2,1,0:T(8,128)(2,1)} async-done(((bf16[2,64,1024]{2,1,0:T(8,128)(2,1)}), bf16[2,1024,1024]{2,1,0:T(8,128)(2,1)}) %all-gather.4.cloned.1.call-update) | async-done | bytes 4194320 | tf_op jit(solution)/shard_map/all_gather | solution.py:195
  119.5 6.5 copy.102
  126.0 8.4 fusion.102
  138.0 4.8 convolution_add_fusion
  177.6 12.0 fusion.103
  189.6 5.3 convert_bitcast_fusion.1
  204.8 11.1 fusion.97
  215.9 16.4 %fusion.104 = (bf16[4096]{0:T(1024)(128)(2,1)}, bf16[512,4096]{1,0:T(8,128)(2,1)}) fusion(f32[512,4096]{1,0:T(8,128)} %fusion.97, f32[4096]{0:T(1024)S(1)} %copy-done.94, bf16[4096,1024]{1,0:T(8,128)(2,1)} %param.50, f32[512,1024]{1,0:T(8,128)S(1)} %copy-done.16, pred[512]{0:T(512)(128)(4,1)S(1)} %copy-done.85), kind=kOutput, calls=%fused_computation.203 | convolution fusion | flops 4341624832 | bytes 23093760 | tf_op jit(solution)/shard_map/dot_general | solution.py:37
  232.3 7.6 multiply_reduce_fusion.1
  248.1 11.8 multiply_reduce_fusion
  260.0 5.7 multiply_convert_fusion.5
  273.2 5.4 convert_bitcast_fusion
  306.3 5.0 multiply_reduce_fusion.2
  316.0 7.1 fusion.99
  323.2 6.8 multiply_reduce_fusion.8
  334.9 7.4 fusion.26
  342.3 6.3 copy.131
  348.8 6.6 multiply_convert_fusion.1
  358.7 6.3 copy.130
  365.1 8.2 maximum_bitcast_fusion
  412.5 9.0 scatter_custom_fusion
  421.5 8.4 convert_element_type.454
  431.5 9.2 convolution_convert_fusion.1
  441.9 5.8 convolution_convert_fusion.3
  449.3 5.7 convolution_convert_fusion.2
  456.7 13.2 convolution_convert_fusion
  470.0 6.7 reduce-scatter.15.cloned.1.call-done
  485.0 56.7 %reduce-scatter.33.cloned.1.call-done = bf16[64,1024]{1,0:T(8,128)(2,1)} async-done(((bf16[1024,1024]{1,0:T(8,128)(2,1)}), bf16[64,1024]{1,0:T(8,128)(2,1)}) %reduce-scatter.33.cloned.1.call-update) | async-done | bytes 131088 | tf_op jit(solution)/shard_map/reduce_scatter | solution.py:396
  541.7 64.6 %reduce-scatter.31.cloned.1.call-done = bf16[64,1024]{1,0:T(8,128)(2,1)} async-done(((bf16[1024,1024]{1,0:T(8,128)(2,1)}), bf16[64,1024]{1,0:T(8,128)(2,1)}) %reduce-scatter.31.cloned.1.call-update) | async-done | bytes 131088 | tf_op jit(solution)/shard_map/reduce_scatter | solution.py:393
  606.3 64.2 %reduce-scatter.35.cloned.1.call-done = bf16[64,1024]{1,0:T(8,128)(2,1)} async-done(((bf16[1024,1024]{1,0:T(8,128)(2,1)}), bf16[64,1024]{1,0:T(8,128)(2,1)}) %reduce-scatter.35.cloned.1.call-update) | async-done | bytes 131088 | tf_op jit(solution)/shard_map/reduce_scatter | solution.py:399
  670.5 64.7 %reduce-scatter.25.cloned.1.call-done = bf16[64,1024]{1,0:T(8,128)(2,1)} async-done(((bf16[1024,1024]{1,0:T(8,128)(2,1)}), bf16[64,1024]{1,0:T(8,128)(2,1)}) %reduce-scatter.25.cloned.1.call-update) | async-done | bytes 131088 | tf_op jit(solution)/shard_map/reduce_scatter | solution.py:372
  735.3 64.3 %reduce-scatter.37.cloned.1.call-done = bf16[64,1024]{1,0:T(8,128)(2,1)} async-done(((bf16[1024,1024]{1,0:T(8,128)(2,1)}), bf16[64,1024]{1,0:T(8,128)(2,1)}) %reduce-scatter.37.cloned.1.call-update) | async-done | bytes 131088 | tf_op jit(solution)/shard_map/reduce_scatter | solution.py:402
  799.6 64.8 %reduce-scatter.19.cloned.1.call-done = bf16[64,1024]{1,0:T(8,128)(2,1)} async-done(((bf16[1024,1024]{1,0:T(8,128)(2,1)}), bf16[64,1024]{1,0:T(8,128)(2,1)}) %reduce-scatter.19.cloned.1.call-update) | async-done | bytes 131088 | tf_op jit(solution)/shard_map/reduce_scatter | solution.py:363
  864.4 88.1 %reduce-scatter.17.cloned.1.call-done = bf16[192,1024]{1,0:T(8,128)(2,1)} async-done(((bf16[3072,1024]{1,0:T(8,128)(2,1)}), bf16[192,1024]{1,0:T(8,128)(2,1)}) %reduce-scatter.17.cloned.1.call-update) | async-done | bytes 393232 | tf_op jit(solution)/shard_map/reduce_scatter | solution.py:357
  952.5 108.5 %reduce-scatter.39.cloned.1.call-done = bf16[64,4096]{1,0:T(8,128)(2,1)} async-done(((bf16[1024,4096]{1,0:T(8,128)(2,1)}), bf16[64,4096]{1,0:T(8,128)(2,1)}) %reduce-scatter.39.cloned.1.call-update) | async-done | bytes 524304 | tf_op jit(solution)/shard_map/reduce_scatter | solution.py:408
  1060.9 108.9 %reduce-scatter.27.cloned.1.call-done = bf16[64,4096]{1,0:T(8,128)(2,1)} async-done(((bf16[1024,4096]{1,0:T(8,128)(2,1)}), bf16[64,4096]{1,0:T(8,128)(2,1)}) %reduce-scatter.27.cloned.1.call-update) | async-done | bytes 524304 | tf_op jit(solution)/shard_map/reduce_scatter | solution.py:378
  1169.9 109.1 %reduce-scatter.29.cloned.1.call-done = bf16[256,1024]{1,0:T(8,128)(2,1)} async-done(((bf16[4096,1024]{1,0:T(8,128)(2,1)}), bf16[256,1024]{1,0:T(8,128)(2,1)}) %reduce-scatter.29.cloned.1.call-update) | async-done | bytes 524304 | tf_op jit(solution)/shard_map/reduce_scatter | solution.py:384
  1278.9 108.9 %reduce-scatter.41.cloned.1.call-done = bf16[256,1024]{1,0:T(8,128)(2,1)} async-done(((bf16[4096,1024]{1,0:T(8,128)(2,1)}), bf16[256,1024]{1,0:T(8,128)(2,1)}) %reduce-scatter.41.cloned.1.call-update) | async-done | bytes 524304 | tf_op jit(solution)/shard_map/reduce_scatter | solution.py:414
  1387.8 65.4 %reduce-scatter.21.cloned.1.call-done = bf16[64,1024]{1,0:T(8,128)(2,1)} async-done(((bf16[1024,1024]{1,0:T(8,128)(2,1)}), bf16[64,1024]{1,0:T(8,128)(2,1)}) %reduce-scatter.21.cloned.1.call-update) | async-done | bytes 131088 | tf_op jit(solution)/shard_map/reduce_scatter | solution.py:366
  1453.2 64.2 %reduce-scatter.23.cloned.1.call-done = bf16[64,1024]{1,0:T(8,128)(2,1)} async-done(((bf16[1024,1024]{1,0:T(8,128)(2,1)}), bf16[64,1024]{1,0:T(8,128)(2,1)}) %reduce-scatter.23.cloned.1.call-update) | async-done | bytes 131088 | tf_op jit(solution)/shard_map/reduce_scatter | solution.py:369
  1517.5 12.2 select_convert_fusion.1
  1536.4 57.7 %all-reduce.8 = (bf16[1024]{0:T(1024)(128)(2,1)S(1)}, bf16[1024]{0:T(1024)(128)(2,1)S(1)}, bf16[4096]{0:T(1024)(128)(2,1)S(1)}, bf16[1024]{0:T(1024)(128)(2,1)S(...) all-reduce(bf16[1024]{0:T(1024)(128)(2,1)S(1)} %get-tuple-element.3, ...), channel_id=4, replica_groups=mesh['utt'=2,'seq'=16] {'seq'}, use_global_device_ids=true, to_apply=%region_19.20.clone | all-reduce | flops 14336 | bytes 57344
  1594.8 5.0 all-reduce.9
  1606.0 10.3 all-reduce.13.cloned.1.call-done
  (393 shorter events, 215.4 us)
Async XLA Ops:
  7.2 162.9 %copy-start = (bf16[1024,1024]{1,0:T(8,128)(2,1)S(1)}, bf16[1024,1024]{1,0:T(8,128)(2,1)}, u32[]{:S(2)}) copy-start(bf16[1024,1024]{1,0:T(8,128)(2,1)} %param.45) | copy-start | bytes 6291460
  7.2 60.4 %all-gather.6.cloned.1.call-start = ((), (), s32[]{:S(2)}) async-start(), calls=%async_computation.15 | async-start | bytes 4456448 | tf_op jit(solution)/shard_map/all_gather | solution.py:194
  14.1 105.4 %all-gather.4.cloned.1.call-start = ((), (), s32[]{:S(2)}) async-start(), calls=%async_computation.14 | async-start | bytes 4456448 | tf_op jit(solution)/shard_map/all_gather | solution.py:195
  16.9 459.8 %reduce-scatter.15.cloned.1.call-start = ((), (), s32[]{:S(2)}) async-start(), calls=%async_computation.16 | async-start | bytes 8912896 | tf_op jit(solution)/shard_map/reduce_scatter | solution.py:336
  43.0 30.9 %copy-start.24 = (bf16[2,64,16,64]{1,3,2,0:T(8,128)(2,1)}, bf16[2,64,16,64]{1,3,2,0:T(8,128)(2,1)S(1)}, u32[]{:S(2)}) copy-start(bf16[2,64,16,64]{1,3,2,0:T(8,128)(2,1)S(1)} %copy.128) | copy-start | bytes 786436
  43.2 12.9 copy-start.88
  56.2 69.8 %copy-start.32 = (pred[2,64,1024]{2,1,0:T(8,128)(4,1)}, pred[2,64,1024]{2,1,0:T(8,128)(4,1)S(1)}, u32[]{:S(2)}) copy-start(pred[2,64,1024]{2,1,0:T(8,128)(4,1)S(1)} %or_and_fusion) | copy-start | bytes 393220
  83.6 42.3 %copy-start.73 = (f32[2,16,64]{2,1,0:T(8,128)}, f32[2,16,64]{2,1,0:T(8,128)S(1)}, u32[]{:S(2)}) copy-start(f32[2,16,64]{2,1,0:T(8,128)S(1)} %fusion.11) | copy-start | bytes 24580
  125.9 9.2 copy-start.11
  135.1 7.7 copy-start.37
  135.1 7.7 slice-start.2
  204.7 35.2 %copy-start.39 = (f32[512,1024]{1,0:T(8,128)}, f32[512,1024]{1,0:T(8,128)S(1)}, u32[]{:S(2)}) copy-start(f32[512,1024]{1,0:T(8,128)S(1)} %get-tuple-element.84) | copy-start | bytes 6291460
  204.8 11.1 copy-start.16
  204.8 11.1 copy-start.85
  204.8 11.1 copy-start.94
  204.8 27.5 %slice-start = ((s8[8388608]{0:T(1024)(128)(4,1)}), s8[4194304]{0:T(1024)(128)(4,1)S(1)}, s32[]{:S(2)}) async-start(s8[8388608]{0:T(1024)(128)(4,1)} %bitcast.177), calls=%async_computation.31 | async-start | bytes 8388608
  215.9 16.4 %slice-start.1 = ((s8[8388608]{0:T(1024)(128)(4,1)}), s8[4194304]{0:T(1024)(128)(4,1)S(1)}, s32[]{:S(2)}) async-start(s8[8388608]{0:T(1024)(128)(4,1)} %bitcast.177), calls=%async_computation.32 | async-start | bytes 8388608
  260.0 5.7 copy-start.42
  273.2 5.4 copy-start.74
  273.2 5.4 copy-start.46
  316.0 7.1 copy-start.47
  323.2 6.8 copy-start.29
  323.2 6.8 copy-start.91
  342.3 6.3 copy-start.52
  348.8 6.6 copy-start.25
  373.3 168.4 %reduce-scatter.33.cloned.1.call-start = ((), (), s32[]{:S(2)}) async-start(), calls=%async_computation.25 | async-start | bytes 2228224 | tf_op jit(solution)/shard_map/reduce_scatter | solution.py:396
  381.2 225.1 %reduce-scatter.31.cloned.1.call-start = ((), (), s32[]{:S(2)}) async-start(), calls=%async_computation.24 | async-start | bytes 2228224 | tf_op jit(solution)/shard_map/reduce_scatter | solution.py:393
  385.2 285.4 %reduce-scatter.35.cloned.1.call-start = ((), (), s32[]{:S(2)}) async-start(), calls=%async_computation.26 | async-start | bytes 2228224 | tf_op jit(solution)/shard_map/reduce_scatter | solution.py:399
  389.2 346.1 %reduce-scatter.25.cloned.1.call-start = ((), (), s32[]{:S(2)}) async-start(), calls=%async_computation.21 | async-start | bytes 2228224 | tf_op jit(solution)/shard_map/reduce_scatter | solution.py:372
  392.3 407.3 %reduce-scatter.37.cloned.1.call-start = ((), (), s32[]{:S(2)}) async-start(), calls=%async_computation.27 | async-start | bytes 2228224 | tf_op jit(solution)/shard_map/reduce_scatter | solution.py:402
  396.4 468.0 %reduce-scatter.19.cloned.1.call-start = ((), (), s32[]{:S(2)}) async-start(), calls=%async_computation.18 | async-start | bytes 2228224 | tf_op jit(solution)/shard_map/reduce_scatter | solution.py:363
  407.7 544.8 %reduce-scatter.17.cloned.1.call-start = ((), (), s32[]{:S(2)}) async-start(), calls=%async_computation.17 | async-start | bytes 6684672 | tf_op jit(solution)/shard_map/reduce_scatter | solution.py:357
  429.9 631.0 %reduce-scatter.39.cloned.1.call-start = ((), (), s32[]{:S(2)}) async-start(), calls=%async_computation.28 | async-start | bytes 8912896 | tf_op jit(solution)/shard_map/reduce_scatter | solution.py:408
  440.7 729.2 %reduce-scatter.27.cloned.1.call-start = ((), (), s32[]{:S(2)}) async-start(), calls=%async_computation.22 | async-start | bytes 8912896 | tf_op jit(solution)/shard_map/reduce_scatter | solution.py:378
  447.7 831.2 %reduce-scatter.29.cloned.1.call-start = ((), (), s32[]{:S(2)}) async-start(), calls=%async_computation.23 | async-start | bytes 8912896 | tf_op jit(solution)/shard_map/reduce_scatter | solution.py:384
  455.1 932.8 %reduce-scatter.41.cloned.1.call-start = ((), (), s32[]{:S(2)}) async-start(), calls=%async_computation.29 | async-start | bytes 8912896 | tf_op jit(solution)/shard_map/reduce_scatter | solution.py:414
  469.9 7.9 copy-start.27
  469.9 983.3 %reduce-scatter.21.cloned.1.call-start = ((), (), s32[]{:S(2)}) async-start(), calls=%async_computation.19 | async-start | bytes 2228224 | tf_op jit(solution)/shard_map/reduce_scatter | solution.py:366
  479.9 1037.5 %reduce-scatter.23.cloned.1.call-start = ((), (), s32[]{:S(2)}) async-start(), calls=%async_computation.20 | async-start | bytes 2228224 | tf_op jit(solution)/shard_map/reduce_scatter | solution.py:369
  482.1 1134.1 %all-reduce.13.cloned.1.call-start = ((), (), s32[]{:S(2)}) async-start(), calls=%async_computation.30 | async-start | bytes 7077888 | tf_op jit(solution)/shard_map/psum | solution.py:422
  484.3 1033.1 %copy-start.97 = (f32[1024]{0:T(1024)S(1)}, f32[1024]{0:T(1024)}, u32[]{:S(2)}) copy-start(f32[1024]{0:T(1024)} %param.51) | copy-start | bytes 12292
  485.0 1032.5 %copy-start.41 = (f32[512,1024]{1,0:T(8,128)S(1)}, f32[512,1024]{1,0:T(8,128)}, u32[]{:S(2)}) copy-start(f32[512,1024]{1,0:T(8,128)} %copy-done.39) | copy-start | bytes 6291460
  1517.5 14.6 copy-start.34
  1534.6 69.4 %copy-start.101 = (f32[128]{0:T(128)S(1)}, f32[128]{0:T(128)}, u32[]{:S(2)}) copy-start(f32[128]{0:T(128)} %copy-done.100) | copy-start | bytes 1540
  1616.3 5.4 copy-start.56
  1621.7 5.7 copy-start.65
  1622.8 6.0 copy-start.63
  1622.8 6.8 copy-start.1
  (77 other events, 204.0 us)
Sparse Core Ops, SparseCore 0:
  14.2 53.3 all-gather.5
  70.3 49.0 all-gather.3
  373.5 103.1 reduce-scatter.14
  480.3 61.3 reduce-scatter.32
  545.7 60.5 reduce-scatter.30
  609.9 60.5 reduce-scatter.34
  674.7 60.4 reduce-scatter.24
  739.0 60.5 reduce-scatter.36
  803.8 60.5 reduce-scatter.18
  868.2 84.2 reduce-scatter.16
  957.1 103.7 reduce-scatter.38
  1065.4 104.4 reduce-scatter.26
  1174.5 104.4 reduce-scatter.28
  1283.4 104.4 reduce-scatter.40
  1391.9 61.3 reduce-scatter.20
  1456.8 60.5 reduce-scatter.22
  1520.7 95.5 all-reduce.12
where the time goes:
time: 1650 us; the launch traced here: 1640 us
  waiting for transfers between devices  1090 us (66%)
  matrix products  244 us (15%)
  local copies, waits for them, and re-layouts  122 us (7%)
  blocking collectives  85.7 us (5%)
  other arithmetic  71.7 us (4%)
  between operations  16.7 us (1%)
    reduce_scatter x1, waiting for transfers between devices, on_device(): lax.psum_scatter(glob_grads[8].astype(jnp.bfloat16), 'seq', scatter_dimen...  109 us
    reduce_scatter x1, waiting for transfers between devices, on_device(): lax.psum_scatter(glob_grads[6].astype(jnp.bfloat16), 'seq', scatter_dimen...  109 us
    reduce_scatter x1, waiting for transfers between devices, on_device(): lax.psum_scatter(local_grads[8].astype(jnp.bfloat16), 'seq', scatter_dime...  109 us
    reduce_scatter x1, waiting for transfers between devices, on_device(): lax.psum_scatter(local_grads[6].astype(jnp.bfloat16), 'seq', scatter_dime...  108 us
    reduce_scatter x1, waiting for transfers between devices, on_device(): lax.psum_scatter(grad_tab.astype(jnp.bfloat16), 'seq', scatter_dimension=...  88.1 us
    reduce_scatter x1, waiting for transfers between devices, on_device(): lax.psum_scatter(glob_grads[2].astype(jnp.bfloat16), 'seq', scatter_dimen...  65.4 us
    reduce_scatter x1, waiting for transfers between devices, on_device(): lax.psum_scatter(glob_grads[1].astype(jnp.bfloat16), 'seq', scatter_dimen...  64.8 us
    reduce_scatter x1, waiting for transfers between devices, on_device(): lax.psum_scatter(glob_grads[4].astype(jnp.bfloat16), 'seq', scatter_dimen...  64.7 us
  transfers between devices with their start and end apart: 17, of which 17 were waited for; matrix products, arithmetic and copies ran while one was open for 9% of the time, Pallas kernels for 0%

commit v1 on v0

--- a/solution.py
+++ b/solution.py
@@ -1,6 +1,10 @@
+import functools
+
 import jax
 import jax.numpy as jnp
 from jax import lax
+from jax.experimental import pallas as pl
+from jax.experimental.pallas import tpu as pltpu
 from jax.sharding import PartitionSpec as P
 
 H = 16
@@ -11,6 +15,342 @@
 
 EPSILON = 1e-05
 NEGATIVE = -1e30
+MESH_ID = pl.DeviceIdType.MESH
+SLOTS = 4
+SROWS = 64
+SCOLS = 512
+DEEP = 8
+
+
+def reduce_kernel(plan, total, *refs):
+    count = len(plan)
+    ins = refs[:count]
+    outs = refs[count : 2 * count]
+    (
+        part, recv_c, half_a, half_b, recv_xa, recv_yb, sum_a, sum_b, recv_xb, line_b,
+        right_a, left_a, right_b, left_b, recv_ya, recv_yb2, staged,
+        load_sem, out_sem, send_sem, recv_sem,
+    ) = refs[2 * count :]
+    f32 = jnp.float32
+    low = jnp.bfloat16
+    utt = lax.axis_index("utt")
+    seq = lax.axis_index("seq")
+    pos = seq // 4
+    col = (seq // 2) % 2
+    core = seq % 2
+    base = pos * 4 + col * 2
+    core_id = (utt, base + 1 - core)
+    col_id = (utt, pos * 4 + (1 - col) * 2 + core)
+    utt_id = (1 - utt, seq)
+    right_id = (utt, lax.rem(seq + 4, 16))
+    left_id = (utt, lax.rem(seq + 12, 16))
+
+    barrier = pltpu.get_barrier_semaphore()
+    for target in (core_id, col_id, utt_id):
+        pl.semaphore_signal(barrier, inc=1, device_id=target, device_id_type=MESH_ID)
+
+    @pl.when(pos < 3)
+    def _():
+        pl.semaphore_signal(barrier, inc=1, device_id=right_id, device_id_type=MESH_ID)
+
+    @pl.when(pos > 0)
+    def _():
+        pl.semaphore_signal(barrier, inc=1, device_id=left_id, device_id_type=MESH_ID)
+
+    pl.semaphore_wait(barrier, jnp.where((pos == 0) | (pos == 3), 4, 5))
+
+    def window(ref, spec, slab, lead):
+        first, _, wide = spec
+        local = slab - first
+        rows = pl.ds(pl.multiple_of((local // wide) * SROWS, SROWS), SROWS)
+        cols = pl.ds(pl.multiple_of((local % wide) * SCOLS, SCOLS), SCOLS)
+        return ref.at[lead + (rows, cols)]
+
+    def load(slab, start):
+        slot = slab % SLOTS
+        if not start:
+            for side in range(2):
+                pltpu.make_async_copy(
+                    ins[0].at[:, side, pl.ds(0, SROWS), pl.ds(0, SCOLS)],
+                    part.at[slot, side],
+                    load_sem.at[slot, side],
+                ).wait()
+            return
+        for ref, spec in zip(ins, plan):
+
+            @pl.when((slab >= spec[0]) & (slab < spec[0] + spec[1]))
+            def _():
+                for side in range(2):
+                    pltpu.make_async_copy(
+                        window(ref, spec, slab, (slice(None), side)),
+                        part.at[slot, side],
+                        load_sem.at[slot, side],
+                    ).start()
+
+    def send(kind, slot, source, target, device):
+        return pltpu.make_async_remote_copy(
+            src_ref=source,
+            dst_ref=target,
+            send_sem=send_sem.at[kind, slot],
+            recv_sem=recv_sem.at[kind, slot],
+            device_id=device,
+            device_id_type=MESH_ID,
+        )
+
+    def core_copy(slot):
+        return send(0, slot, part.at[slot, 1 - core], recv_c.at[slot], core_id)
+
+    def col_copy_a(slot):
+        return send(1, slot, half_a.at[slot, 1 - col], recv_xa.at[slot], col_id)
+
+    def utt_copy_b(slot):
+        return send(2, slot, half_b.at[slot, 1 - utt], recv_yb.at[slot], utt_id)
+
+    def col_copy_b(slot):
+        return send(3, slot, sum_b.at[slot, 1 - col], recv_xb.at[slot], col_id)
+
+    def utt_copy_a(slot, deep):
+        return send(4, slot, sum_a.at[deep, pos], recv_ya.at[slot], utt_id)
+
+    def utt_copy_b2(slot, deep):
+        return send(5, slot, line_b.at[deep, pos], recv_yb2.at[slot], utt_id)
+
+    def line_right(kind, slot, deep, step, source, target):
+        dest = jnp.minimum(4 - step + pos, 3)
+        return send(kind + step - 1, slot, source.at[deep, dest], target.at[slot, step - 1], right_id)
+
+    def line_left(kind, slot, deep, step, source, target):
+        dest = jnp.maximum(pos - 4 + step, 0)
+        return send(kind + step - 1, slot, source.at[deep, dest], target.at[slot, step - 1], left_id)
+
+    def line_start(slot, deep, step, source, right, left, kind):
+        @pl.when((pos <= step - 1) & (pos < 3))
+        def _():
+            line_right(kind, slot, deep, step, source, right).start()
+
+        @pl.when((pos >= 4 - step) & (pos > 0))
+        def _():
+            line_left(kind + 3, slot, deep, step, source, left).start()
+
+    def line_finish(slot, deep, step, source, right, left, kind):
+        @pl.when((pos <= step - 1) & (pos < 3))
+        def _():
+            line_right(kind, slot, deep, step, source, right).wait_send()
+
+        @pl.when((pos >= 4 - step) & (pos > 0))
+        def _():
+            line_left(kind + 3, slot, deep, step, source, left).wait_send()
+
+        @pl.when((pos >= 1) & (pos <= step))
+        def _():
+            line_right(kind, slot, deep, step, source, right).wait_recv()
+            dest = 3 - step + pos
+            source[deep, dest] = (
+                source[deep, dest].astype(f32) + right[slot, step - 1].astype(f32)
+            ).astype(low)
+
+        @pl.when((pos <= 2) & (pos >= 3 - step))
+        def _():
+            line_left(kind + 3, slot, deep, step, source, left).wait_recv()
+            dest = pos + step - 3
+            source[deep, dest] = (
+                source[deep, dest].astype(f32) + left[slot, step - 1].astype(f32)
+            ).astype(low)
+
+    line_a = (sum_a, right_a, left_a, 6)
+    line_bb = (line_b, right_b, left_b, 12)
+
+    load(0, True)
+
+    @pl.loop(0, total + 8)
+    def _(tick):
+        def stage(offset):
+            slab = tick - offset
+            return slab, lax.rem(slab + SLOTS * 4, SLOTS), pl.when((slab >= 0) & (slab < total))
+
+        slab, slot, guard = stage(0)
+
+        @pl.when(slab + 1 < total)
+        def _():
+            load(slab + 1, True)
+
+        @guard
+        def _():
+            load(slab, False)
+            core_copy(slot).start()
+
+        slab1, slot1, guard = stage(1)
+
+        @guard
+        def _():
+            core_copy(slot1).wait()
+            for line in range(4):
+                for side in range(2):
+                    both = part[slot1, core, 2 * line + side].astype(f32) + recv_c[
+                        slot1, 2 * line + side
+                    ].astype(f32)
+                    both = both.astype(low)
+                    half_a[slot1, side, line] = both[:32]
+                    half_b[slot1, 0, side, line] = both[32:48]
+                    half_b[slot1, 1, side, line] = both[48:]
+            col_copy_a(slot1).start()
+            utt_copy_b(slot1).start()
+
+        slab2, slot2, guard = stage(2)
+        deep2 = lax.rem(slab2 + DEEP, DEEP)
+
+        @guard
+        def _():
+            col_copy_a(slot2).wait()
+            sum_a[deep2] = (
+                half_a[slot2, col].astype(f32) + recv_xa[slot2].astype(f32)
+            ).astype(low)
+            line_start(slot2, deep2, 1, *line_a)
+            utt_copy_b(slot2).wait()
+            sum_b[slot2] = (
+                half_b[slot2, utt].astype(f32) + recv_yb[slot2].astype(f32)
+            ).astype(low)
+            col_copy_b(slot2).start()
+
+        slab3, slot3, guard = stage(3)
+        deep3 = lax.rem(slab3 + DEEP, DEEP)
+
+        @guard
+        def _():
+            line_finish(slot3, deep3, 1, *line_a)
+            line_start(slot3, deep3, 2, *line_a)
+            col_copy_b(slot3).wait()
+            line_b[deep3] = (
+                sum_b[slot3, col].astype(f32) + recv_xb[slot3].astype(f32)
+            ).astype(low)
+            line_start(slot3, deep3, 1, *line_bb)
+
+        slab4, slot4, guard = stage(4)
+        deep4 = lax.rem(slab4 + DEEP, DEEP)
+
+        @guard
+        def _():
+            line_finish(slot4, deep4, 2, *line_a)
+            line_start(slot4, deep4, 3, *line_a)
+            line_finish(slot4, deep4, 1, *line_bb)
+            line_start(slot4, deep4, 2, *line_bb)
+
+        slab5, slot5, guard = stage(5)
+        deep5 = lax.rem(slab5 + DEEP, DEEP)
+
+        @guard
+        def _():
+            line_finish(slot5, deep5, 3, *line_a)
+            utt_copy_a(slot5, deep5).start()
+            line_finish(slot5, deep5, 2, *line_bb)
+            line_start(slot5, deep5, 3, *line_bb)
+
+        slab6, slot6, guard = stage(6)
+        deep6 = lax.rem(slab6 + DEEP, DEEP)
+
+        @guard
+        def _():
+            utt_copy_a(slot6, deep6).wait()
+            staged[slot6, 0:32] = sum_a[deep6, pos].astype(f32) + recv_ya[slot6].astype(f32)
+            line_finish(slot6, deep6, 3, *line_bb)
+            utt_copy_b2(slot6, deep6).start()
+
+        slab7, slot7, guard = stage(7)
+        deep7 = lax.rem(slab7 + DEEP, DEEP)
+
+        @guard
+        def _():
+            utt_copy_b2(slot7, deep7).wait()
+            mine = line_b[deep7, pos].astype(f32)
+            theirs = recv_yb2[slot7].astype(f32)
+            staged[slot7, 32:48] = jnp.where(utt == 0, mine, theirs)
+            staged[slot7, 48:64] = jnp.where(utt == 0, theirs, mine)
+            for ref, spec in zip(outs, plan):
+
+                @pl.when((slab7 >= spec[0]) & (slab7 < spec[0] + spec[1]))
+                def _():
+                    pltpu.make_async_copy(
+                        staged.at[slot7], window(ref, spec, slab7, ()), out_sem.at[slot7]
+                    ).start()
+
+        slab8, slot8, guard = stage(8)
+
+        @guard
+        def _():
+            pltpu.make_async_copy(
+                staged.at[slot8], outs[0].at[pl.ds(0, SROWS), pl.ds(0, SCOLS)], out_sem.at[slot8]
+            ).wait()
+
+
+def reduce_grads(arrays):
+    views, plan, shapes, total = [], [], [], 0
+    for item in arrays:
+        rows, cols = item.shape[0] // 16, item.shape[1]
+        views.append(item.reshape(8, 2, rows, cols))
+        slabs = (rows // SROWS) * (cols // SCOLS)
+        plan.append((total, slabs, cols // SCOLS))
+        shapes.append(jax.ShapeDtypeStruct((rows, cols), jnp.float32))
+        total += slabs
+    low = jnp.bfloat16
+    hbm = pl.BlockSpec(memory_space=pl.ANY)
+    return pl.pallas_call(
+        functools.partial(reduce_kernel, tuple(plan), total),
+        out_shape=tuple(shapes),
+        in_specs=[hbm] * len(views),
+        out_specs=tuple([hbm] * len(views)),
+        scratch_shapes=[
+            pltpu.VMEM((SLOTS, 2, 8, 64, SCOLS), low),
+            pltpu.VMEM((SLOTS, 8, 64, SCOLS), low),
+            pltpu.VMEM((SLOTS, 2, 4, 32, SCOLS), low),
+            pltpu.VMEM((SLOTS, 2, 2, 4, 16, SCOLS), low),
+            pltpu.VMEM((SLOTS, 4, 32, SCOLS), low),
+            pltpu.VMEM((SLOTS, 2, 4, 16, SCOLS), low),
+            pltpu.VMEM((DEEP, 4, 32, SCOLS), low),
+            pltpu.VMEM((SLOTS, 2, 4, 16, SCOLS), low),
+            pltpu.VMEM((SLOTS, 4, 16, SCOLS), low),
+            pltpu.VMEM((DEEP, 4, 16, SCOLS), low),
+            pltpu.VMEM((SLOTS, 3, 32, SCOLS), low),
+            pltpu.VMEM((SLOTS, 3, 32, SCOLS), low),
+            pltpu.VMEM((SLOTS, 3, 16, SCOLS), low),
+            pltpu.VMEM((SLOTS, 3, 16, SCOLS), low),
+            pltpu.VMEM((SLOTS, 32, SCOLS), low),
+            pltpu.VMEM((SLOTS, 16, SCOLS), low),
+            pltpu.VMEM((SLOTS, 64, SCOLS), jnp.float32),
+            pltpu.SemaphoreType.DMA((SLOTS, 2)),
+            pltpu.SemaphoreType.DMA((SLOTS,)),
+            pltpu.SemaphoreType.DMA((18, SLOTS)),
+            pltpu.SemaphoreType.DMA((18, SLOTS)),
+        ],
+        compiler_params=pltpu.CompilerParams(
+            collective_id=1, has_side_effects=True, vmem_limit_bytes=40 << 20
+        ),
+    )(*views)
+
+
+def reduce_all(grads):
+    low = [item.astype(jnp.bfloat16) for item in grads]
+    if lax.axis_size("seq") != 16 or lax.axis_size("utt") != 2:
+        return tuple(
+            lax.psum(
+                lax.psum_scatter(item, "seq", scatter_dimension=0, tiled=True), "utt"
+            ).astype(jnp.float32)
+            for item in low
+        )
+    wide = [index for index, item in enumerate(low) if item.ndim == 2]
+    flat = [index for index, item in enumerate(low) if item.ndim == 1]
+    small = jnp.concatenate([low[index].reshape(16, -1) for index in flat], axis=1)
+    small = jnp.pad(small, ((0, 0), (0, SROWS * SCOLS - small.shape[1])))
+    sums = reduce_grads([low[index] for index in wide] + [small.reshape(16 * SROWS, SCOLS)])
+    out = [None] * len(low)
+    for index, total in zip(wide, sums):
+        out[index] = total
+    first = 0
+    rest = sums[-1].reshape(-1)
+    for index in flat:
+        size = low[index].shape[0] // 16
+        out[index] = rest[first : first + size]
+        first += size
+    return tuple(out)
 
 
 def normalize(values, gain_vec):
@@ -353,120 +693,12 @@
     grad_inputs, glob_grads = block_back(
         global_in, glob_front, glob_mixed, glob_kept, glob_params, glob_cotan, global_back
     )
-    partial_sum = (
-        lax.psum_scatter(
-            grad_tab.astype(jnp.bfloat16), "seq", scatter_dimension=0, tiled=True
-        ).astype(jnp.float32),
-        lax.psum_scatter(
-            glob_grads[0].astype(jnp.bfloat16), "seq", scatter_dimension=0, tiled=True
-        ).astype(jnp.float32),
-        lax.psum_scatter(
-            glob_grads[1].astype(jnp.bfloat16), "seq", scatter_dimension=0, tiled=True
-        ).astype(jnp.float32),
-        lax.psum_scatter(
-            glob_grads[2].astype(jnp.bfloat16), "seq", scatter_dimension=0, tiled=True
-        ).astype(jnp.float32),
-        lax.psum_scatter(
-            glob_grads[3].astype(jnp.bfloat16), "seq", scatter_dimension=0, tiled=True
-        ).astype(jnp.float32),
-        lax.psum_scatter(
-            glob_grads[4].astype(jnp.bfloat16), "seq", scatter_dimension=0, tiled=True
-        ).astype(jnp.float32),
-        lax.psum_scatter(
-            glob_grads[5].astype(jnp.bfloat16), "seq", scatter_dimension=0, tiled=True
-        ).astype(jnp.float32),
-        lax.psum_scatter(
-            glob_grads[6].astype(jnp.bfloat16), "seq", scatter_dimension=0, tiled=True
-        ).astype(jnp.float32),
-        lax.psum_scatter(
-            glob_grads[7].astype(jnp.bfloat16), "seq", scatter_dimension=0, tiled=True
-        ).astype(jnp.float32),
-        lax.psum_scatter(
-            glob_grads[8].astype(jnp.bfloat16), "seq", scatter_dimension=0, tiled=True
-        ).astype(jnp.float32),
-        lax.psum_scatter(
-            glob_grads[9].astype(jnp.bfloat16), "seq", scatter_dimension=0, tiled=True
-        ).astype(jnp.float32),
-        lax.psum_scatter(
-            local_grads[0].astype(jnp.bfloat16), "seq", scatter_dimension=0, tiled=True
-        ).astype(jnp.float32),
-        lax.psum_scatter(
-            local_grads[1].astype(jnp.bfloat16), "seq", scatter_dimension=0, tiled=True
-        ).astype(jnp.float32),
-        lax.psum_scatter(
-            local_grads[2].astype(jnp.bfloat16), "seq", scatter_dimension=0, tiled=True
-        ).astype(jnp.float32),
-        lax.psum_scatter(
-            local_grads[3].astype(jnp.bfloat16), "seq", scatter_dimension=0, tiled=True
-        ).astype(jnp.float32),
-        lax.psum_scatter(
-            local_grads[4].astype(jnp.bfloat16), "seq", scatter_dimension=0, tiled=True
-        ).astype(jnp.float32),
-        lax.psum_scatter(
-            local_grads[5].astype(jnp.bfloat16), "seq", scatter_dimension=0, tiled=True
-        ).astype(jnp.float32),
-        lax.psum_scatter(
-            local_grads[6].astype(jnp.bfloat16), "seq", scatter_dimension=0, tiled=True
-        ).astype(jnp.float32),
-        lax.psum_scatter(
-            local_grads[7].astype(jnp.bfloat16), "seq", scatter_dimension=0, tiled=True
-        ).astype(jnp.float32),
-        lax.psum_scatter(
-            local_grads[8].astype(jnp.bfloat16), "seq", scatter_dimension=0, tiled=True
-        ).astype(jnp.float32),
-        lax.psum_scatter(
-            local_grads[9].astype(jnp.bfloat16), "seq", scatter_dimension=0, tiled=True
-        ).astype(jnp.float32),
-    )
-    reduced = (
-        lax.psum(partial_sum[0].astype(jnp.bfloat16), "utt").astype(jnp.float32),
-        lax.psum(partial_sum[1].astype(jnp.bfloat16), "utt").astype(jnp.float32),
-        lax.psum(partial_sum[2].astype(jnp.bfloat16), "utt").astype(jnp.float32),
-        lax.psum(partial_sum[3].astype(jnp.bfloat16), "utt").astype(jnp.float32),
-        lax.psum(partial_sum[4].astype(jnp.bfloat16), "utt").astype(jnp.float32),
-        lax.psum(partial_sum[5].astype(jnp.bfloat16), "utt").astype(jnp.float32),
-        lax.psum(partial_sum[6].astype(jnp.bfloat16), "utt").astype(jnp.float32),
-        lax.psum(partial_sum[7].astype(jnp.bfloat16), "utt").astype(jnp.float32),
-        lax.psum(partial_sum[8].astype(jnp.bfloat16), "utt").astype(jnp.float32),
-        lax.psum(partial_sum[9].astype(jnp.bfloat16), "utt").astype(jnp.float32),
-        lax.psum(partial_sum[10].astype(jnp.bfloat16), "utt").astype(jnp.float32),
-        lax.psum(partial_sum[11].astype(jnp.bfloat16), "utt").astype(jnp.float32),
-        lax.psum(partial_sum[12].astype(jnp.bfloat16), "utt").astype(jnp.float32),
-        lax.psum(partial_sum[13].astype(jnp.bfloat16), "utt").astype(jnp.float32),
-        lax.psum(partial_sum[14].astype(jnp.bfloat16), "utt").astype(jnp.float32),
-        lax.psum(partial_sum[15].astype(jnp.bfloat16), "utt").astype(jnp.float32),
-        lax.psum(partial_sum[16].astype(jnp.bfloat16), "utt").astype(jnp.float32),
-        lax.psum(partial_sum[17].astype(jnp.bfloat16), "utt").astype(jnp.float32),
-        lax.psum(partial_sum[18].astype(jnp.bfloat16), "utt").astype(jnp.float32),
-        lax.psum(partial_sum[19].astype(jnp.bfloat16), "utt").astype(jnp.float32),
-        lax.psum(partial_sum[20].astype(jnp.bfloat16), "utt").astype(jnp.float32),
-    )
+    reduced = reduce_all((grad_tab,) + glob_grads + local_grads)
     return (
         global_rows.reshape(utter_count, frame_count, model_width),
         local_rows.reshape(utter_count, frame_count, local_len, model_width),
         grad_inputs.reshape(utter_count, frame_count, model_width),
-        reduced[0],
-        reduced[1],
-        reduced[2],
-        reduced[3],
-        reduced[4],
-        reduced[5],
-        reduced[6],
-        reduced[7],
-        reduced[8],
-        reduced[9],
-        reduced[10],
-        reduced[11],
-        reduced[12],
-        reduced[13],
-        reduced[14],
-        reduced[15],
-        reduced[16],
-        reduced[17],
-        reduced[18],
-        reduced[19],
-        reduced[20],
-    )
+    ) + reduced
 
 
 def solution(mesh):

time: 1650 us -> 774 us (0.47)
  waiting for transfers between devices: 1090 us -> 48.6 us
  Pallas kernels: 0 us -> 254 us
  blocking collectives: 85.7 us -> 23 us
    reduce_scatter x13 -> x0, waiting for transfers between devices: 1030 us -> none  [the longest x1 109 us: on_device(): lax.psum_scatter(glob_grads[8].astype(jnp.bfloat16), 'seq', scatter_dimen...]
    pallas_call x0 -> x1, Pallas kernels: none -> 254 us  [reduce_grads(): pl.pallas_call(functools.partial(reduce_kernel, tuple(plan), total), out_...]
    unnamed x1 -> x0, blocking collectives: 57.7 us -> none
    convert_element_type x22 -> x1, other arithmetic: 25.8 us -> 8.33 us  [reduce_all(): low = [item.astype(jnp.bfloat16) for item in grads]]
  transfers between devices with their start and end apart: 17 -> 3, of which waited for: 17 -> 3; matrix products, arithmetic and copies ran while one was open for 9% -> 18% of each run, Pallas kernels for 0% -> 0%
where the time goes in v1:
time: 774 us; the launch traced here: 765 us
  Pallas kernels  254 us (33%)
  matrix products  240 us (31%)
  local copies, waits for them, and re-layouts  126 us (16%)
  other arithmetic  58.1 us (8%)
  waiting for transfers between devices  48.6 us (6%)
  blocking collectives  23 us (3%)
  between operations  15.4 us (2%)
    pallas_call x1, Pallas kernels, reduce_grads(): pl.pallas_call(functools.partial(reduce_kernel, tuple(plan), total), out_...  254 us
    dot_general x12, matrix products, project_back(): lax.dot_general(gradient, weight, (((1,), (1,)), ((), ())), preferred_ele...  55.7 us
    dot_general x12, matrix products, project(): return jnp.dot(left_side, weight, preferred_element_type=jnp.float32)  54.7 us
    dot_general x12, matrix products, weight_grad(): lax.dot_general(left_side, gradient, (((0,), (0,)), ((), ())), preferred_...  45.2 us
    all_gather x1, waiting for transfers between devices, on_device(): part_values = lax.all_gather(value_block, 'seq', axis=1, tiled=True)  33.7 us
    unnamed x211, local copies, waits for them, and re-layouts  23.6 us
    all_gather x1, blocking collectives, on_device(): part_usable = lax.all_gather(usable, 'seq', axis=1, tiled=True)  23 us
  transfers between devices with their start and end apart: 3, of which 3 were waited for; matrix products, arithmetic and copies ran while one was open for 18% of the time, Pallas kernels for 0%

profile of v1, /device:TPU:0, one launch (start us, length us, event | category | flops | bytes accessed | tf_op | source)
XLA Modules:
  0.0 764.6 jit_solution(9355354562755251308)
XLA Ops:
  17.0 23.0 %all-gather = bf16[16,64,2]{1,2,0:T(2,128)(2,1)S(1)} all-gather(bf16[1,64,2]{1,2,0:T(2,128)(2,1)S(1)} %convert_bitcast_fusion.3), channel_id=1, replica_groups=mesh['utt'=2,'seq'=16] {'seq'}, dimensions={0}, use_global_device_ids=true | all-gather | bytes 4352 | tf_op jit(solution)/shard_map/all_gather | solution.py:536
  44.4 6.4 gather_fusion
  59.0 8.6 %all-gather.6.cloned.1.call-done = bf16[2,1024,1024]{2,1,0:T(8,128)(2,1)} async-done(((bf16[2,64,1024]{2,1,0:T(8,128)(2,1)}), bf16[2,1024,1024]{2,1,0:T(8,128)(2,1)}) %all-gather.6.cloned.1.call-update) | async-done | bytes 4194320 | tf_op jit(solution)/shard_map/all_gather | solution.py:534
  67.6 6.2 copy.104
  73.9 7.1 select_reduce_fusion
  81.0 4.8 fusion.11
  85.8 33.7 %all-gather.4.cloned.1.call-done = bf16[2,1024,1024]{2,1,0:T(8,128)(2,1)} async-done(((bf16[2,64,1024]{2,1,0:T(8,128)(2,1)}), bf16[2,1024,1024]{2,1,0:T(8,128)(2,1)}) %all-gather.4.cloned.1.call-update) | async-done | bytes 4194320 | tf_op jit(solution)/shard_map/all_gather | solution.py:535
  119.5 6.5 copy.102
  126.0 8.3 %fusion.104 = (bf16[2,64,16,64]{1,3,2,0:T(8,128)(2,1)S(1)}, f32[2,64,16,64]{1,3,2,0:T(8,128)}) fusion(f32[2,64,16]{1,2,0:T(8,128)S(1)} %bitcast.209, bf16[2,1024,16,64]{1,3,2,0:T(8,128)(2,1)} %bitcast.187, f32[2,16,64,1024]{3,2,1,0:T(8,128)} %get-tuple-element.83, f32[2,16,64]{2,1,0:T(8,128)S(1)} %broadcast_maximum_fusion, ...), kind=kOutput, calls=%fused_computation.203 | convolution fusion | flops 279183360 | bytes 13516800 | tf_op jit(solution)/shard_map/uhqk,ukhd->uqhd/dot_general | solution.py:546
  138.0 4.8 convolution_add_fusion
  157.6 4.4 reshape.635
  162.0 4.1 convolution_convert_fusion.11
  166.1 4.0 reshape.637
  170.2 4.1 convolution_convert_fusion.12
  174.3 4.0 reshape.636
  178.4 12.0 %fusion.105 = (f32[128,16,4]{2,1,0:T(8,128)}, f32[128,16,4,4]{2,3,1,0:T(4,128)}) fusion(pred[4,4]{0,1:T(4,128)(4,1)S(1)} %copy-done.90, bf16[128,4,16,64]{3,2,1,0:T(8,128)(2,1)} %reshape.637, bf16[128,4,16,64]{3,2,1,0:T(8,128)(2,1)} %reshape.636), kind=kOutput, calls=%fused_computation.204 | convolution fusion | flops 4325379 | bytes 2261008 | tf_op jit(solution)/shard_map/sub | solution.py:368
  190.3 5.0 convert_bitcast_fusion.1
  197.3 4.1 convert_element_type.332
  205.4 11.1 %fusion.97 = f32[512,4096]{1,0:T(8,128)} fusion(bf16[1024,4096]{1,0:T(8,128)(2,1)} %param.48, f32[512,1024]{1,0:T(8,128)S(1)} %get-tuple-element.91, f32[1024]{0:T(1024)S(1)} %copy-done.71, f32[512]{0:T(512)S(1)} %fusion.84), kind=kOutput, calls=%fused_computation.198 | convolution fusion | flops 4296540160 | bytes 18880512 | tf_op jit(solution)/shard_map/dot_general | solution.py:373
  216.5 15.8 %fusion.106 = (bf16[4096]{0:T(1024)(128)(2,1)S(1)}, bf16[512,4096]{1,0:T(8,128)(2,1)}) fusion(f32[512,4096]{1,0:T(8,128)} %fusion.97, f32[4096]{0:T(1024)S(1)} %copy-done.83, bf16[4096,1024]{1,0:T(8,128)(2,1)} %param.50, f32[512,1024]{1,0:T(8,128)S(1)} %copy-done.16, pred[512]{0:T(512)(128)(4,1)S(1)} %copy-done.77), kind=kOutput, calls=%fused_computation.205 | convolution fusion | flops 4341624832 | bytes 23093760 | tf_op jit(solution)/shard_map/dot_general | solution.py:377
  232.4 7.2 multiply_reduce_fusion.1
  243.9 4.0 reshape.640
  247.9 6.7 convert_bitcast_fusion
  254.6 11.7 %multiply_reduce_fusion = (f32[128,16,4]{2,1,0:T(8,128)}, f32[128,16,4,4]{2,3,1,0:T(4,128)}) fusion(f32[128,16,4,4]{2,3,1,0:T(4,128)} %get-tuple-element.89, f32[128,16,4]{2,1,0:T(8,128)} %get-tuple-element.88, bf16[128,4,16,64]{3,2,1,0:T(8,128)(2,1)} %reshape.635, bf16[128,4,16,64]{3,2,1,0:T(8,128)(2,1)} %reshape.640), kind=kOutput, calls=%fused_computation.36 | convolution fusion | flops 4284416 | bytes 2424832 | tf_op jit(solution)/shard_map/nihd,njhd->nhij/dot_general | solution.py:590
  266.3 5.3 multiply_convert_fusion.5
  271.6 4.0 fusion.42
  281.2 4.1 convert_element_type.351
  288.8 4.1 convert_element_type.345
  292.9 4.7 fusion.115
  299.5 4.1 convert_element_type.348
  314.4 7.1 fusion.99
  321.5 6.8 multiply_reduce_fusion.8
  335.0 7.6 fusion.26
  342.6 6.8 multiply_convert_fusion.1
  349.3 6.7 copy.131
  356.1 5.4 multiply_convert_fusion
  361.5 6.2 copy.130
  367.7 8.2 %maximum_bitcast_fusion = bf16[1024,2,2048]{2,0,1:T(8,128)(2,1)} fusion(bf16[2,1024,1024]{2,1,0:T(8,128)(2,1)} %copy.131, bf16[2,1024,1024]{2,1,0:T(8,128)(2,1)} %copy.130), kind=kLoop, calls=%fused_computation.12 | loop fusion | flops 16777216 | bytes 16777216 | tf_op jit(solution)/shard_map/convert_element_type | solution.py:677
  381.8 12.9 %select_convert_fusion.1 = bf16[512,1024]{1,0:T(8,128)(2,1)S(1)} fusion(f32[512,1024]{1,0:T(8,128)S(1)} %copy-done.40, bf16[4096,1024]{1,0:T(8,128)(2,1)} %param.50, f32[1024]{0:T(1024)S(1)} %copy-done.85, pred[512]{0:T(512)(128)(4,1)S(1)} %copy-done.77, f32[512,4096]{1,0:T(8,128)} %fusion.97, f32[4096]{0:T(1024)S(1)} %copy-done.83), kind=kOutput, calls=%fused_computation.71 | convolution fusion | flops 4318035968 | bytes 19943936 | tf_op jit(solution)/shard_map/dot_general | solution.py:373
  395.9 5.8 fusion.58
  407.1 10.0 %scatter_custom_fusion = f32[3072,1024]{1,0:T(8,128)} fusion(s32[384]{0:T(512)S(1)} %reshape.676, f32[384,1024]{1,0:T(8,128)} %reshape.678, f32[]{:T(128)} %constant.24.clone.1), kind=kCustom, calls=%fused_computation.24 | custom fusion | flops 393216 | bytes 12583424 | tf_op jit(solution)/shard_map/scatter-add | solution.py:621
  417.1 8.3 %convert_element_type.367 = bf16[3072,1024]{1,0:T(8,128)(2,1)} convert(f32[3072,1024]{1,0:T(8,128)} %scatter_custom_fusion) | non-fusion elementwise | flops 3145728 | bytes 18874368 | tf_op jit(solution)/shard_map/convert_element_type | solution.py:331
  445.2 5.7 convolution_convert_fusion.3
  451.0 6.0 convolution_convert_fusion.2
  457.0 7.3 convolution_convert_fusion.1
  464.4 8.6 %convolution_convert_fusion = bf16[4096,1024]{1,0:T(8,128)(2,1)} fusion(f32[512,1024]{1,0:T(8,128)S(1)} %copy-done.17, pred[512]{0:T(512)(128)(4,1)S(1)} %copy-done.77, f32[512,4096]{1,0:T(8,128)S(1)} %bitcast.217, f32[4096]{0:T(1024)S(1)} %copy-done.83), kind=kOutput, calls=%fused_computation.19 | convolution fusion | flops 4320657408 | bytes 18891264 | tf_op jit(solution)/shard_map/dot_general | solution.py:383
  472.9 6.3 reduce-scatter.2.cloned.1.call-done
  491.3 253.8 %shard_map.442 = (f32[192,1024]{1,0:T(8,128)S(1)}, f32[64,1024]{1,0:T(8,128)S(1)}, f32[64,1024]{1,0:T(8,128)S(1)}, f32[64,1024]{1,0:T(8,128)S(1)}, f32[64,1024]{...) custom-call(bf16[8,2,192,1024]{3,2,1,0:T(8,128)(2,1)} %bitcast.182, ...), custom_call_target="tpu_custom_call" | custom-call | tf_op jit(solution)/shard_map/pallas_call | solution.py:296
  (328 shorter events, 135.7 us)
Async XLA Ops:
  7.2 148.2 %copy-start = (bf16[1024,1024]{1,0:T(8,128)(2,1)S(1)}, bf16[1024,1024]{1,0:T(8,128)(2,1)}, u32[]{:S(2)}) copy-start(bf16[1024,1024]{1,0:T(8,128)(2,1)} %param.45) | copy-start | bytes 6291460
  7.2 60.4 %all-gather.6.cloned.1.call-start = ((), (), s32[]{:S(2)}) async-start(), calls=%async_computation.2 | async-start | bytes 4456448 | tf_op jit(solution)/shard_map/all_gather | solution.py:534
  14.1 105.4 %all-gather.4.cloned.1.call-start = ((), (), s32[]{:S(2)}) async-start(), calls=%async_computation.1 | async-start | bytes 4456448 | tf_op jit(solution)/shard_map/all_gather | solution.py:535
  16.9 462.4 %reduce-scatter.2.cloned.1.call-start = ((), (), s32[]{:S(2)}) async-start(), calls=%async_computation.3 | async-start | bytes 8912896 | tf_op jit(solution)/shard_map/reduce_scatter | solution.py:676
  43.0 30.8 %copy-start.26 = (bf16[2,64,16,64]{1,3,2,0:T(8,128)(2,1)}, bf16[2,64,16,64]{1,3,2,0:T(8,128)(2,1)S(1)}, u32[]{:S(2)}) copy-start(bf16[2,64,16,64]{1,3,2,0:T(8,128)(2,1)S(1)} %copy.128) | copy-start | bytes 786436
  43.2 13.0 %copy-start.78 = (pred[128]{0:T(512)(128)(4,1)}, pred[128]{0:T(512)(128)(4,1)S(1)}, u32[]{:S(2)}) copy-start(pred[128]{0:T(512)(128)(4,1)S(1)} %lt.51) | copy-start | bytes 388
  56.2 69.7 %copy-start.34 = (pred[2,64,1024]{2,1,0:T(8,128)(4,1)}, pred[2,64,1024]{2,1,0:T(8,128)(4,1)S(1)}, u32[]{:S(2)}) copy-start(pred[2,64,1024]{2,1,0:T(8,128)(4,1)S(1)} %or_and_fusion) | copy-start | bytes 393220
  85.8 40.2 %copy-start.64 = (f32[2,16,64]{2,1,0:T(8,128)}, f32[2,16,64]{2,1,0:T(8,128)S(1)}, u32[]{:S(2)}) copy-start(f32[2,16,64]{2,1,0:T(8,128)S(1)} %fusion.11) | copy-start | bytes 24580
  126.0 9.2 %copy-start.11 = (bf16[2,64,1024]{2,1,0:T(8,128)(2,1)S(1)}, bf16[2,64,1024]{2,1,0:T(8,128)(2,1)}, u32[]{:S(2)}) copy-start(bf16[2,64,1024]{2,1,0:T(8,128)(2,1)} %param.27) | copy-start | bytes 786436
  135.1 7.7 %copy-start.37 = (bf16[128,1024]{1,0:T(8,128)(2,1)}, bf16[128,1024]{1,0:T(8,128)(2,1)S(1)}, u32[]{:S(2)}) copy-start(bf16[128,1024]{1,0:T(8,128)(2,1)S(1)} %convert_element_type.318) | copy-start | bytes 786436
  135.2 7.7 %slice-start.2 = ((s8[8388608]{0:T(1024)(128)(4,1)}), s8[4194304]{0:T(1024)(128)(4,1)S(1)}, s32[]{:S(2)}) async-start(s8[8388608]{0:T(1024)(128)(4,1)} %bitcast.214), calls=%async_computation.6 | async-start | bytes 8388608
  138.0 4.9 copy-start.79
  138.0 4.9 slice-start.3
  138.0 4.9 copy-start.84
  205.3 34.3 %copy-start.39 = (f32[512,1024]{1,0:T(8,128)}, f32[512,1024]{1,0:T(8,128)S(1)}, u32[]{:S(2)}) copy-start(f32[512,1024]{1,0:T(8,128)S(1)} %get-tuple-element.91) | copy-start | bytes 6291460
  205.3 34.3 %copy-start.67 = (f32[512]{0:T(512)}, f32[512]{0:T(512)S(1)}, u32[]{:S(2)}) copy-start(f32[512]{0:T(512)S(1)} %fusion.84) | copy-start | bytes 6148
  205.4 11.1 %copy-start.16 = (f32[512,1024]{1,0:T(8,128)S(1)}, f32[512,1024]{1,0:T(8,128)}, u32[]{:S(2)}) copy-start(f32[512,1024]{1,0:T(8,128)} %reshape.639) | copy-start | bytes 6291460
  205.4 11.1 %copy-start.77 = (pred[512]{0:T(512)(128)(4,1)S(1)}, pred[512]{0:T(512)(128)(4,1)}, u32[]{:S(2)}) copy-start(pred[512]{0:T(512)(128)(4,1)} %broadcast_in_dim.177) | copy-start | bytes 1540
  205.4 11.1 %copy-start.83 = (f32[4096]{0:T(1024)S(1)}, f32[4096]{0:T(1024)}, u32[]{:S(2)}) copy-start(f32[4096]{0:T(1024)} %param.49) | copy-start | bytes 49156
  205.4 27.0 %slice-start = ((s8[8388608]{0:T(1024)(128)(4,1)}), s8[4194304]{0:T(1024)(128)(4,1)S(1)}, s32[]{:S(2)}) async-start(s8[8388608]{0:T(1024)(128)(4,1)} %bitcast.212), calls=%async_computation.4 | async-start | bytes 8388608
  216.5 15.9 %slice-start.1 = ((s8[8388608]{0:T(1024)(128)(4,1)}), s8[4194304]{0:T(1024)(128)(4,1)S(1)}, s32[]{:S(2)}) async-start(s8[8388608]{0:T(1024)(128)(4,1)} %bitcast.212), calls=%async_computation.5 | async-start | bytes 8388608
  266.3 5.3 copy-start.42
  292.9 4.7 copy-start.45
  314.4 7.1 copy-start.49
  321.5 6.8 copy-start.32
  321.5 6.8 copy-start.81
  335.0 7.6 copy-start.7
  349.3 6.7 copy-start.27
  379.1 49.2 %copy-start.28 = (bf16[2,64,1024]{2,1,0:T(8,128)(2,1)}, bf16[2,64,1024]{2,1,0:T(8,128)(2,1)S(1)}, u32[]{:S(2)}) copy-start(bf16[2,64,1024]{2,1,0:T(8,128)(2,1)S(1)} %fusion.78) | copy-start | bytes 786436
  395.9 9.5 %copy-start.19 = (f32[2,64,3,1024]{3,2,1,0:T(4,128)S(1)}, f32[2,64,3,1024]{3,2,1,0:T(4,128)}, u32[]{:S(2)}) copy-start(f32[2,64,3,1024]{3,2,1,0:T(4,128)} %slice.53) | copy-start | bytes 4718596
  405.4 22.9 %copy-start.36 = (bf16[128,1024]{1,0:T(8,128)(2,1)}, bf16[128,1024]{1,0:T(8,128)(2,1)S(1)}, u32[]{:S(2)}) copy-start(bf16[128,1024]{1,0:T(8,128)(2,1)S(1)} %convert_element_type.360) | copy-start | bytes 786436
  417.1 8.3 %copy-start.6 = (bf16[2,64,3,1024]{3,2,1,0:T(4,128)(2,1)S(1)}, bf16[2,64,3,1024]{3,2,1,0:T(4,128)(2,1)}, u32[]{:S(2)}) copy-start(bf16[2,64,3,1024]{3,2,1,0:T(4,128)(2,1)} %broadcast_select_fusion) | copy-start | bytes 2359300
  417.1 8.3 %copy-start.21 = (bf16[2,64,1,1024]{3,2,1,0:T(2,128)(2,1)S(1)}, bf16[2,64,1,1024]{3,2,1,0:T(2,128)(2,1)}, u32[]{:S(2)}) copy-start(bf16[2,64,1,1024]{3,2,1,0:T(2,128)(2,1)} %copy-done.20) | copy-start | bytes 786436
  417.1 8.3 %copy-start.61 = (f32[2,64,4]{2,1,0:T(8,128)S(1)}, f32[2,64,4]{2,1,0:T(8,128)}, u32[]{:S(2)}) copy-start(f32[2,64,4]{2,1,0:T(8,128)} %get-tuple-element.76) | copy-start | bytes 6148
  445.2 5.7 copy-start.10
  445.2 5.7 copy-start.50
  450.9 6.1 copy-start.41
  451.0 6.1 copy-start.68
  451.0 6.1 copy-start.72
  451.0 6.1 copy-start.91
  451.0 13.4 %slice-start.4 = ((s8[8388608]{0:T(1024)(128)(4,1)}), s8[4194304]{0:T(1024)(128)(4,1)S(1)}, s32[]{:S(2)}) async-start(s8[8388608]{0:T(1024)(128)(4,1)} %bitcast.216), calls=%async_computation.8 | async-start | bytes 8388608
  457.0 7.3 copy-start.17
  457.0 7.3 slice-start.5
  464.4 16.0 %copy-start.29 = (bf16[2,64,1024]{2,1,0:T(8,128)(2,1)S(1)}, bf16[2,64,1024]{2,1,0:T(8,128)(2,1)}, u32[]{:S(2)}) copy-start(bf16[2,64,1024]{2,1,0:T(8,128)(2,1)} %copy-done.28) | copy-start | bytes 786436
  480.4 4.2 copy-start.23
  480.4 4.2 copy-start.48
  491.3 255.1 %copy-start.89 = (f32[128]{0:T(128)S(1)}, f32[128]{0:T(128)}, u32[]{:S(2)}) copy-start(f32[128]{0:T(128)} %copy-done.88) | copy-start | bytes 1540
  491.3 255.1 %copy-start.46 = (f32[128,1024]{1,0:T(8,128)S(1)}, f32[128,1024]{1,0:T(8,128)}, u32[]{:S(2)}) copy-start(f32[128,1024]{1,0:T(8,128)} %get-tuple-element.97) | copy-start | bytes 1572868
  (53 other events, 128.4 us)
Sparse Core Ops, SparseCore 0:
  14.2 53.3 all-gather.5
  70.4 49.0 all-gather.3
  376.1 103.1 reduce-scatter.1

commit v2 on v1

--- a/solution.py
+++ b/solution.py
@@ -15,6 +15,8 @@
 
 EPSILON = 1e-05
 NEGATIVE = -1e30
+F32 = jnp.float32
+LOW = jnp.bfloat16
 MESH_ID = pl.DeviceIdType.MESH
 SLOTS = 4
 SROWS = 64
@@ -351,6 +353,280 @@
         out[index] = rest[first : first + size]
         first += size
     return tuple(out)
+
+
+def mul(left_side, right_side):
+    return jnp.dot(left_side, right_side, preferred_element_type=F32)
+
+
+def mul_t(left_side, right_side):
+    return lax.dot_general(
+        left_side, right_side, (((1,), (1,)), ((), ())), preferred_element_type=F32
+    )
+
+
+def t_mul(left_side, right_side):
+    return lax.dot_general(
+        left_side, right_side, (((0,), (0,)), ((), ())), preferred_element_type=F32
+    )
+
+
+def scale_of(values):
+    return lax.rsqrt(jnp.mean(values * values, axis=-1, keepdims=True) + EPSILON)
+
+
+def scale_back(values, gain, grad):
+    scale = scale_of(values)
+    inner = grad * gain
+    shared = jnp.mean(values * inner, axis=-1, keepdims=True) * (scale * scale * scale)
+    return inner * scale - values * shared, grad * values * scale
+
+
+def head_sums(width):
+    rows = lax.broadcasted_iota(jnp.int32, (width, 128), 0) // HD
+    cols = lax.broadcasted_iota(jnp.int32, (width, 128), 1)
+    return (rows == cols).astype(LOW)
+
+
+def head_spread(width):
+    rows = lax.broadcasted_iota(jnp.int32, (128, width), 0)
+    cols = lax.broadcasted_iota(jnp.int32, (128, width), 1) // HD
+    return (rows == cols).astype(LOW)
+
+
+def sum_heads(product, sums):
+    high = product.astype(LOW)
+    rest = (product - high.astype(F32)).astype(LOW)
+    return mul(high, sums) + mul(rest, sums)
+
+
+def front_kernel(
+    x_ref, n1_ref, wq_ref, wk_ref, wv_ref, wo_ref, n2_ref,
+    normed_ref, q_ref, k_ref, v_ref, probs_ref, mixed_ref, mid_ref, mid_norm_ref,
+):
+    places, frames, width = x_ref.shape
+    rows = places * frames
+    x = x_ref[...].astype(F32).reshape(rows, width)
+    normed = (x * scale_of(x) * n1_ref[...]).astype(LOW)
+    normed_ref[...] = normed.reshape(places, frames, width)
+    q_ref[...] = mul(normed, wq_ref[...]).astype(LOW).reshape(places, frames, width)
+    k_ref[...] = mul(normed, wk_ref[...]).astype(LOW).reshape(places, frames, width)
+    v_ref[...] = mul(normed, wv_ref[...]).astype(LOW).reshape(places, frames, width)
+    sums, spread = head_sums(width), head_spread(width)
+    pair = 0
+    for i in range(places):
+        query = q_ref[i].astype(F32)
+        scores = [
+            sum_heads(query * k_ref[j].astype(F32), sums) * HD ** (-0.5) for j in range(i + 1)
+        ]
+        peak = scores[0]
+        for item in scores[1:]:
+            peak = jnp.maximum(peak, item)
+        raised = [jnp.exp(item - peak) for item in scores]
+        total = raised[0]
+        for item in raised[1:]:
+            total = total + item
+        mixed = None
+        for j in range(i + 1):
+            probs = raised[j] / total
+            probs_ref[pair] = probs
+            pair += 1
+            term = mul(probs.astype(LOW), spread) * v_ref[j].astype(F32)
+            mixed = term if mixed is None else mixed + term
+        mixed_ref[i] = mixed.astype(LOW)
+    mid = x + mul(mixed_ref[...].reshape(rows, width), wo_ref[...])
+    mid_ref[...] = mid.reshape(places, frames, width)
+    mid_norm_ref[...] = (
+        (mid * scale_of(mid) * n2_ref[...]).astype(LOW).reshape(places, frames, width)
+    )
+
+
+def local_front(x, params):
+    places, frames, width = x.shape
+    pairs = places * (places + 1) // 2
+    step = 64
+    rows = pl.BlockSpec((places, step, width), lambda i: (0, i, 0))
+    whole = lambda item: pl.BlockSpec(item.shape, lambda i: (0, 0), pipeline_mode=pl.Buffered(1))
+    n1, n2 = params[0].reshape(1, -1), params[5].reshape(1, -1)
+    operands = (x, n1, params[1], params[2], params[3], params[4], n2)
+    like = lambda kind: jax.ShapeDtypeStruct((places, frames, width), kind)
+    return pl.pallas_call(
+        front_kernel,
+        grid=(frames // step,),
+        in_specs=[rows] + [whole(item) for item in operands[1:]],
+        out_specs=[rows] * 4
+        + [pl.BlockSpec((pairs, step, 128), lambda i: (0, i, 0))]
+        + [rows] * 3,
+        out_shape=[
+            like(LOW), like(LOW), like(LOW), like(LOW),
+            jax.ShapeDtypeStruct((pairs, frames, 128), F32),
+            like(LOW), like(F32), like(LOW),
+        ],
+        compiler_params=pltpu.CompilerParams(vmem_limit_bytes=56 << 20),
+    )(*operands)
+
+
+def gelu_parts(u):
+    scale = 0.7978845608028654
+    inner = jnp.tanh(scale * (u + 0.044715 * u * u * u))
+    half = 0.5 * (1.0 + inner)
+    slope = half + 0.5 * u * (1.0 - inner * inner) * scale * (1.0 + 3 * 0.044715 * u * u)
+    return u * half, slope
+
+
+def ffn_kernel(
+    hn_ref, dout_ref, mid_ref, w1_ref, b1_ref, w2_ref, b2_ref,
+    y_ref, dhn_ref, dw1_ref, dw2_ref, db1_ref, acc_ref, hn_t_ref,
+):
+    at = pl.program_id(0)
+    last = pl.num_programs(0) - 1
+
+    @pl.when(at == 0)
+    def _():
+        hn_t_ref[...] = hn_ref[...].T
+        acc_ref[...] = mid_ref[...] + b2_ref[...]
+        dhn_ref[...] = jnp.zeros_like(dhn_ref)
+
+    hn, dout = hn_ref[...], dout_ref[...]
+    u = mul(hn, w1_ref[...]) + b1_ref[...]
+    act, slope = gelu_parts(u)
+    act = act.astype(LOW)
+    acc_ref[...] += mul(act, w2_ref[...])
+    du = (mul_t(dout, w2_ref[...]) * slope).astype(LOW)
+    db1_ref[...] = jnp.sum(du.astype(F32), axis=0, keepdims=True)
+    dhn_ref[...] += mul_t(du, w1_ref[...])
+    dw1_ref[...] = mul(hn_t_ref[...], du).astype(LOW)
+    dw2_ref[...] = t_mul(act, dout).astype(LOW)
+
+    @pl.when(at == last)
+    def _():
+        y_ref[...] = acc_ref[...].astype(LOW)
+
+
+def local_ffn(hn, dout, mid, params):
+    rows, width = hn.shape
+    wide = params[6].shape[1]
+    step = 512
+    whole = pl.BlockSpec((rows, width), lambda i: (0, 0), pipeline_mode=pl.Buffered(1))
+    out_whole = pl.BlockSpec((rows, width), lambda i: (0, 0))
+    return pl.pallas_call(
+        ffn_kernel,
+        grid=(wide // step,),
+        in_specs=[
+            whole, whole, whole,
+            pl.BlockSpec((width, step), lambda i: (0, i)),
+            pl.BlockSpec((1, step), lambda i: (0, i)),
+            pl.BlockSpec((step, width), lambda i: (i, 0)),
+            pl.BlockSpec((1, width), lambda i: (0, 0)),
+        ],
+        out_specs=[
+            out_whole, out_whole,
+            pl.BlockSpec((width, step), lambda i: (0, i)),
+            pl.BlockSpec((step, width), lambda i: (i, 0)),
+            pl.BlockSpec((1, step), lambda i: (0, i)),
+        ],
+        out_shape=[
+            jax.ShapeDtypeStruct((rows, width), LOW),
+            jax.ShapeDtypeStruct((rows, width), F32),
+            jax.ShapeDtypeStruct((width, wide), LOW),
+            jax.ShapeDtypeStruct((wide, width), LOW),
+            jax.ShapeDtypeStruct((1, wide), F32),
+        ],
+        scratch_shapes=[pltpu.VMEM((rows, width), F32), pltpu.VMEM((width, rows), LOW)],
+        compiler_params=pltpu.CompilerParams(vmem_limit_bytes=56 << 20),
+    )(hn, dout, mid, params[6], params[7].reshape(1, -1), params[8], params[9].reshape(1, -1))
+
+
+def back_kernel(
+    x_ref, mid_ref, dhn_ref, dout_ref, q_ref, k_ref, v_ref, probs_ref,
+    n1_ref, n2_ref, wq_ref, wk_ref, wv_ref, wo_ref,
+    dattn_ref, dq_ref, dk_ref, dv_ref, first_ref, rest_ref, dn1_ref, dn2_ref,
+    dmid_ref,
+):
+    places, frames, width = x_ref.shape
+    rows = places * frames
+
+    @pl.when(pl.program_id(0) == 0)
+    def _():
+        dn1_ref[...] = jnp.zeros_like(dn1_ref)
+        dn2_ref[...] = jnp.zeros_like(dn2_ref)
+
+    mid = mid_ref[...].reshape(rows, width)
+    dmid, gain = scale_back(mid, n2_ref[...], dhn_ref[...].reshape(rows, width))
+    dn2_ref[...] += jnp.sum(gain, axis=0, keepdims=True)
+    dmid = dmid + dout_ref[...].astype(F32).reshape(rows, width)
+    dmid_ref[...] = dmid
+    dattn = dmid.astype(LOW)
+    dattn_ref[...] = dattn.reshape(places, frames, width)
+    dmixed = mul_t(dattn, wo_ref[...]).astype(LOW).reshape(places, frames, width)
+    sums, spread = head_sums(width), head_spread(width)
+    pair = 0
+    dk, dv = [None] * places, [None] * places
+    add = lambda old, term: term if old is None else old + term
+    for i in range(places):
+        grad = dmixed[i].astype(F32)
+        query = q_ref[i].astype(F32)
+        dp = [sum_heads(grad * v_ref[j].astype(F32), sums) for j in range(i + 1)]
+        delta = None
+        for j in range(i + 1):
+            delta = add(delta, probs_ref[pair + j] * dp[j])
+        dq = None
+        for j in range(i + 1):
+            probs = probs_ref[pair + j]
+            ds = (probs * (dp[j] - delta)).astype(LOW)
+            ds = mul(ds, spread)
+            dq = add(dq, ds * k_ref[j].astype(F32))
+            dk[j] = add(dk[j], ds * query)
+            dv[j] = add(dv[j], mul(probs.astype(LOW), spread) * grad)
+        pair += i + 1
+        dq_ref[i] = (dq * HD ** (-0.5)).astype(LOW)
+    for j in range(places):
+        dk_ref[j] = (dk[j] * HD ** (-0.5)).astype(LOW)
+        dv_ref[j] = dv[j].astype(LOW)
+    dnormed = (
+        mul_t(dq_ref[...].reshape(rows, width), wq_ref[...])
+        + mul_t(dk_ref[...].reshape(rows, width), wk_ref[...])
+        + mul_t(dv_ref[...].reshape(rows, width), wv_ref[...])
+    )
+    x = x_ref[...].astype(F32).reshape(rows, width)
+    dx, gain = scale_back(x, n1_ref[...], dnormed)
+    dn1_ref[...] += jnp.sum(gain, axis=0, keepdims=True)
+    dx = (dx + dmid_ref[...]).reshape(places, frames, width)
+    first_ref[...] = dx[0]
+    rest_ref[...] = dx[1:].astype(LOW)
+
+
+def local_back(x, mid, dhn, dout, q, k, v, probs, params):
+    places, frames, width = x.shape
+    pairs = probs.shape[0]
+    step = 64
+    rows = pl.BlockSpec((places, step, width), lambda i: (0, i, 0))
+    whole = lambda item: pl.BlockSpec(item.shape, lambda i: (0, 0), pipeline_mode=pl.Buffered(1))
+    like = lambda kind: jax.ShapeDtypeStruct((places, frames, width), kind)
+    fixed = (params[0].reshape(1, -1), params[5].reshape(1, -1)) + tuple(params[1:5])
+    vector = pl.BlockSpec((1, width), lambda i: (0, 0))
+    return pl.pallas_call(
+        back_kernel,
+        grid=(frames // step,),
+        in_specs=[rows] * 7
+        + [pl.BlockSpec((pairs, step, 128), lambda i: (0, i, 0))]
+        + [whole(item) for item in fixed],
+        out_specs=[rows] * 4
+        + [
+            pl.BlockSpec((step, width), lambda i: (i, 0)),
+            pl.BlockSpec((places - 1, step, width), lambda i: (0, i, 0)),
+            vector, vector,
+        ],
+        out_shape=[
+            like(LOW), like(LOW), like(LOW), like(LOW),
+            jax.ShapeDtypeStruct((frames, width), F32),
+            jax.ShapeDtypeStruct((places - 1, frames, width), LOW),
+            jax.ShapeDtypeStruct((1, width), F32),
+            jax.ShapeDtypeStruct((1, width), F32),
+        ],
+        scratch_shapes=[pltpu.VMEM((places * step, width), F32)],
+        compiler_params=pltpu.CompilerParams(vmem_limit_bytes=60 << 20),
+    )(x, mid, dhn, dout, q, k, v, probs, *fixed)
 
 
 def normalize(values, gain_vec):
@@ -554,77 +830,58 @@
     glob_mixed = attn_heads.reshape(row_count, model_width).astype(jnp.bfloat16)
     glob_result, glob_kept = block_outputs(global_in, glob_mixed, glob_params)
     global_rows = jnp.where(valid.reshape(row_count, 1), glob_result, 0.0).astype(jnp.bfloat16)
-    table_ids = codes + VOCAB * jnp.arange(CB, dtype=jnp.int32)[None, None, :]
-    embedded = jnp.take(table, table_ids.reshape(-1), axis=0).reshape(
-        utter_count, frame_count, CB, model_width
-    )
-    local_in = jnp.concatenate(
-        [global_rows.reshape(utter_count, frame_count, 1, model_width), embedded], axis=2
-    )
-    local_in = local_in.astype(jnp.float32).reshape(row_count * local_len, model_width)
-    local_front = block_inputs(local_in, local_params)
-    local_q = local_front[1].reshape(row_count, local_len, H, HD)
-    local_k = local_front[2].reshape(row_count, local_len, H, HD)
-    local_v = local_front[3].reshape(row_count, local_len, H, HD)
-    lower = (
-        jnp.arange(local_len, dtype=jnp.int32)[:, None]
-        >= jnp.arange(local_len, dtype=jnp.int32)[None, :]
-    )
-    local_scores = jnp.einsum(
-        "nihd,njhd->nhij", local_q, local_k, preferred_element_type=jnp.float32
-    ) * HD ** (-0.5)
-    local_probs = softmax_rows(jnp.where(lower, local_scores, NEGATIVE))
-    local_mixed = jnp.einsum(
-        "nhij,njhd->nihd",
-        local_probs.astype(jnp.bfloat16),
+    code_rows = codes.transpose(2, 0, 1).reshape(CB, row_count)
+    table_ids = code_rows + VOCAB * jnp.arange(CB, dtype=jnp.int32)[:, None]
+    embedded = table.at[table_ids].get(mode="promise_in_bounds")
+    local_in = jnp.concatenate([global_rows[None], embedded], axis=0)
+    local_shape = (local_len, row_count, model_width)
+    flat_shape = (local_len * row_count, model_width)
+    normed, local_q, local_k, local_v, local_probs, mixed, middle, middle_norm = local_front(
+        local_in, local_params
+    )
+    row_valid = valid.reshape(1, row_count, 1)
+    local_cotan = cotan_local.transpose(2, 0, 1, 3).reshape(local_shape)
+    local_cotan = jnp.where(row_valid, local_cotan, 0)
+    local_result, grad_hidden, grad_w_up, grad_w_down, grad_b_up = local_ffn(
+        middle_norm.reshape(flat_shape),
+        local_cotan.reshape(flat_shape),
+        middle.reshape(flat_shape),
+        local_params,
+    )
+    local_rows = jnp.where(row_valid, local_result.reshape(local_shape), 0)
+    local_rows = local_rows.reshape(local_len, utter_count, frame_count, model_width)
+    local_rows = local_rows.transpose(1, 2, 0, 3)
+    grad_attn, grad_q, grad_k, grad_v, grad_first, grad_rest, grad_n1, grad_n2 = local_back(
+        local_in,
+        middle,
+        grad_hidden.reshape(local_shape),
+        local_cotan,
+        local_q,
+        local_k,
         local_v,
-        preferred_element_type=jnp.float32,
-    )
-    local_mixed = local_mixed.reshape(row_count * local_len, model_width).astype(jnp.bfloat16)
-    local_result, local_kept = block_outputs(local_in, local_mixed, local_params)
-    local_valid = jnp.repeat(valid.reshape(-1), local_len)[:, None]
-    local_rows = jnp.where(local_valid, local_result, 0.0).astype(jnp.bfloat16)
-
-    def local_back(grad_mixed):
-        grad_heads = grad_mixed.reshape(row_count, local_len, H, HD)
-        grad_probs = jnp.einsum(
-            "nihd,njhd->nhij", grad_heads, local_v, preferred_element_type=jnp.float32
-        )
-        grads_s = (
-            local_probs * (grad_probs - jnp.sum(local_probs * grad_probs, axis=-1, keepdims=True))
-        ).astype(jnp.bfloat16)
-        grad_query = jnp.einsum(
-            "nhij,njhd->nihd", grads_s, local_k, preferred_element_type=jnp.float32
-        ) * HD ** (-0.5)
-        grad_key = jnp.einsum(
-            "nhij,nihd->njhd", grads_s, local_q, preferred_element_type=jnp.float32
-        ) * HD ** (-0.5)
-        grad_value = jnp.einsum(
-            "nhij,nihd->njhd",
-            local_probs.astype(jnp.bfloat16),
-            grad_heads,
-            preferred_element_type=jnp.float32,
-        )
-        return (
-            grad_query.reshape(-1, model_width).astype(jnp.bfloat16),
-            grad_key.reshape(-1, model_width).astype(jnp.bfloat16),
-            grad_value.reshape(-1, model_width).astype(jnp.bfloat16),
-        )
-
-    local_cotan = jnp.where(
-        local_valid, cotan_local.astype(jnp.float32).reshape(-1, model_width), 0.0
-    )
-    grad_local_in, local_grads = block_back(
-        local_in, local_front, local_mixed, local_kept, local_params, local_cotan, local_back
-    )
-    grad_local_in = grad_local_in.reshape(utter_count, frame_count, local_len, model_width)
-    grad_tab = jax.ops.segment_sum(
-        grad_local_in[:, :, 1:].reshape(-1, model_width),
-        table_ids.reshape(-1),
-        num_segments=CB * VOCAB,
-    )
+        local_probs,
+        local_params,
+    )
+    normed = normed.reshape(flat_shape)
+    local_grads = (
+        grad_n1[0],
+        weight_grad(normed, grad_q.reshape(flat_shape)),
+        weight_grad(normed, grad_k.reshape(flat_shape)),
+        weight_grad(normed, grad_v.reshape(flat_shape)),
+        weight_grad(mixed.reshape(flat_shape), grad_attn.reshape(flat_shape)),
+        grad_n2[0],
+        grad_w_up,
+        grad_b_up[0],
+        grad_w_down,
+        jnp.sum(local_cotan.astype(F32), axis=(0, 1)),
+    )
+    picked = code_rows[:, None, :] == jnp.arange(VOCAB, dtype=jnp.int32)[None, :, None]
+    grad_tab = jnp.einsum(
+        "cvn,cnd->cvd", picked.astype(LOW), grad_rest, preferred_element_type=F32
+    ).reshape(CB * VOCAB, model_width)
+    grad_first = grad_first.reshape(utter_count, frame_count, model_width)
     glob_cotan = jnp.where(
-        valid[:, :, None], cotan_global.astype(jnp.float32) + grad_local_in[:, :, 0], 0.0
+        valid[:, :, None], cotan_global.astype(jnp.float32) + grad_first, 0.0
     )
     glob_cotan = glob_cotan.reshape(row_count, model_width)
 
@@ -696,7 +953,7 @@
     reduced = reduce_all((grad_tab,) + glob_grads + local_grads)
     return (
         global_rows.reshape(utter_count, frame_count, model_width),
-        local_rows.reshape(utter_count, frame_count, local_len, model_width),
+        local_rows,
         grad_inputs.reshape(utter_count, frame_count, model_width),
     ) + reduced
 

time: 774 us -> 664 us (0.86)
  matrix products: 240 us -> 105 us
  Pallas kernels: 254 us -> 322 us
  local copies, waits for them, and re-layouts: 126 us -> 64.7 us
  waiting for transfers between devices: 48.6 us -> 103 us
  other arithmetic: 58.1 us -> 26.7 us
    pallas_call x0 -> x3, Pallas kernels: none -> 68.5 us  [the longest x1 35.4 us: local_ffn(): pl.pallas_call(ffn_kernel, grid=(wide // step,), in_specs=[whole, whole,...]
    reduce_scatter x1, waiting for transfers between devices: 6.34 us -> 51.1 us  [global_back(): lax.psum_scatter(joined.transpose(1, 0, 2).astype(jnp.bfloat16), 'seq', s...]
    dot_general x12 -> x6, matrix products: 54.7 us -> 14.7 us  [project(): return jnp.dot(left_side, weight, preferred_element_type=jnp.float32)]
    dot_general x12 -> x6, matrix products: 55.7 us -> 18.7 us  [project_back(): lax.dot_general(gradient, weight, (((1,), (1,)), ((), ())), preferred_ele...]
    convert_element_type x10 -> x0, local copies, waits for them, and re-layouts: 29.7 us -> none  [the longest x2 7.6 us: local_back(): grad_query.reshape(-1, model_width).astype(jnp.bfloat16)]
    dot_general x5 -> x1, matrix products: 31.1 us -> 4.49 us  [on_device(): jnp.einsum('cvn,cnd->cvd', picked.astype(LOW), grad_rest, preferred_eleme...]
    reshape x11 -> x1, local copies, waits for them, and re-layouts: 24.8 us -> 0.08 us  [on_device(): code_rows = codes.transpose(2, 0, 1).reshape(CB, row_count)]
    dot_general x12 -> x10, matrix products: 45.2 us -> 31.9 us  [weight_grad(): lax.dot_general(left_side, gradient, (((0,), (0,)), ((), ())), preferred_...]
  transfers between devices with their start and end apart: 3 -> 3, of which waited for: 3 -> 3; matrix products, arithmetic and copies ran while one was open for 18% -> 12% of each run, Pallas kernels for 0% -> 0%
where the time goes in v2:
time: 664 us; the launch traced here: 659 us
  Pallas kernels  322 us (48%)
  matrix products  105 us (16%)
  waiting for transfers between devices  103 us (16%)
  local copies, waits for them, and re-layouts  64.7 us (10%)
  other arithmetic  26.7 us (4%)
  blocking collectives  23.1 us (3%)
  between operations  14.9 us (2%)
    pallas_call x1, Pallas kernels, reduce_grads(): pl.pallas_call(functools.partial(reduce_kernel, tuple(plan), total), out_...  254 us
    reduce_scatter x1, waiting for transfers between devices, global_back(): lax.psum_scatter(joined.transpose(1, 0, 2).astype(jnp.bfloat16), 'seq', s...  51.1 us
    all_gather x1, waiting for transfers between devices, on_device(): part_values = lax.all_gather(value_block, 'seq', axis=1, tiled=True)  37.8 us
    pallas_call x1, Pallas kernels, local_ffn(): pl.pallas_call(ffn_kernel, grid=(wide // step,), in_specs=[whole, whole,...  35.4 us
    dot_general x10, matrix products, weight_grad(): lax.dot_general(left_side, gradient, (((0,), (0,)), ((), ())), preferred_...  31.9 us
    all_gather x1, blocking collectives, on_device(): part_usable = lax.all_gather(usable, 'seq', axis=1, tiled=True)  23.1 us
    dot_general x6, matrix products, project_back(): lax.dot_general(gradient, weight, (((1,), (1,)), ((), ())), preferred_ele...  18.7 us
    unnamed x133, local copies, waits for them, and re-layouts  18 us
  transfers between devices with their start and end apart: 3, of which 3 were waited for; matrix products, arithmetic and copies ran while one was open for 12% of the time, Pallas kernels for 0%

profile of v2, /device:TPU:0, one launch (start us, length us, event | category | flops | bytes accessed | tf_op | source)
XLA Modules:
  0.0 659.2 jit_solution(6814122645531565063)
XLA Ops:
  10.8 2.7 convolution_convert_fusion.6
  15.2 23.1 %all-gather = bf16[16,64,2]{1,2,0:T(2,128)(2,1)S(1)} all-gather(bf16[1,64,2]{1,2,0:T(2,128)(2,1)S(1)} %convert_bitcast_fusion.1), channel_id=1, replica_groups=mesh['utt'=2,'seq'=16] {'seq'}, dimensions={0}, use_global_device_ids=true | all-gather | bytes 4352 | tf_op jit(solution)/shard_map/all_gather | solution.py:812
  38.5 2.0 convolution_convert_fusion.7
  42.1 1.5 copy.89
  43.7 7.2 %gather_fusion = bf16[384,1024]{1,0:T(8,128)(2,1)} fusion(bf16[3072,1024]{1,0:T(8,128)(2,1)} %param.31, s32[1024]{0:T(1024)S(1)} %pad_clamp_fusion), kind=kCustom, calls=%fused_computation | custom fusion | bytes 1574400 | tf_op jit(solution)/shard_map/gather | solution.py:835
  53.5 13.7 %all-gather.6.cloned.1.call-done = bf16[2,1024,1024]{2,1,0:T(8,128)(2,1)} async-done(((bf16[2,64,1024]{2,1,0:T(8,128)(2,1)}), bf16[2,1024,1024]{2,1,0:T(8,128)(2,1)}) %all-gather.6.cloned.1.call-update) | async-done | bytes 4194320 | tf_op jit(solution)/shard_map/all_gather | solution.py:810
  67.2 6.3 copy.86
  73.5 3.9 select_reduce_fusion
  77.4 2.5 fusion.1
  81.3 37.8 %all-gather.4.cloned.1.call-done = bf16[2,1024,1024]{2,1,0:T(8,128)(2,1)} async-done(((bf16[2,64,1024]{2,1,0:T(8,128)(2,1)}), bf16[2,1024,1024]{2,1,0:T(8,128)(2,1)}) %all-gather.4.cloned.1.call-update) | async-done | bytes 4194320 | tf_op jit(solution)/shard_map/all_gather | solution.py:811
  119.1 6.2 copy.84
  125.3 8.4 %fusion.64 = (bf16[2,64,16,64]{1,3,2,0:T(8,128)(2,1)S(1)}, f32[2,64,16,64]{1,3,2,0:T(8,128)}) fusion(f32[2,64,16]{1,2,0:T(8,128)S(1)} %bitcast.205, bf16[2,1024,16,64]{1,3,2,0:T(8,128)(2,1)} %bitcast.177, f32[2,16,64,1024]{3,2,1,0:T(8,128)} %copy-done.4, f32[2,16,64]{2,1,0:T(8,128)S(1)} %broadcast_maximum_fusion, pred[2,64,1024]{2,1,0:T(8,128)(4,1)S(1)} %or_and_fusion), kind=kOutput, calls=%fused_computation.130 | convolution fusion | flops 279183360 | bytes 13516800 | tf_op jit(solution)/shard_map/uhqk,ukhd->uqhd/dot_general | solution.py:822
  134.5 2.3 multiply_reduce_fusion.3
  136.8 4.8 convolution_add_fusion
  141.7 1.6 fusion.33
  144.5 15.3 %shard_map.442 = (bf16[4,128,1024]{2,1,0:T(8,128)(2,1)}, bf16[4,128,1024]{2,1,0:T(8,128)(2,1)}, bf16[4,128,1024]{2,1,0:T(8,128)(2,1)}, bf16[4,128,1024]{2,1,0:T(...) custom-call(bf16[4,128,1024]{2,1,0:T(8,128)(2,1)} %pad_maximum_fusio, ...), custom_call_target="tpu_custom_call" | custom-call | tf_op jit(solution)/shard_map/pallas_call | solution.py:453
  159.8 35.4 %shard_map.443 = (bf16[512,1024]{1,0:T(8,128)(2,1)}, f32[512,1024]{1,0:T(8,128)}, bf16[1024,4096]{1,0:T(8,128)(2,1)}, bf16[4096,1024]{1,0:T(8,128)(2,1)}, f32[1,4096]{1,0:T(1,128)}) custom-call(bf16[512,1024]{1,0:T(8,128)(2,1)} %bitcast.196, bf16[512,1024]{1,0:T(8,128)(2,1)} %bitcast_select_fusion.1.dout_ref, f32[512,1024]{1,0:T(8,128)} %bitcast.183, ...), custom_call_target="tpu_custom_call" | custom-call | tf_op jit(solution)/shard_map/pallas_call | solution.py:512
  195.2 17.8 %shard_map.444 = (bf16[4,128,1024]{2,1,0:T(8,128)(2,1)}, bf16[4,128,1024]{2,1,0:T(8,128)(2,1)}, bf16[4,128,1024]{2,1,0:T(8,128)(2,1)}, bf16[4,128,1024]{2,1,0:T(...) custom-call(bf16[4,128,1024]{2,1,0:T(8,128)(2,1)} %pad_maximum_fusion., ...), custom_call_target="tpu_custom_call" | custom-call | tf_op jit(solution)/shard_map/pallas_call | solution.py:608
  214.4 8.4 %fusion.59 = (bf16[4096]{0:T(1024)(128)(2,1)}, bf16[128,4096]{1,0:T(8,128)(2,1)S(1)}) fusion(f32[128,4096]{1,0:T(8,128)} %copy-done.7, bf16[128,1024]{1,0:T(8,128)(2,1)S(1)} %bitcast_convert_fusion.6, bf16[4096,1024]{1,0:T(8,128)(2,1)} %param.40), kind=kOutput, calls=%fused_computation.126 | convolution fusion | flops 1084747776 | bytes 11804672 | tf_op jit(solution)/shard_map/dot_general | solution.py:653
  222.8 3.5 multiply_reduce_fusion.1
  229.3 1.5 copy.93
  232.2 7.5 %fusion.16 = bf16[2,16,64,1024]{3,2,1,0:T(8,128)(2,1)} fusion(bf16[2,64,16,64]{1,3,2,0:T(8,128)(2,1)S(1)} %copy.93, f32[2,16,64,1024]{3,2,1,0:T(8,128)} %copy-done.4, f32[2,16,64]{2,1,0:T(8,128)} %log_add_fusion, pred[2,64,1024]{2,1,0:T(8,128)(4,1)S(1)} %or_and_fusion), kind=kOutput, calls=%fused_computation.33 | convolution fusion | flops 278921216 | bytes 12984320 | tf_op jit(solution)/shard_map/uhqk,uqhd->ukhd/dot_general | solution.py:919
  239.8 5.5 multiply_convert_fusion.1
  245.3 3.3 multiply_convert_fusion
  248.6 6.3 copy.97
  254.9 6.2 copy.98
  261.1 8.2 %maximum_bitcast_fusion = bf16[1024,2,2048]{2,0,1:T(8,128)(2,1)} fusion(bf16[2,1024,1024]{2,1,0:T(8,128)(2,1)} %copy.98, bf16[2,1024,1024]{2,1,0:T(8,128)(2,1)} %copy.97), kind=kLoop, calls=%fused_computation.1 | loop fusion | flops 16777216 | bytes 16777216 | tf_op jit(solution)/shard_map/convert_element_type | solution.py:934
  270.9 3.8 select_reduce_fusion.1
  275.2 6.3 fusion.30
  281.6 2.3 copy.94
  283.9 2.2 convert_element_type.206
  286.1 3.4 convolution_convert_fusion.4
  289.4 3.4 fusion.65
  292.8 2.1 convolution_convert_fusion.3
  294.9 2.6 bitcast_convert_fusion.3
  297.5 2.6 bitcast_convert_fusion.2
  300.2 2.7 bitcast_convert_fusion.1
  302.9 2.7 bitcast_convert_fusion
  305.5 4.5 convolution_convert_fusion.2
  310.0 6.0 convolution_convert_fusion.1
  316.0 5.7 convolution_convert_fusion
  321.7 51.1 %reduce-scatter.2.cloned.1.call-done = bf16[64,2,2048]{2,0,1:T(8,128)(2,1)} async-done(((bf16[1024,2,2048]{2,0,1:T(8,128)(2,1)}), bf16[64,2,2048]{2,0,1:T(8,128)(2,1)}) %reduce-scatter.2.cloned.1.call-update) | async-done | bytes 524304 | tf_op jit(solution)/shard_map/reduce_scatter | solution.py:933
  374.0 2.1 bitcast_convert_fusion.4
  376.1 2.1 bitcast_convert_fusion.5
  379.1 1.7 fusion.44
  382.5 1.6 copy-done.2
  384.1 1.6 copy-done.3
  385.7 253.8 %shard_map.445 = (f32[192,1024]{1,0:T(8,128)S(1)}, f32[64,1024]{1,0:T(8,128)S(1)}, f32[64,1024]{1,0:T(8,128)S(1)}, f32[64,1024]{1,0:T(8,128)S(1)}, f32[64,1024]{...) custom-call(bf16[8,2,192,1024]{3,2,1,0:T(8,128)(2,1)} %bitcast.172, ...), custom_call_target="tpu_custom_call" | custom-call | tf_op jit(solution)/shard_map/pallas_call | solution.py:298
  (196 shorter events, 37.0 us)
Async XLA Ops:
  7.2 6.5 copy-start
  7.2 7.7 %copy-start.52 = (s32[2]{0:T(128)S(1)}, s32[2]{0:T(128)}, u32[]{:S(2)}) copy-start(s32[2]{0:T(128)} %param.29) | copy-start | bytes 28
  7.2 7.9 %copy-start.33 = (s32[2,64,3]{1,0,2:T(2,128)S(1)}, s32[2,64,3]{1,0,2:T(2,128)}, u32[]{:S(2)}) copy-start(s32[2,64,3]{1,0,2:T(2,128)} %param.28) | copy-start | bytes 4612
  7.2 8.0 %copy-start.51 = (s32[2,64]{1,0:T(2,128)S(1)}, s32[2,64]{1,0:T(2,128)}, u32[]{:S(2)}) copy-start(s32[2,64]{1,0:T(2,128)} %param.30) | copy-start | bytes 1540
  7.2 60.0 %all-gather.6.cloned.1.call-start = ((), (), s32[]{:S(2)}) async-start(), calls=%async_computation.2 | async-start | bytes 4456448 | tf_op jit(solution)/shard_map/all_gather | solution.py:810
  9.8 28.6 %copy-start.36 = (f32[128]{0:T(128)}, f32[128]{0:T(128)S(1)}, u32[]{:S(2)}) copy-start(f32[128]{0:T(128)S(1)} %rsqrt.25) | copy-start | bytes 1540
  13.6 105.5 %all-gather.4.cloned.1.call-start = ((), (), s32[]{:S(2)}) async-start(), calls=%async_computation.1 | async-start | bytes 4456448 | tf_op jit(solution)/shard_map/all_gather | solution.py:811
  14.9 357.9 %reduce-scatter.2.cloned.1.call-start = ((), (), s32[]{:S(2)}) async-start(), calls=%async_computation.3 | async-start | bytes 8912896 | tf_op jit(solution)/shard_map/reduce_scatter | solution.py:933
  15.0 23.5 %copy-start.41 = (pred[2,64]{1,0:T(4,128)(4,1)}, pred[2,64]{1,0:T(4,128)(4,1)S(1)}, u32[]{:S(2)}) copy-start(pred[2,64]{1,0:T(4,128)(4,1)S(1)} %broadcast_compare_fusion.1) | copy-start | bytes 388
  53.5 19.9 %copy-start.14 = (bf16[2,64,16,64]{1,3,2,0:T(8,128)(2,1)S(1)}, bf16[2,64,16,64]{1,3,2,0:T(8,128)(2,1)}, u32[]{:S(2)}) copy-start(bf16[2,64,16,64]{1,3,2,0:T(8,128)(2,1)} %copy.95) | copy-start | bytes 786436
  77.4 3.3 copy-start.4
  125.3 9.2 %copy-start.9 = (bf16[2,64,1024]{2,1,0:T(8,128)(2,1)S(1)}, bf16[2,64,1024]{2,1,0:T(8,128)(2,1)}, u32[]{:S(2)}) copy-start(bf16[2,64,1024]{2,1,0:T(8,128)(2,1)} %param.27) | copy-start | bytes 786436
  133.7 3.1 copy-start.27
  134.5 7.2 %copy-start.20 = (bf16[128,1024]{1,0:T(8,128)(2,1)}, bf16[128,1024]{1,0:T(8,128)(2,1)S(1)}, u32[]{:S(2)}) copy-start(bf16[128,1024]{1,0:T(8,128)(2,1)S(1)} %convert_element_type.193) | copy-start | bytes 786436
  134.5 7.2 %slice-start.2 = ((s8[8388608]{0:T(1024)(128)(4,1)}), s8[4194304]{0:T(1024)(128)(4,1)S(1)}, s32[]{:S(2)}) async-start(s8[8388608]{0:T(1024)(128)(4,1)} %bitcast.216), calls=%async_computation.6 | async-start | bytes 8388608
  136.8 4.9 slice-start.3
  136.8 4.9 copy-start.50
  143.4 16.4 %copy-start.29 = (bf16[128,1024]{1,0:T(8,128)(2,1)}, bf16[128,1024]{1,0:T(8,128)(2,1)S(1)}, u32[]{:S(2)}) copy-start(bf16[128,1024]{1,0:T(8,128)(2,1)S(1)} %fusion.33) | copy-start | bytes 786436
  195.2 17.8 %copy-start.28 = (bf16[2,64,1024]{2,1,0:T(8,128)(2,1)S(1)}, bf16[2,64,1024]{2,1,0:T(8,128)(2,1)}, u32[]{:S(2)}) copy-start(bf16[2,64,1024]{2,1,0:T(8,128)(2,1)} %param.52) | copy-start | bytes 786436
  195.2 17.8 %copy-start.42 = (pred[2,64]{1,0:T(4,128)(4,1)S(1)}, pred[2,64]{1,0:T(4,128)(4,1)}, u32[]{:S(2)}) copy-start(pred[2,64]{1,0:T(4,128)(4,1)} %copy-done.41) | copy-start | bytes 388
  213.0 9.8 %slice-start = ((s8[8388608]{0:T(1024)(128)(4,1)}), s8[4194304]{0:T(1024)(128)(4,1)S(1)}, s32[]{:S(2)}) async-start(s8[8388608]{0:T(1024)(128)(4,1)} %bitcast.169), calls=%async_computation.4 | async-start | bytes 8388608
  214.4 8.4 %copy-start.24 = (bf16[128,1024]{1,0:T(8,128)(2,1)}, bf16[128,1024]{1,0:T(8,128)(2,1)S(1)}, u32[]{:S(2)}) copy-start(bf16[128,1024]{1,0:T(8,128)(2,1)S(1)} %bitcast_convert_fusion.6) | copy-start | bytes 786436
  214.4 8.4 %slice-start.1 = ((s8[8388608]{0:T(1024)(128)(4,1)}), s8[4194304]{0:T(1024)(128)(4,1)S(1)}, s32[]{:S(2)}) async-start(s8[8388608]{0:T(1024)(128)(4,1)} %bitcast.169), calls=%async_computation.5 | async-start | bytes 8388608
  222.8 3.5 copy-start.17
  222.8 4.5 copy-start.10
  232.2 7.5 %copy-start.5 = (bf16[2,1024,1024]{1,2,0:T(8,128)(2,1)S(1)}, bf16[2,1024,1024]{1,2,0:T(8,128)(2,1)}, u32[]{:S(2)}) copy-start(bf16[2,1024,1024]{1,2,0:T(8,128)(2,1)} %copy.84) | copy-start | bytes 12582916
  232.2 7.5 %copy-start.30 = (f32[2,16,64]{2,1,0:T(8,128)S(1)}, f32[2,16,64]{2,1,0:T(8,128)}, u32[]{:S(2)}) copy-start(f32[2,16,64]{2,1,0:T(8,128)} %log_add_fusion) | copy-start | bytes 24580
  239.8 5.5 copy-start.15
  245.3 3.3 copy-start.6
  269.3 5.5 copy-start.39
  269.3 5.5 copy-start.40
  269.3 5.7 copy-start.32
  269.4 5.7 copy-start.34
  269.4 5.8 copy-start.35
  281.5 11.3 %copy-start.13 = (f32[128,1024]{1,0:T(8,128)S(1)}, f32[128,1024]{1,0:T(8,128)}, u32[]{:S(2)}) copy-start(f32[128,1024]{1,0:T(8,128)} %copy-done.12) | copy-start | bytes 1572868
  286.0 6.8 %copy-start.21 = (bf16[128,1024]{1,0:T(8,128)(2,1)S(1)}, bf16[128,1024]{1,0:T(8,128)(2,1)}, u32[]{:S(2)}) copy-start(bf16[128,1024]{1,0:T(8,128)(2,1)} %copy-done.20) | copy-start | bytes 786436
  286.0 8.8 %copy-start.45 = (bf16[4,128,1024]{2,1,0:T(8,128)(2,1)S(1)}, bf16[4,128,1024]{2,1,0:T(8,128)(2,1)}, u32[]{:S(2)}) copy-start(bf16[4,128,1024]{2,1,0:T(8,128)(2,1)} %get-tuple-element.69) | copy-start | bytes 3145732
  286.1 8.8 %copy-start.49 = (bf16[4,128,1024]{2,1,0:T(8,128)(2,1)S(1)}, bf16[4,128,1024]{2,1,0:T(8,128)(2,1)}, u32[]{:S(2)}) copy-start(bf16[4,128,1024]{2,1,0:T(8,128)(2,1)} %get-tuple-element.70) | copy-start | bytes 3145732
  300.2 2.7 copy-start.46
  305.5 4.5 copy-start.18
  310.0 6.0 copy-start.8
  310.0 6.0 copy-start.25
  316.0 58.0 %copy-start.16 = (bf16[2,64,1024]{2,1,0:T(8,128)(2,1)S(1)}, bf16[2,64,1024]{2,1,0:T(8,128)(2,1)}, u32[]{:S(2)}) copy-start(bf16[2,64,1024]{2,1,0:T(8,128)(2,1)} %fusion.47) | copy-start | bytes 786436
  372.7 5.5 copy-start.11
  372.7 5.5 copy-start.23
  374.0 5.1 copy-start.37
  385.7 255.1 %copy-start.54 = (f32[128]{0:T(128)S(1)}, f32[128]{0:T(128)}, u32[]{:S(2)}) copy-start(f32[128]{0:T(128)} %copy-done.53) | copy-start | bytes 1540
  385.7 255.1 %copy-start.22 = (f32[128,1024]{1,0:T(8,128)S(1)}, f32[128,1024]{1,0:T(8,128)}, u32[]{:S(2)}) copy-start(f32[128,1024]{1,0:T(8,128)} %get-tuple-element.125) | copy-start | bytes 1572868
  (14 other events, 23.1 us)
Sparse Core Ops, SparseCore 0:
  13.7 53.4 all-gather.5
  70.0 49.0 all-gather.3
  269.5 103.1 reduce-scatter.1

commit v3 on v2

--- a/solution.py
+++ b/solution.py
@@ -17,6 +17,7 @@
 NEGATIVE = -1e30
 F32 = jnp.float32
 LOW = jnp.bfloat16
+LANES = 128
 MESH_ID = pl.DeviceIdType.MESH
 SLOTS = 4
 SROWS = 64
@@ -629,6 +630,360 @@
     )(x, mid, dhn, dout, q, k, v, probs, *fixed)
 
 
+def greet(count):
+    utt, me = lax.axis_index("utt"), lax.axis_index("seq")
+    barrier = pltpu.get_barrier_semaphore()
+
+    @pl.loop(1, count)
+    def _(step):
+        pl.semaphore_signal(
+            barrier, inc=1, device_id=(utt, lax.rem(me + step, count)), device_id_type=MESH_ID
+        )
+
+    return barrier
+
+
+def remote(source, target, send_sem, recv_sem, place):
+    return pltpu.make_async_remote_copy(
+        src_ref=source,
+        dst_ref=target,
+        send_sem=send_sem,
+        recv_sem=recv_sem,
+        device_id=(lax.axis_index("utt"), place),
+        device_id_type=MESH_ID,
+    )
+
+
+def two_heads(rows):
+    lane = lax.broadcasted_iota(jnp.int32, rows.shape, 1)
+    zero = jnp.zeros_like(rows)
+    return jnp.concatenate([jnp.where(lane < HD, rows, zero), jnp.where(lane < HD, zero, rows)], axis=0)
+
+
+def join_heads(tall):
+    rows = tall.T
+    lane = lax.broadcasted_iota(jnp.int32, (HD, LANES), 1)
+    return jnp.where(lane < HD, rows[:HD], rows[HD:])
+
+
+def masked_scores(scores, bias, first, block):
+    key = first + lax.broadcasted_iota(jnp.int32, scores.shape, 0)
+    query = block * HD + lax.rem(lax.broadcasted_iota(jnp.int32, scores.shape, 1), HD)
+    return jnp.where(key < query, scores + bias, jnp.where(key == query, scores, NEGATIVE))
+
+
+def fill_bias(bias_ref, mask):
+    for block in range(mask.shape[0]):
+        row = lax.broadcasted_iota(jnp.int32, (HD, LANES), 0)
+        lane = lax.broadcasted_iota(jnp.int32, (HD, LANES), 1)
+        flags = jnp.broadcast_to(mask[block, 0:1, :], (HD, LANES))
+        diagonal = jnp.where(row == lane, flags.astype(F32), 0.0).astype(LOW)
+        usable = mul(diagonal, jnp.ones((LANES, LANES), LOW))
+        bias_ref[block * HD : (block + 1) * HD, :] = (usable - 1.0) * 1e30
+
+
+def attend_kernel(
+    count, x_ref, mask_ref, n1_ref, wq_ref, wk_ref, wv_ref,
+    normed_ref, mixed_ref, saved_ref, log_ref,
+    packed, held, mixed_all, pieces, bias, v_t, send_sem, recv_sem, send_two, recv_two, save_sem,
+):
+    share = count // 16
+    me = lax.axis_index("seq")
+    unit, part = me // share, me % share
+    own_utt, own_pair = unit // 8, unit % 8
+    own_cols = pl.ds(pl.multiple_of(own_pair * LANES, LANES), LANES)
+    utts, frames, width = x_ref.shape
+    barrier = greet(count)
+
+    x = x_ref[...].astype(F32).reshape(utts * frames, width)
+    normed = (x * scale_of(x) * n1_ref[...]).astype(LOW)
+    normed_ref[...] = normed
+    packed[:, 0:64] = (mul(normed, wq_ref[...]).astype(LOW)).reshape(utts, frames, width)
+    packed[:, 64:128] = mul(normed, wk_ref[...]).astype(LOW).reshape(utts, frames, width)
+    packed[:, 128:192] = mul(normed, wv_ref[...]).astype(LOW).reshape(utts, frames, width)
+    for pair in range(8):
+        packed[:, 192:208, pair * LANES : (pair + 1) * LANES] = jnp.broadcast_to(
+            mask_ref[...], (utts, 16, LANES)
+        )
+    pl.semaphore_wait(barrier, count - 1)
+
+    def outgoing(step):
+        place = lax.rem(me + step, count)
+        target = place // share
+        cols = pl.ds(pl.multiple_of((target % 8) * LANES, LANES), LANES)
+        return remote(
+            packed.at[target // 8, :, cols], held.at[me], send_sem.at[step], recv_sem.at[step], place
+        )
+
+    @pl.loop(1, count)
+    def _(step):
+        outgoing(step).start()
+
+    held[me] = packed[own_utt, :, own_cols]
+
+    @pl.loop(1, count)
+    def _(step):
+        place = lax.rem(me + count - step, count)
+        remote(held.at[place], held.at[place], send_sem.at[step], recv_sem.at[step], place).wait_recv()
+
+    save = pltpu.make_async_copy(held, saved_ref, save_sem)
+    save.start()
+    v_t[...] = held[:, 128:192].reshape(count * HD, LANES).T
+    fill_bias(bias, held[:, 192:208])
+
+    def returning(block):
+        return remote(
+            pieces.at[block],
+            mixed_all.at[own_utt, :, own_cols],
+            send_two.at[block],
+            recv_two.at[unit],
+            block,
+        )
+
+    for group in range(count // 4):
+        below = group * 256
+        here = below + 256
+
+        @pl.loop(0, 4 // share)
+        def _(index):
+            block = 4 * group + share * index + part
+            query = two_heads(held[block, 0:64] * LOW(HD ** (-0.5)))
+            keys = held[4 * group : 4 * group + 4, 64:128].reshape(256, LANES)
+            near = masked_scores(mul_t(keys, query), bias[below:here], below, block)
+            peak = jnp.max(near, axis=0, keepdims=True)
+            if group:
+                keys = held[0 : 4 * group, 64:128].reshape(below, LANES)
+                far = mul_t(keys, query) + bias[0:below]
+                peak = jnp.maximum(peak, jnp.max(far, axis=0, keepdims=True))
+                far = jnp.exp(far - peak)
+            near = jnp.exp(near - peak)
+            total = jnp.sum(near, axis=0, keepdims=True)
+            if group:
+                total = total + jnp.sum(far, axis=0, keepdims=True)
+            inverse = 1.0 / total
+            mixed = mul(v_t[:, below:here], (near * inverse).astype(LOW))
+            if group:
+                mixed = mixed + mul(v_t[:, 0:below], (far * inverse).astype(LOW))
+            log_ref[block] = jnp.broadcast_to(peak + jnp.log(total), (8, LANES))
+            pieces[block] = join_heads(mixed).astype(LOW)
+
+            @pl.when(block != me)
+            def _():
+                returning(block).start()
+
+            @pl.when(block == me)
+            def _():
+                mixed_all[own_utt, :, own_cols] = pieces[block]
+
+    @pl.loop(0, 16)
+    def _(other):
+        place = other * share + me % share
+        cols = pl.ds(pl.multiple_of((other % 8) * LANES, LANES), LANES)
+
+        @pl.when(place != me)
+        def _():
+            here = mixed_all.at[other // 8, :, cols]
+            remote(here, here, send_two.at[0], recv_two.at[other], place).wait_recv()
+
+    @pl.loop(1, count)
+    def _(step):
+        outgoing(step).wait_send()
+
+    @pl.loop(0, count // share)
+    def _(index):
+        block = share * index + part
+
+        @pl.when(block != me)
+        def _():
+            returning(block).wait_send()
+
+    mixed_ref[...] = mixed_all[...]
+    save.wait()
+
+
+def global_attend(x, mask, params):
+    count = lax.axis_size("seq")
+    utts, frames, width = x.shape
+    vmem = pl.BlockSpec(memory_space=pltpu.VMEM)
+    hbm = pl.BlockSpec(memory_space=pl.ANY)
+    return pl.pallas_call(
+        functools.partial(attend_kernel, count),
+        in_specs=[vmem] * 6,
+        out_specs=[vmem, vmem, hbm, vmem],
+        out_shape=[
+            jax.ShapeDtypeStruct((utts * frames, width), LOW),
+            jax.ShapeDtypeStruct((utts, frames, width), LOW),
+            jax.ShapeDtypeStruct((count, 208, LANES), LOW),
+            jax.ShapeDtypeStruct((count, 8, LANES), F32),
+        ],
+        scratch_shapes=[
+            pltpu.VMEM((utts, 208, width), LOW),
+            pltpu.VMEM((count, 208, LANES), LOW),
+            pltpu.VMEM((utts, frames, width), LOW),
+            pltpu.VMEM((count, HD, LANES), LOW),
+            pltpu.VMEM((count * HD, LANES), F32),
+            pltpu.VMEM((LANES, count * HD), LOW),
+            pltpu.SemaphoreType.DMA((count,)),
+            pltpu.SemaphoreType.DMA((count,)),
+            pltpu.SemaphoreType.DMA((count,)),
+            pltpu.SemaphoreType.DMA((16,)),
+            pltpu.SemaphoreType.DMA,
+        ],
+        compiler_params=pltpu.CompilerParams(
+            collective_id=2, has_side_effects=True, vmem_limit_bytes=48 << 20
+        ),
+    )(x, mask, params[0].reshape(1, -1), params[1], params[2], params[3])
+
+
+def attend_back_kernel(
+    count, grad_ref, held, log_ref,
+    dqkv_ref,
+    grads, landed, pieces, dk_acc, dv_acc, bias, k_t, send_sem, recv_sem, send_two, recv_two,
+):
+    share = count // 16
+    me = lax.axis_index("seq")
+    unit, part = me // share, me % share
+    own_utt, own_pair = unit // 8, unit % 8
+    own_cols = pl.ds(pl.multiple_of(own_pair * LANES, LANES), LANES)
+    barrier = greet(count)
+    k_t[...] = held[:, 64:128].reshape(count * HD, LANES).T
+    fill_bias(bias, held[:, 192:208])
+    dk_acc[...] = jnp.zeros_like(dk_acc)
+    dv_acc[...] = jnp.zeros_like(dv_acc)
+    pl.semaphore_wait(barrier, count - 1)
+
+    def outgoing(other):
+        cols = pl.ds(pl.multiple_of((other % 8) * LANES, LANES), LANES)
+        place = other * share + part
+        return place, remote(
+            grad_ref.at[other // 8, :, cols], grads.at[me // share], send_sem.at[other],
+            recv_sem.at[me // share], place,
+        )
+
+    @pl.loop(1, 16)
+    def _(step):
+        _, copy = outgoing(lax.rem(unit + step, 16))
+        copy.start()
+
+    grads[unit] = grad_ref[own_utt, :, own_cols]
+
+    @pl.loop(1, 16)
+    def _(step):
+        other = lax.rem(unit + step, 16)
+        here = grads.at[other]
+        remote(here, here, send_sem.at[other], recv_sem.at[other], other * share + part).wait_recv()
+
+    def returning(block):
+        return remote(
+            pieces.at[block],
+            landed.at[part, :, own_utt, :, own_cols],
+            send_two.at[block],
+            recv_two.at[me],
+            block,
+        )
+
+    for group in reversed(range(count // 4)):
+        below = group * 256
+        here = below + 256
+
+        @pl.loop(0, 4 // share)
+        def _(index):
+            block = 4 * group + share * index + part
+            query = two_heads(held[block, 0:64] * LOW(HD ** (-0.5)))
+            grad = two_heads(grads[block // share])
+            log_total = log_ref[block][0:1]
+            near_v = held[4 * group : 4 * group + 4, 128:192].reshape(256, LANES)
+            near_k = held[4 * group : 4 * group + 4, 64:128].reshape(256, LANES)
+            near = masked_scores(mul_t(near_k, query), bias[below:here], below, block)
+            near = jnp.exp(near - log_total)
+            near_dp = mul_t(near_v, grad)
+            delta = jnp.sum(near * near_dp, axis=0, keepdims=True)
+            if group:
+                far_v = held[0 : 4 * group, 128:192].reshape(below, LANES)
+                far_k = held[0 : 4 * group, 64:128].reshape(below, LANES)
+                far = jnp.exp(mul_t(far_k, query) + bias[0:below] - log_total)
+                far_dp = mul_t(far_v, grad)
+                delta = delta + jnp.sum(far * far_dp, axis=0, keepdims=True)
+                far_ds = (far * (far_dp - delta)).astype(LOW)
+                dk_acc[0:below] += mul(far_ds, query)
+                dv_acc[0:below] += mul(far.astype(LOW), grad)
+            near_ds = (near * (near_dp - delta)).astype(LOW)
+            dk_acc[below:here] += mul(near_ds, query)
+            dv_acc[below:here] += mul(near.astype(LOW), grad)
+            dq = mul(k_t[:, below:here], near_ds)
+            if group:
+                dq = dq + mul(k_t[:, 0:below], far_ds)
+            pieces[block, 0] = (join_heads(dq) * HD ** (-0.5)).astype(LOW)
+
+        for block in range(4 * group, 4 * group + 4):
+            rows = slice(block * HD, (block + 1) * HD)
+            pieces[block, 1] = dk_acc[rows].astype(LOW)
+            pieces[block, 2] = dv_acc[rows].astype(LOW)
+            if share > 1:
+
+                @pl.when(block % share != part)
+                def _():
+                    pieces[block, 0] = jnp.zeros((HD, LANES), LOW)
+
+            @pl.when(block != me)
+            def _():
+                returning(block).start()
+
+            @pl.when(block == me)
+            def _():
+                landed[part, :, own_utt, :, own_cols] = pieces[block]
+
+    @pl.loop(1, count)
+    def _(step):
+        place = lax.rem(me + step, count)
+        other, other_part = place // share, place % share
+        cols = pl.ds(pl.multiple_of((other % 8) * LANES, LANES), LANES)
+        here = landed.at[other_part, :, other // 8, :, cols]
+        remote(here, here, send_two.at[place], recv_two.at[place], place).wait_recv()
+
+    @pl.loop(1, 16)
+    def _(step):
+        _, copy = outgoing(lax.rem(unit + step, 16))
+        copy.wait_send()
+
+    @pl.loop(1, count)
+    def _(step):
+        returning(lax.rem(me + step, count)).wait_send()
+
+    total = landed[0]
+    for other_part in range(1, share):
+        total = (total.astype(F32) + landed[other_part].astype(F32)).astype(LOW)
+    dqkv_ref[...] = total
+
+
+def global_attend_back(grad_mixed, saved, log_total):
+    count = lax.axis_size("seq")
+    utts, frames, width = grad_mixed.shape
+    vmem = pl.BlockSpec(memory_space=pltpu.VMEM)
+    return pl.pallas_call(
+        functools.partial(attend_back_kernel, count),
+        in_specs=[vmem] * 3,
+        out_specs=vmem,
+        out_shape=jax.ShapeDtypeStruct((3, utts, frames, width), LOW),
+        scratch_shapes=[
+            pltpu.VMEM((16, HD, LANES), LOW),
+            pltpu.VMEM((count // 16, 3, utts, frames, width), LOW),
+            pltpu.VMEM((count, 3, HD, LANES), LOW),
+            pltpu.VMEM((count * HD, LANES), F32),
+            pltpu.VMEM((count * HD, LANES), F32),
+            pltpu.VMEM((count * HD, LANES), F32),
+            pltpu.VMEM((LANES, count * HD), LOW),
+            pltpu.SemaphoreType.DMA((16,)),
+            pltpu.SemaphoreType.DMA((16,)),
+            pltpu.SemaphoreType.DMA((count,)),
+            pltpu.SemaphoreType.DMA((count,)),
+        ],
+        compiler_params=pltpu.CompilerParams(
+            collective_id=3, has_side_effects=True, vmem_limit_bytes=48 << 20
+        ),
+    )(grad_mixed, saved, log_total)
+
+
 def normalize(values, gain_vec):
     return (
         values * lax.rsqrt(jnp.mean(values * values, axis=-1, keepdims=True) + EPSILON) * gain_vec
@@ -639,12 +994,6 @@
     return jax.nn.gelu(values, approximate=True)
 
 
-def softmax_rows(scores):
-    row_peak = jnp.max(scores, axis=-1, keepdims=True)
-    raised = jnp.exp(scores - row_peak)
-    return raised / jnp.sum(raised, axis=-1, keepdims=True)
-
-
 def project(left_side, weight):
     return jnp.dot(left_side, weight, preferred_element_type=jnp.float32)
 
@@ -659,18 +1008,6 @@
     return lax.dot_general(
         left_side, gradient, (((0,), (0,)), ((), ())), preferred_element_type=jnp.float32
     )
-
-
-def head_split(matrix):
-    return matrix.reshape(matrix.shape[0], matrix.shape[1], H, HD)
-
-
-def block_inputs(inputs, params):
-    normed = normalize(inputs, params[0]).astype(jnp.bfloat16)
-    queries = project(normed, params[1]).astype(jnp.bfloat16)
-    key_rows = project(normed, params[2]).astype(jnp.bfloat16)
-    value_rows = project(normed, params[3]).astype(jnp.bfloat16)
-    return (normed, queries, key_rows, value_rows)
 
 
 def block_outputs(inputs, mixed_rows, params):
@@ -682,8 +1019,7 @@
     return (result, (middle, middle_norm, pre_active, active))
 
 
-def block_back(inputs, front_parts, mixed_rows, kept_parts, params, grad_out, attention_back):
-    normed, queries, key_rows, value_rows = front_parts
+def block_back(inputs, normed, mixed_rows, kept_parts, params, grad_out, attention_back):
     middle, middle_norm, pre_active, active = kept_parts
     grad_branch = grad_out.astype(jnp.bfloat16)
     grad_b_down = jnp.sum(grad_branch.astype(jnp.float32), axis=0)
@@ -719,26 +1055,6 @@
         grad_b_down,
     )
     return (grad_inputs + grad_middle, weight_grads)
-
-
-def permitted(row_ids, col_ids, usable_cols):
-    causal = col_ids[None, :] <= row_ids[:, None]
-    itself = col_ids[None, :] == row_ids[:, None]
-    return (causal[None] & ((usable_cols[:, None, :] > 0) | itself[None]))[:, None]
-
-
-def probs_from(query_heads, key_heads, allowed, log_total):
-    scores = jnp.einsum(
-        "uqhd,ukhd->uhqk", query_heads, key_heads, preferred_element_type=jnp.float32
-    ) * HD ** (-0.5)
-    return jnp.where(allowed, jnp.exp(scores - log_total[..., None]), 0.0)
-
-
-def score_grads(probs, grad_heads, value_heads, delta_rows):
-    grad_probs = jnp.einsum(
-        "uqhd,ukhd->uhqk", grad_heads, value_heads, preferred_element_type=jnp.float32
-    )
-    return (probs * (grad_probs - delta_rows[..., None])).astype(jnp.bfloat16)
 
 
 def on_device(
@@ -775,7 +1091,8 @@
     local_len = CB + 1
     positions = lax.axis_index("seq") * frame_count + jnp.arange(frame_count, dtype=jnp.int32)
     valid = positions[None, :] < lengths[:, None]
-    usable = frame_mask.astype(jnp.bfloat16)
+    usable = jnp.pad(frame_mask.astype(LOW), ((0, 0), (0, LANES - frame_count)))
+    usable = jnp.broadcast_to(usable[:, None, :], (utter_count, 16, LANES))
     glob_params = (
         glob_norm_one,
         glob_w_query,
@@ -801,33 +1118,8 @@
         local_b_down,
     )
     global_in = frames.astype(jnp.float32).reshape(row_count, model_width)
-    glob_front = block_inputs(global_in, glob_params)
-    query_block = glob_front[1].reshape(utter_count, frame_count, model_width)
-    key_block = glob_front[2].reshape(utter_count, frame_count, model_width)
-    value_block = glob_front[3].reshape(utter_count, frame_count, model_width)
-    query_heads = head_split(query_block)
-    run_max = jnp.full((utter_count, H, frame_count), NEGATIVE, jnp.float32)
-    part_keys = lax.all_gather(key_block, "seq", axis=1, tiled=True)
-    part_values = lax.all_gather(value_block, "seq", axis=1, tiled=True)
-    part_usable = lax.all_gather(usable, "seq", axis=1, tiled=True)
-    span = part_keys.shape[1]
-    allowed = permitted(positions, jnp.arange(span, dtype=jnp.int32), part_usable)
-    scores = jnp.einsum(
-        "uqhd,ukhd->uhqk", query_heads, head_split(part_keys), preferred_element_type=jnp.float32
-    ) * HD ** (-0.5)
-    scores = jnp.where(allowed, scores, NEGATIVE)
-    new_max = jnp.maximum(run_max, jnp.max(scores, axis=-1))
-    weights = jnp.where(allowed, jnp.exp(scores - new_max[..., None]), 0.0)
-    new_sum = jnp.sum(weights, axis=-1)
-    new_accum = jnp.einsum(
-        "uhqk,ukhd->uqhd",
-        weights.astype(jnp.bfloat16),
-        head_split(part_values),
-        preferred_element_type=jnp.float32,
-    )
-    log_total = new_max + jnp.log(new_sum)
-    attn_heads = new_accum / new_sum.transpose(0, 2, 1)[..., None]
-    glob_mixed = attn_heads.reshape(row_count, model_width).astype(jnp.bfloat16)
+    glob_normed, glob_mixed, saved, log_total = global_attend(frames, usable, glob_params)
+    glob_mixed = glob_mixed.reshape(row_count, model_width)
     glob_result, glob_kept = block_outputs(global_in, glob_mixed, glob_params)
     global_rows = jnp.where(valid.reshape(row_count, 1), glob_result, 0.0).astype(jnp.bfloat16)
     code_rows = codes.transpose(2, 0, 1).reshape(CB, row_count)
@@ -886,69 +1178,13 @@
     glob_cotan = glob_cotan.reshape(row_count, model_width)
 
     def global_back(grad_mixed):
-        grad_block = grad_mixed.reshape(utter_count, frame_count, model_width)
-        grad_heads = head_split(grad_block)
-        delta_rows = jnp.sum(grad_heads.astype(jnp.float32) * attn_heads, axis=-1).transpose(
-            0, 2, 1
+        grads = global_attend_back(
+            grad_mixed.reshape(utter_count, frame_count, model_width), saved, log_total
         )
-        all_keys, all_values, all_usable = (
-            lax.all_gather(key_block, "seq", axis=1, tiled=True),
-            lax.all_gather(value_block, "seq", axis=1, tiled=True),
-            lax.all_gather(usable, "seq", axis=1, tiled=True),
-        )
-        every_col = jnp.arange(all_keys.shape[1], dtype=jnp.int32)
-        probs = probs_from(
-            query_heads,
-            head_split(all_keys),
-            permitted(positions, every_col, all_usable),
-            log_total,
-        )
-        grads_s = score_grads(probs, grad_heads, head_split(all_values), delta_rows)
-        grad_query = jnp.einsum(
-            "uhqk,ukhd->uqhd", grads_s, head_split(all_keys), preferred_element_type=jnp.float32
-        ) * HD ** (-0.5)
-        span = frame_count * lax.axis_size("seq")
-        col_ids = jnp.arange(span, dtype=jnp.int32)
-        part_probs = probs_from(
-            query_heads, head_split(all_keys), permitted(positions, col_ids, all_usable), log_total
-        )
-        part_grads = score_grads(part_probs, grad_heads, head_split(all_values), delta_rows)
-        term_keys = jnp.einsum(
-            "uhqk,uqhd->ukhd", part_grads, query_heads, preferred_element_type=jnp.float32
-        ) * HD ** (-0.5)
-        term_values = jnp.einsum(
-            "uhqk,uqhd->ukhd",
-            part_probs.astype(jnp.bfloat16),
-            grad_heads,
-            preferred_element_type=jnp.float32,
-        )
-        joined = jnp.concatenate(
-            [
-                term_keys.reshape(utter_count, span, model_width),
-                term_values.reshape(utter_count, span, model_width),
-            ],
-            axis=-1,
-        )
-        summed = (
-            lax.psum_scatter(
-                joined.transpose(1, 0, 2).astype(jnp.bfloat16),
-                "seq",
-                scatter_dimension=0,
-                tiled=True,
-            )
-            .astype(jnp.float32)
-            .transpose(1, 0, 2)
-        )
-        grad_key = summed[:, :, :model_width]
-        grad_value = summed[:, :, model_width:]
-        return (
-            grad_query.reshape(row_count, model_width).astype(jnp.bfloat16),
-            grad_key.reshape(row_count, model_width).astype(jnp.bfloat16),
-            grad_value.reshape(row_count, model_width).astype(jnp.bfloat16),
-        )
+        return tuple(grads.reshape(3, row_count, model_width))
 
     grad_inputs, glob_grads = block_back(
-        global_in, glob_front, glob_mixed, glob_kept, glob_params, glob_cotan, global_back
+        global_in, glob_normed, glob_mixed, glob_kept, glob_params, glob_cotan, global_back
     )
     reduced = reduce_all((grad_tab,) + glob_grads + local_grads)
     return (

time: 664 us -> 510 us (0.77)
  waiting for transfers between devices: 103 us -> 0 us
  Pallas kernels: 322 us -> 398 us
  matrix products: 105 us -> 59.4 us
  local copies, waits for them, and re-layouts: 64.7 us -> 26.3 us
  blocking collectives: 23.1 us -> 0 us
  between operations: 14.9 us -> 1.62 us
  other arithmetic: 26.7 us -> 15.2 us
    pallas_call x0 -> x2, Pallas kernels: none -> 75.4 us  [the longest x1 42.1 us: global_attend_back(): pl.pallas_call(functools.partial(attend_back_kernel, count), in_specs=[vm...]
    all_gather x2 -> x0, waiting for transfers between devices: 51.4 us -> none  [the longest x1 37.8 us: on_device(): part_values = lax.all_gather(value_block, 'seq', axis=1, tiled=True)]
    reduce_scatter x1 -> x0, waiting for transfers between devices: 51.1 us -> none  [global_back(): lax.psum_scatter(joined.transpose(1, 0, 2).astype(jnp.bfloat16), 'seq', s...]
    dot_general x6 -> x0, matrix products: 35 us -> none  [the longest x1 8.35 us: on_device(): jnp.einsum('uhqk,ukhd->uqhd', weights.astype(jnp.bfloat16), head_split(pa...]
    all_gather x1 -> x0, blocking collectives: 23.1 us -> none  [on_device(): part_usable = lax.all_gather(usable, 'seq', axis=1, tiled=True)]
    all_gather x2 -> x0, local copies, waits for them, and re-layouts: 12.5 us -> none  [the longest x1 6.27 us: on_device(): part_keys = lax.all_gather(key_block, 'seq', axis=1, tiled=True)]
    reshape x2 -> x0, local copies, waits for them, and re-layouts: 12.5 us -> none  [the longest x1 6.25 us: global_back(): term_keys.reshape(utter_count, span, model_width)]
    convert_element_type x3 -> x1, other arithmetic: 10.1 us -> 0.68 us  [on_device(): usable = jnp.pad(frame_mask.astype(LOW), ((0, 0), (0, LANES - frame_count)))]
  transfers between devices with their start and end apart: 3 -> 0, of which waited for: 3 -> 0; matrix products, arithmetic and copies ran while one was open for 12% -> 0% of each run, Pallas kernels for 0% -> 0%
where the time goes in v3:
time: 510 us; the launch traced here: 500 us
  Pallas kernels  398 us (78%)
  matrix products  59.4 us (12%)
  local copies, waits for them, and re-layouts  26.3 us (5%)
  other arithmetic  15.2 us (3%)
    pallas_call x1, Pallas kernels, reduce_grads(): pl.pallas_call(functools.partial(reduce_kernel, tuple(plan), total), out_...  254 us
    pallas_call x1, Pallas kernels, global_attend_back(): pl.pallas_call(functools.partial(attend_back_kernel, count), in_specs=[vm...  42.1 us
    pallas_call x1, Pallas kernels, local_ffn(): pl.pallas_call(ffn_kernel, grid=(wide // step,), in_specs=[whole, whole,...  35.8 us
    pallas_call x1, Pallas kernels, global_attend(): pl.pallas_call(functools.partial(attend_kernel, count), in_specs=[vmem] *...  33.4 us
    dot_general x10, matrix products, weight_grad(): lax.dot_general(left_side, gradient, (((0,), (0,)), ((), ())), preferred_...  27.8 us
    dot_general x6, matrix products, project_back(): lax.dot_general(gradient, weight, (((1,), (1,)), ((), ())), preferred_ele...  19.4 us
    pallas_call x1, Pallas kernels, local_back(): pl.pallas_call(back_kernel, grid=(frames // step,), in_specs=[rows] * 7 +...  17.6 us
    pallas_call x1, Pallas kernels, local_front(): pl.pallas_call(front_kernel, grid=(frames // step,), in_specs=[rows] + [w...  14.8 us

profile of v3, /device:TPU:0, one launch (start us, length us, event | category | flops | bytes accessed | tf_op | source)
XLA Modules:
  0.0 500.4 jit_solution(8815653792840259131)
XLA Ops:
  0.7 0.9 broadcast_compare_fusion
  2.4 1.1 multiply_reduce_fusion.1
  3.5 0.8 eq.15
  4.3 0.8 reshape.356
  5.2 7.0 %gather_fusion = bf16[384,1024]{1,0:T(8,128)(2,1)} fusion(bf16[3072,1024]{1,0:T(8,128)(2,1)} %param.31, s32[1024]{0:T(1024)S(1)} %pad_clamp_fusion), kind=kCustom, calls=%fused_computation | custom fusion | bytes 1574400 | tf_op jit(solution)/shard_map/gather | solution.py:1127
  12.1 1.6 copy.58
  13.8 1.3 bitcast_select_fusion.1.dout_ref
  15.0 1.3 bitcast_select_fusion.dout_ref
  16.7 33.4 %shard_map.442 = (bf16[128,1024]{1,0:T(8,128)(2,1)S(1)}, bf16[2,64,1024]{2,1,0:T(8,128)(2,1)S(1)}, bf16[16,208,128]{2,1,0:T(8,128)(2,1)S(1)}, f32[16,8,128]{2,1,0:T(8,128)S(1)}) custom-call(bf16[2,64,1024]{2,1,0:T(8,128)(2,1)S(1)} %copy-done.6, bf16[2,16,128]{2,1,0:T(8,128)(2,1)S(1)} %broadcast_in_dim.82.mask_ref, f32[1,1024]{1,0:T(1,128)S(1)} %bitcast.117, ...), custom_call_target="tpu_custom_call" | custom-call | tf_op jit(solution)/shard_map/pallas_call | solution.py:809
  50.9 5.4 %convolution_add_fusion = f32[128,4096]{1,0:T(8,128)S(1)} fusion(bf16[1024,4096]{1,0:T(8,128)(2,1)} %param.38, f32[4096]{0:T(1024)S(1)} %copy-done.32, f32[128,1024]{1,0:T(8,128)S(1)} %get-tuple-element.124, f32[1024]{0:T(1024)S(1)} %copy-done.28, f32[128]{0:T(128)S(1)} %fusion.20), kind=kOutput, calls=%fused_computation.3 | convolution fusion | flops 1074659328 | bytes 11031040 | tf_op jit(solution)/shard_map/dot_general | solution.py:998
  56.4 1.6 fusion.9
  58.7 1.1 pad_maximum_fusion.x_ref
  59.7 14.8 %shard_map.443 = (bf16[4,128,1024]{2,1,0:T(8,128)(2,1)}, bf16[4,128,1024]{2,1,0:T(8,128)(2,1)}, bf16[4,128,1024]{2,1,0:T(8,128)(2,1)}, bf16[4,128,1024]{2,1,0:T(...) custom-call(bf16[4,128,1024]{2,1,0:T(8,128)(2,1)} %pad_maximum_fusio, ...), custom_call_target="tpu_custom_call" | custom-call | tf_op jit(solution)/shard_map/pallas_call | solution.py:454
  74.6 35.8 %shard_map.444 = (bf16[512,1024]{1,0:T(8,128)(2,1)}, f32[512,1024]{1,0:T(8,128)}, bf16[1024,4096]{1,0:T(8,128)(2,1)}, bf16[4096,1024]{1,0:T(8,128)(2,1)}, f32[1,4096]{1,0:T(1,128)}) custom-call(bf16[512,1024]{1,0:T(8,128)(2,1)} %bitcast.140, bf16[512,1024]{1,0:T(8,128)(2,1)} %bitcast_select_fusion.1.dout_ref, f32[512,1024]{1,0:T(8,128)} %bitcast.124, ...), custom_call_target="tpu_custom_call" | custom-call | tf_op jit(solution)/shard_map/pallas_call | solution.py:513
  110.4 17.6 %shard_map.445 = (bf16[4,128,1024]{2,1,0:T(8,128)(2,1)}, bf16[4,128,1024]{2,1,0:T(8,128)(2,1)}, bf16[4,128,1024]{2,1,0:T(8,128)(2,1)}, bf16[4,128,1024]{2,1,0:T(...) custom-call(bf16[4,128,1024]{2,1,0:T(8,128)(2,1)} %pad_maximum_fusion., ...), custom_call_target="tpu_custom_call" | custom-call | tf_op jit(solution)/shard_map/pallas_call | solution.py:609
  128.0 2.0 convert_reduce_fusion
  129.9 3.8 select_reduce_fusion
  134.2 1.1 bitcast_convert_fusion.4
  135.3 4.3 bitcast_convert_fusion
  139.6 8.0 %fusion.21 = (bf16[4096]{0:T(1024)(128)(2,1)S(1)}, bf16[128,4096]{1,0:T(8,128)(2,1)}) fusion(f32[128,4096]{1,0:T(8,128)S(1)} %copy-done.11, bf16[128,1024]{1,0:T(8,128)(2,1)S(1)} %bitcast_convert_fusion.4, bf16[4096,1024]{1,0:T(8,128)(2,1)} %param.40), kind=kOutput, calls=%fused_computation.74 | convolution fusion | flops 1084747776 | bytes 11804672 | tf_op jit(solution)/shard_map/dot_general | solution.py:1002
  147.6 6.8 %multiply_reduce_fusion = (bf16[1024]{0:T(1024)(128)(2,1)S(1)}, f32[128]{0:T(128)S(1)}, f32[128,1024]{1,0:T(8,128)S(1)}) fusion(f32[128,1024]{1,0:T(8,128)S(1)} %get-tuple-element.124, f32[128]{0:T(128)S(1)} %fusion.20, f32[1024]{0:T(1024)S(1)} %copy-done.28, bf16[128,4096]{1,0:T(8,128)(2,1)} %get-tuple-element.109, bf16[1024,4096]{1,0:T(8,128)(2,1)} %param.38), kind=kOutput, calls=%fused_computation.50 | convolution fusion | flops 1074527104 | bytes 10492928 | tf_op jit(solution)/shard_map/dot_general | solution.py:1002
  154.4 1.0 fusion.12
  155.5 1.9 convolution_convert_fusion.7
  157.5 42.1 %shard_map.446 = bf16[3,2,64,1024]{3,2,1,0:T(8,128)(2,1)S(1)} custom-call(bf16[2,64,1024]{2,1,0:T(8,128)(2,1)S(1)} %bitcast.113, bf16[16,208,128]{2,1,0:T(8,128)(2,1)S(1)} %copy-done.8, f32[16,8,128]{2,1,0:T(8,128)S(1)} %get-tuple-element.74.log_ref), custom_call_target="tpu_custom_call" | custom-call | tf_op jit(solution)/shard_map/pallas_call | solution.py:963
  199.7 0.8 fusion.26
  200.5 0.9 copy-done.5
  201.4 0.9 convolution_add_fusion.2
  203.0 1.0 fusion.16
  204.1 1.0 fusion.13
  205.6 2.1 convolution_convert_fusion.3
  207.7 0.7 convolution_convert_fusion.4
  208.5 0.7 convolution_convert_fusion.5
  209.2 0.7 convolution_convert_fusion.6
  210.0 2.6 bitcast_convert_fusion.3
  212.6 2.6 bitcast_convert_fusion.2
  215.3 2.6 bitcast_convert_fusion.1
  217.9 5.6 %convolution_convert_fusion = bf16[4096,1024]{1,0:T(8,128)(2,1)} fusion(bf16[128,1024]{1,0:T(8,128)(2,1)S(1)} %copy-done.26, f32[128,4096]{1,0:T(8,128)S(1)} %copy-done.12), kind=kOutput, calls=%fused_computation.1 | convolution fusion | flops 1082654720 | bytes 10747904 | tf_op jit(solution)/shard_map/dot_general | solution.py:1008
  223.5 4.7 convolution_convert_fusion.2
  228.2 5.7 %convolution_convert_fusion.1 = bf16[1024,4096]{1,0:T(8,128)(2,1)} fusion(bf16[128,4096]{1,0:T(8,128)(2,1)S(1)} %copy-done.17, f32[128,1024]{1,0:T(8,128)S(1)} %get-tuple-element.124, f32[1024]{0:T(1024)S(1)} %copy-done.28, f32[128]{0:T(128)S(1)} %fusion.20), kind=kOutput, calls=%fused_computation.2 | convolution fusion | flops 1078329344 | bytes 9966080 | tf_op jit(solution)/shard_map/dot_general | solution.py:1008
  233.9 254.3 %shard_map.447 = (f32[192,1024]{1,0:T(8,128)S(1)}, f32[64,1024]{1,0:T(8,128)S(1)}, f32[64,1024]{1,0:T(8,128)S(1)}, f32[64,1024]{1,0:T(8,128)S(1)}, f32[64,1024]{...) custom-call(bf16[8,2,192,1024]{3,2,1,0:T(8,128)(2,1)} %bitcast.120, ...), custom_call_target="tpu_custom_call" | custom-call | tf_op jit(solution)/shard_map/pallas_call | solution.py:299
  489.5 0.9 copy.87
  490.4 0.7 copy.88
  492.5 0.7 copy.91
  493.2 1.0 copy.92
  494.2 1.0 copy.93
  495.9 0.7 copy.95
  498.0 1.0 copy.98
  498.9 1.0 copy.99
  (122 shorter events, 9.8 us)
Async XLA Ops:
  0.7 49.4 %copy-start = (bf16[1024,1024]{1,0:T(8,128)(2,1)S(1)}, bf16[1024,1024]{1,0:T(8,128)(2,1)}, u32[]{:S(2)}) copy-start(bf16[1024,1024]{1,0:T(8,128)(2,1)} %param.36) | copy-start | bytes 6291460
  12.1 4.1 copy-start.6
  12.1 4.1 copy-start.9
  13.7 2.5 copy-start.2
  13.7 2.9 copy-start.4
  50.1 6.2 %copy-start.7 = (bf16[16,208,128]{2,1,0:T(8,128)(2,1)}, bf16[16,208,128]{2,1,0:T(8,128)(2,1)S(1)}, u32[]{:S(2)}) copy-start(bf16[16,208,128]{2,1,0:T(8,128)(2,1)S(1)} %get-tuple-element.73.held) | copy-start | bytes 2555908
  50.1 0.7 copy-start.28
  50.1 0.8 copy-start.32
  50.1 6.2 %slice-start = ((s8[8388608]{0:T(1024)(128)(4,1)}), s8[4194304]{0:T(1024)(128)(4,1)S(1)}, s32[]{:S(2)}) async-start(s8[8388608]{0:T(1024)(128)(4,1)} %bitcast.154), calls=%async_computation | async-start | bytes 8388608
  50.9 5.5 %slice-start.1 = ((s8[8388608]{0:T(1024)(128)(4,1)}), s8[4194304]{0:T(1024)(128)(4,1)S(1)}, s32[]{:S(2)}) async-start(s8[8388608]{0:T(1024)(128)(4,1)} %bitcast.154), calls=%async_computation.1 | async-start | bytes 8388608
  50.9 5.5 %copy-start.39 = (f32[1024]{0:T(1024)S(1)}, f32[1024]{0:T(1024)}, u32[]{:S(2)}) copy-start(f32[1024]{0:T(1024)} %param.41) | copy-start | bytes 12292
  56.4 1.6 copy-start.10
  56.4 2.3 copy-start.18
  58.0 0.7 copy-start.30
  110.3 17.6 %copy-start.29 = (bf16[2,64,1024]{2,1,0:T(8,128)(2,1)S(1)}, bf16[2,64,1024]{2,1,0:T(8,128)(2,1)}, u32[]{:S(2)}) copy-start(bf16[2,64,1024]{2,1,0:T(8,128)(2,1)} %param.52) | copy-start | bytes 786436
  128.0 5.9 %copy-start.33 = (f32[1,1024]{1,0:T(1,128)S(1)}, f32[1,1024]{1,0:T(1,128)}, u32[]{:S(2)}) copy-start(f32[1,1024]{1,0:T(1,128)} %get-tuple-element.85) | copy-start | bytes 12292
  128.0 5.9 %copy-start.34 = (f32[1,1024]{1,0:T(1,128)S(1)}, f32[1,1024]{1,0:T(1,128)}, u32[]{:S(2)}) copy-start(f32[1,1024]{1,0:T(1,128)} %get-tuple-element.86) | copy-start | bytes 12292
  128.0 6.1 %copy-start.31 = (f32[1,4096]{1,0:T(1,128)S(1)}, f32[1,4096]{1,0:T(1,128)}, u32[]{:S(2)}) copy-start(f32[1,4096]{1,0:T(1,128)} %get-tuple-element.87) | copy-start | bytes 49156
  135.2 4.4 copy-start.25
  135.2 4.4 copy-start.11
  147.6 6.8 %copy-start.16 = (f32[2,64,1024]{2,1,0:T(8,128)S(1)}, f32[2,64,1024]{2,1,0:T(8,128)}, u32[]{:S(2)}) copy-start(f32[2,64,1024]{2,1,0:T(8,128)} %get-tuple-element.107) | copy-start | bytes 1572868
  155.5 2.0 copy-start.8
  157.4 42.2 %copy-start.3 = (bf16[1024,1024]{1,0:T(8,128)(2,1)S(1)}, bf16[1024,1024]{1,0:T(8,128)(2,1)}, u32[]{:S(2)}) copy-start(bf16[1024,1024]{1,0:T(8,128)(2,1)} %wq_ref.3) | copy-start | bytes 6291460
  199.5 1.9 copy-start.5
  199.6 2.6 copy-start.19
  199.7 2.6 copy-start.21
  199.7 2.6 copy-start.23
  201.4 1.6 copy-start.13
  203.0 1.0 copy-start.14
  204.1 1.6 copy-start.15
  205.3 2.5 copy-start.20
  205.6 2.8 copy-start.24
  207.7 1.5 copy-start.22
  208.5 1.5 copy-start.35
  208.5 1.6 copy-start.38
  210.0 2.6 copy-start.37
  212.6 2.6 copy-start.36
  215.3 2.6 copy-start.12
  215.3 2.6 copy-start.26
  217.9 5.6 %copy-start.27 = (bf16[3,128,1024]{2,1,0:T(8,128)(2,1)S(1)}, bf16[3,128,1024]{2,1,0:T(8,128)(2,1)}, u32[]{:S(2)}) copy-start(bf16[3,128,1024]{2,1,0:T(8,128)(2,1)} %get-tuple-element.75) | copy-start | bytes 2359300
  223.5 4.7 copy-start.17
  497.3 2.6 copy-start.1

commit v4 on v3

--- a/solution.py
+++ b/solution.py
@@ -1,4 +1,5 @@
 import functools
+import types
 
 import jax
 import jax.numpy as jnp
@@ -19,341 +20,15 @@
 LOW = jnp.bfloat16
 LANES = 128
 MESH_ID = pl.DeviceIdType.MESH
-SLOTS = 4
-SROWS = 64
-SCOLS = 512
-DEEP = 8
-
-
-def reduce_kernel(plan, total, *refs):
-    count = len(plan)
-    ins = refs[:count]
-    outs = refs[count : 2 * count]
-    (
-        part, recv_c, half_a, half_b, recv_xa, recv_yb, sum_a, sum_b, recv_xb, line_b,
-        right_a, left_a, right_b, left_b, recv_ya, recv_yb2, staged,
-        load_sem, out_sem, send_sem, recv_sem,
-    ) = refs[2 * count :]
-    f32 = jnp.float32
-    low = jnp.bfloat16
-    utt = lax.axis_index("utt")
-    seq = lax.axis_index("seq")
-    pos = seq // 4
-    col = (seq // 2) % 2
-    core = seq % 2
-    base = pos * 4 + col * 2
-    core_id = (utt, base + 1 - core)
-    col_id = (utt, pos * 4 + (1 - col) * 2 + core)
-    utt_id = (1 - utt, seq)
-    right_id = (utt, lax.rem(seq + 4, 16))
-    left_id = (utt, lax.rem(seq + 12, 16))
-
-    barrier = pltpu.get_barrier_semaphore()
-    for target in (core_id, col_id, utt_id):
-        pl.semaphore_signal(barrier, inc=1, device_id=target, device_id_type=MESH_ID)
-
-    @pl.when(pos < 3)
-    def _():
-        pl.semaphore_signal(barrier, inc=1, device_id=right_id, device_id_type=MESH_ID)
-
-    @pl.when(pos > 0)
-    def _():
-        pl.semaphore_signal(barrier, inc=1, device_id=left_id, device_id_type=MESH_ID)
-
-    pl.semaphore_wait(barrier, jnp.where((pos == 0) | (pos == 3), 4, 5))
-
-    def window(ref, spec, slab, lead):
-        first, _, wide = spec
-        local = slab - first
-        rows = pl.ds(pl.multiple_of((local // wide) * SROWS, SROWS), SROWS)
-        cols = pl.ds(pl.multiple_of((local % wide) * SCOLS, SCOLS), SCOLS)
-        return ref.at[lead + (rows, cols)]
-
-    def load(slab, start):
-        slot = slab % SLOTS
-        if not start:
-            for side in range(2):
-                pltpu.make_async_copy(
-                    ins[0].at[:, side, pl.ds(0, SROWS), pl.ds(0, SCOLS)],
-                    part.at[slot, side],
-                    load_sem.at[slot, side],
-                ).wait()
-            return
-        for ref, spec in zip(ins, plan):
-
-            @pl.when((slab >= spec[0]) & (slab < spec[0] + spec[1]))
-            def _():
-                for side in range(2):
-                    pltpu.make_async_copy(
-                        window(ref, spec, slab, (slice(None), side)),
-                        part.at[slot, side],
-                        load_sem.at[slot, side],
-                    ).start()
-
-    def send(kind, slot, source, target, device):
-        return pltpu.make_async_remote_copy(
-            src_ref=source,
-            dst_ref=target,
-            send_sem=send_sem.at[kind, slot],
-            recv_sem=recv_sem.at[kind, slot],
-            device_id=device,
-            device_id_type=MESH_ID,
-        )
-
-    def core_copy(slot):
-        return send(0, slot, part.at[slot, 1 - core], recv_c.at[slot], core_id)
-
-    def col_copy_a(slot):
-        return send(1, slot, half_a.at[slot, 1 - col], recv_xa.at[slot], col_id)
-
-    def utt_copy_b(slot):
-        return send(2, slot, half_b.at[slot, 1 - utt], recv_yb.at[slot], utt_id)
-
-    def col_copy_b(slot):
-        return send(3, slot, sum_b.at[slot, 1 - col], recv_xb.at[slot], col_id)
-
-    def utt_copy_a(slot, deep):
-        return send(4, slot, sum_a.at[deep, pos], recv_ya.at[slot], utt_id)
-
-    def utt_copy_b2(slot, deep):
-        return send(5, slot, line_b.at[deep, pos], recv_yb2.at[slot], utt_id)
-
-    def line_right(kind, slot, deep, step, source, target):
-        dest = jnp.minimum(4 - step + pos, 3)
-        return send(kind + step - 1, slot, source.at[deep, dest], target.at[slot, step - 1], right_id)
-
-    def line_left(kind, slot, deep, step, source, target):
-        dest = jnp.maximum(pos - 4 + step, 0)
-        return send(kind + step - 1, slot, source.at[deep, dest], target.at[slot, step - 1], left_id)
-
-    def line_start(slot, deep, step, source, right, left, kind):
-        @pl.when((pos <= step - 1) & (pos < 3))
-        def _():
-            line_right(kind, slot, deep, step, source, right).start()
-
-        @pl.when((pos >= 4 - step) & (pos > 0))
-        def _():
-            line_left(kind + 3, slot, deep, step, source, left).start()
-
-    def line_finish(slot, deep, step, source, right, left, kind):
-        @pl.when((pos <= step - 1) & (pos < 3))
-        def _():
-            line_right(kind, slot, deep, step, source, right).wait_send()
-
-        @pl.when((pos >= 4 - step) & (pos > 0))
-        def _():
-            line_left(kind + 3, slot, deep, step, source, left).wait_send()
-
-        @pl.when((pos >= 1) & (pos <= step))
-        def _():
-            line_right(kind, slot, deep, step, source, right).wait_recv()
-            dest = 3 - step + pos
-            source[deep, dest] = (
-                source[deep, dest].astype(f32) + right[slot, step - 1].astype(f32)
-            ).astype(low)
-
-        @pl.when((pos <= 2) & (pos >= 3 - step))
-        def _():
-            line_left(kind + 3, slot, deep, step, source, left).wait_recv()
-            dest = pos + step - 3
-            source[deep, dest] = (
-                source[deep, dest].astype(f32) + left[slot, step - 1].astype(f32)
-            ).astype(low)
-
-    line_a = (sum_a, right_a, left_a, 6)
-    line_bb = (line_b, right_b, left_b, 12)
-
-    load(0, True)
-
-    @pl.loop(0, total + 8)
-    def _(tick):
-        def stage(offset):
-            slab = tick - offset
-            return slab, lax.rem(slab + SLOTS * 4, SLOTS), pl.when((slab >= 0) & (slab < total))
-
-        slab, slot, guard = stage(0)
-
-        @pl.when(slab + 1 < total)
-        def _():
-            load(slab + 1, True)
-
-        @guard
-        def _():
-            load(slab, False)
-            core_copy(slot).start()
-
-        slab1, slot1, guard = stage(1)
-
-        @guard
-        def _():
-            core_copy(slot1).wait()
-            for line in range(4):
-                for side in range(2):
-                    both = part[slot1, core, 2 * line + side].astype(f32) + recv_c[
-                        slot1, 2 * line + side
-                    ].astype(f32)
-                    both = both.astype(low)
-                    half_a[slot1, side, line] = both[:32]
-                    half_b[slot1, 0, side, line] = both[32:48]
-                    half_b[slot1, 1, side, line] = both[48:]
-            col_copy_a(slot1).start()
-            utt_copy_b(slot1).start()
-
-        slab2, slot2, guard = stage(2)
-        deep2 = lax.rem(slab2 + DEEP, DEEP)
-
-        @guard
-        def _():
-            col_copy_a(slot2).wait()
-            sum_a[deep2] = (
-                half_a[slot2, col].astype(f32) + recv_xa[slot2].astype(f32)
-            ).astype(low)
-            line_start(slot2, deep2, 1, *line_a)
-            utt_copy_b(slot2).wait()
-            sum_b[slot2] = (
-                half_b[slot2, utt].astype(f32) + recv_yb[slot2].astype(f32)
-            ).astype(low)
-            col_copy_b(slot2).start()
-
-        slab3, slot3, guard = stage(3)
-        deep3 = lax.rem(slab3 + DEEP, DEEP)
-
-        @guard
-        def _():
-            line_finish(slot3, deep3, 1, *line_a)
-            line_start(slot3, deep3, 2, *line_a)
-            col_copy_b(slot3).wait()
-            line_b[deep3] = (
-                sum_b[slot3, col].astype(f32) + recv_xb[slot3].astype(f32)
-            ).astype(low)
-            line_start(slot3, deep3, 1, *line_bb)
-
-        slab4, slot4, guard = stage(4)
-        deep4 = lax.rem(slab4 + DEEP, DEEP)
-
-        @guard
-        def _():
-            line_finish(slot4, deep4, 2, *line_a)
-            line_start(slot4, deep4, 3, *line_a)
-            line_finish(slot4, deep4, 1, *line_bb)
-            line_start(slot4, deep4, 2, *line_bb)
-
-        slab5, slot5, guard = stage(5)
-        deep5 = lax.rem(slab5 + DEEP, DEEP)
-
-        @guard
-        def _():
-            line_finish(slot5, deep5, 3, *line_a)
-            utt_copy_a(slot5, deep5).start()
-            line_finish(slot5, deep5, 2, *line_bb)
-            line_start(slot5, deep5, 3, *line_bb)
-
-        slab6, slot6, guard = stage(6)
-        deep6 = lax.rem(slab6 + DEEP, DEEP)
-
-        @guard
-        def _():
-            utt_copy_a(slot6, deep6).wait()
-            staged[slot6, 0:32] = sum_a[deep6, pos].astype(f32) + recv_ya[slot6].astype(f32)
-            line_finish(slot6, deep6, 3, *line_bb)
-            utt_copy_b2(slot6, deep6).start()
-
-        slab7, slot7, guard = stage(7)
-        deep7 = lax.rem(slab7 + DEEP, DEEP)
-
-        @guard
-        def _():
-            utt_copy_b2(slot7, deep7).wait()
-            mine = line_b[deep7, pos].astype(f32)
-            theirs = recv_yb2[slot7].astype(f32)
-            staged[slot7, 32:48] = jnp.where(utt == 0, mine, theirs)
-            staged[slot7, 48:64] = jnp.where(utt == 0, theirs, mine)
-            for ref, spec in zip(outs, plan):
-
-                @pl.when((slab7 >= spec[0]) & (slab7 < spec[0] + spec[1]))
-                def _():
-                    pltpu.make_async_copy(
-                        staged.at[slot7], window(ref, spec, slab7, ()), out_sem.at[slot7]
-                    ).start()
-
-        slab8, slot8, guard = stage(8)
-
-        @guard
-        def _():
-            pltpu.make_async_copy(
-                staged.at[slot8], outs[0].at[pl.ds(0, SROWS), pl.ds(0, SCOLS)], out_sem.at[slot8]
-            ).wait()
-
-
-def reduce_grads(arrays):
-    views, plan, shapes, total = [], [], [], 0
-    for item in arrays:
-        rows, cols = item.shape[0] // 16, item.shape[1]
-        views.append(item.reshape(8, 2, rows, cols))
-        slabs = (rows // SROWS) * (cols // SCOLS)
-        plan.append((total, slabs, cols // SCOLS))
-        shapes.append(jax.ShapeDtypeStruct((rows, cols), jnp.float32))
-        total += slabs
-    low = jnp.bfloat16
-    hbm = pl.BlockSpec(memory_space=pl.ANY)
-    return pl.pallas_call(
-        functools.partial(reduce_kernel, tuple(plan), total),
-        out_shape=tuple(shapes),
-        in_specs=[hbm] * len(views),
-        out_specs=tuple([hbm] * len(views)),
-        scratch_shapes=[
-            pltpu.VMEM((SLOTS, 2, 8, 64, SCOLS), low),
-            pltpu.VMEM((SLOTS, 8, 64, SCOLS), low),
-            pltpu.VMEM((SLOTS, 2, 4, 32, SCOLS), low),
-            pltpu.VMEM((SLOTS, 2, 2, 4, 16, SCOLS), low),
-            pltpu.VMEM((SLOTS, 4, 32, SCOLS), low),
-            pltpu.VMEM((SLOTS, 2, 4, 16, SCOLS), low),
-            pltpu.VMEM((DEEP, 4, 32, SCOLS), low),
-            pltpu.VMEM((SLOTS, 2, 4, 16, SCOLS), low),
-            pltpu.VMEM((SLOTS, 4, 16, SCOLS), low),
-            pltpu.VMEM((DEEP, 4, 16, SCOLS), low),
-            pltpu.VMEM((SLOTS, 3, 32, SCOLS), low),
-            pltpu.VMEM((SLOTS, 3, 32, SCOLS), low),
-            pltpu.VMEM((SLOTS, 3, 16, SCOLS), low),
-            pltpu.VMEM((SLOTS, 3, 16, SCOLS), low),
-            pltpu.VMEM((SLOTS, 32, SCOLS), low),
-            pltpu.VMEM((SLOTS, 16, SCOLS), low),
-            pltpu.VMEM((SLOTS, 64, SCOLS), jnp.float32),
-            pltpu.SemaphoreType.DMA((SLOTS, 2)),
-            pltpu.SemaphoreType.DMA((SLOTS,)),
-            pltpu.SemaphoreType.DMA((18, SLOTS)),
-            pltpu.SemaphoreType.DMA((18, SLOTS)),
-        ],
-        compiler_params=pltpu.CompilerParams(
-            collective_id=1, has_side_effects=True, vmem_limit_bytes=40 << 20
-        ),
-    )(*views)
 
 
 def reduce_all(grads):
-    low = [item.astype(jnp.bfloat16) for item in grads]
-    if lax.axis_size("seq") != 16 or lax.axis_size("utt") != 2:
-        return tuple(
-            lax.psum(
-                lax.psum_scatter(item, "seq", scatter_dimension=0, tiled=True), "utt"
-            ).astype(jnp.float32)
-            for item in low
-        )
-    wide = [index for index, item in enumerate(low) if item.ndim == 2]
-    flat = [index for index, item in enumerate(low) if item.ndim == 1]
-    small = jnp.concatenate([low[index].reshape(16, -1) for index in flat], axis=1)
-    small = jnp.pad(small, ((0, 0), (0, SROWS * SCOLS - small.shape[1])))
-    sums = reduce_grads([low[index] for index in wide] + [small.reshape(16 * SROWS, SCOLS)])
-    out = [None] * len(low)
-    for index, total in zip(wide, sums):
-        out[index] = total
-    first = 0
-    rest = sums[-1].reshape(-1)
-    for index in flat:
-        size = low[index].shape[0] // 16
-        out[index] = rest[first : first + size]
-        first += size
-    return tuple(out)
+    return tuple(
+        lax.psum(
+            lax.psum_scatter(item.astype(LOW), "seq", scatter_dimension=0, tiled=True), "utt"
+        ).astype(F32)
+        for item in grads
+    )
 
 
 def mul(left_side, right_side):
@@ -982,6 +657,651 @@
             collective_id=3, has_side_effects=True, vmem_limit_bytes=48 << 20
         ),
     )(grad_mixed, saved, log_total)
+
+
+SLOTS = 4
+DEEP = 8
+SROWS = 64
+SCOLS = 512
+DRAIN = 8
+PLAN = (
+    (0, 8, 8), (8, 8, 2), (16, 2, 2), (18, 2, 2), (20, 2, 2), (22, 2, 2), (24, 6, 2),
+    (30, 8, 2), (38, 8, 8), (46, 2, 2), (48, 2, 2), (50, 2, 2), (52, 2, 2), (54, 1, 1),
+)
+SLABS = 55
+LOADED = 16
+AT_BACK = 8
+AT_ATTEND = 10
+AT_LANDED = 20
+
+
+def tail_kernel(names, out_count, *refs):
+    r = types.SimpleNamespace(**dict(zip(names, refs)))
+    outs = refs[names.index("out_0") : names.index("out_0") + out_count]
+    utt = lax.axis_index("utt")
+    seq = lax.axis_index("seq")
+    count = 16
+    pos = seq // 4
+    col = (seq // 2) % 2
+    core = seq % 2
+    core_id = (utt, pos * 4 + col * 2 + 1 - core)
+    col_id = (utt, pos * 4 + (1 - col) * 2 + core)
+    utt_id = (1 - utt, seq)
+    right_id = (utt, lax.rem(seq + 4, 16))
+    left_id = (utt, lax.rem(seq + 12, 16))
+
+    barrier = greet(count)
+    pl.semaphore_signal(barrier, inc=1, device_id=utt_id, device_id_type=MESH_ID)
+
+    def window(ref, spec, slab, lead):
+        local = slab - spec[0]
+        rows = pl.ds(pl.multiple_of((local // spec[2]) * SROWS, SROWS), SROWS)
+        cols = pl.ds(pl.multiple_of((local % spec[2]) * SCOLS, SCOLS), SCOLS)
+        return ref.at[lead + (rows, cols)]
+
+    def load_start(slab):
+        slot = slab % SLOTS
+        for ref, spec in ((r.l_up, PLAN[0]), (r.l_down, PLAN[1])):
+
+            @pl.when((slab >= spec[0]) & (slab < spec[0] + spec[1]))
+            def _():
+                for side in range(2):
+                    pltpu.make_async_copy(
+                        window(ref, spec, slab, (slice(None), side)),
+                        r.part.at[slot, side],
+                        r.load_sem.at[slot, side],
+                    ).start()
+
+    def load_wait(slot):
+        for side in range(2):
+            pltpu.make_async_copy(
+                r.l_up.at[:, side, pl.ds(0, SROWS), pl.ds(0, SCOLS)],
+                r.part.at[slot, side],
+                r.load_sem.at[slot, side],
+            ).wait()
+
+    def weights(block, slot):
+        start = block * SCOLS if isinstance(block, int) else pl.multiple_of(block * SCOLS, SCOLS)
+        return (
+            pltpu.make_async_copy(
+                r.g_w_up.at[:, pl.ds(start, SCOLS)], r.up_buf.at[slot], r.weight_sem.at[slot, 0]
+            ),
+            pltpu.make_async_copy(
+                r.g_w_down.at[pl.ds(start, SCOLS)], r.down_buf.at[slot], r.weight_sem.at[slot, 1]
+            ),
+        )
+
+    fetches = (
+        (r.g_w_o, r.square.at[0]), (r.g_w_q, r.square.at[1]), (r.g_w_k, r.square.at[2]),
+        (r.g_w_v, r.square.at[3]), (r.saved, r.held), (r.l_normed, r.l_x.at[0]),
+        (r.l_mixed, r.l_x.at[1]), (r.l_dq, r.l_g.at[0]), (r.l_dk, r.l_g.at[1]),
+        (r.l_dv, r.l_g.at[2]), (r.l_dattn, r.l_g.at[3]), (r.rest, r.table_g),
+        (r.g_act, r.act_buf), (r.g_mixed, r.g_x.at[0]), (r.g_normed, r.g_x.at[1]),
+    )
+
+    def fetch(*which):
+        return [
+            pltpu.make_async_copy(*fetches[index], r.fetch_sem.at[index]) for index in which
+        ]
+
+    for copy in weights(0, 0) + tuple(fetch(0)):
+        copy.start()
+    load_start(0)
+
+    def send(kind, slot, source, target, device):
+        return pltpu.make_async_remote_copy(
+            src_ref=source,
+            dst_ref=target,
+            send_sem=r.send_sem.at[kind, slot],
+            recv_sem=r.recv_sem.at[kind, slot],
+            device_id=device,
+            device_id_type=MESH_ID,
+        )
+
+    def core_copy(slot):
+        return send(0, slot, r.part.at[slot, 1 - core], r.recv_c.at[slot], core_id)
+
+    def col_copy_a(slot):
+        return send(1, slot, r.half_a.at[slot, 1 - col], r.recv_xa.at[slot], col_id)
+
+    def utt_copy_b(slot):
+        return send(2, slot, r.half_b.at[slot, 1 - utt], r.recv_yb.at[slot], utt_id)
+
+    def col_copy_b(slot):
+        return send(3, slot, r.sum_b.at[slot, 1 - col], r.recv_xb.at[slot], col_id)
+
+    def utt_copy_a(slot, deep):
+        return send(4, slot, r.sum_a.at[deep, pos], r.recv_ya.at[slot], utt_id)
+
+    def utt_copy_b2(slot, deep):
+        return send(5, slot, r.line_b.at[deep, pos], r.recv_yb2.at[slot], utt_id)
+
+    def line_right(kind, slot, deep, step, source, target):
+        dest = jnp.minimum(4 - step + pos, 3)
+        return send(kind + step - 1, slot, source.at[deep, dest], target.at[slot, step - 1], right_id)
+
+    def line_left(kind, slot, deep, step, source, target):
+        dest = jnp.maximum(pos - 4 + step, 0)
+        return send(kind + step - 1, slot, source.at[deep, dest], target.at[slot, step - 1], left_id)
+
+    def line_start(slot, deep, step, source, right, left, kind):
+        @pl.when((pos <= step - 1) & (pos < 3))
+        def _():
+            line_right(kind, slot, deep, step, source, right).start()
+
+        @pl.when((pos >= 4 - step) & (pos > 0))
+        def _():
+            line_left(kind + 3, slot, deep, step, source, left).start()
+
+    def line_finish(slot, deep, step, source, right, left, kind):
+        @pl.when((pos <= step - 1) & (pos < 3))
+        def _():
+            line_right(kind, slot, deep, step, source, right).wait_send()
+
+        @pl.when((pos >= 4 - step) & (pos > 0))
+        def _():
+            line_left(kind + 3, slot, deep, step, source, left).wait_send()
+
+        @pl.when((pos >= 1) & (pos <= step))
+        def _():
+            line_right(kind, slot, deep, step, source, right).wait_recv()
+            dest = 3 - step + pos
+            source[deep, dest] = (
+                source[deep, dest].astype(F32) + right[slot, step - 1].astype(F32)
+            ).astype(LOW)
+
+        @pl.when((pos <= 2) & (pos >= 3 - step))
+        def _():
+            line_left(kind + 3, slot, deep, step, source, left).wait_recv()
+            dest = pos + step - 3
+            source[deep, dest] = (
+                source[deep, dest].astype(F32) + left[slot, step - 1].astype(F32)
+            ).astype(LOW)
+
+    line_a = (r.sum_a, r.right_a, r.left_a, 6)
+    line_bb = (r.line_b, r.right_b, r.left_b, 12)
+
+    def advance(tick):
+        def stage(offset):
+            slab = tick - offset
+            return (
+                slab,
+                lax.rem(slab + SLOTS * 4, SLOTS),
+                lax.rem(slab + DEEP, DEEP),
+                pl.when((slab >= 0) & (slab < SLABS)),
+            )
+
+        slab, slot, _, guard = stage(0)
+        load_start(slab + 1)
+
+        @pl.when(slab < LOADED)
+        def _():
+            load_wait(slot)
+
+        @guard
+        def _():
+            core_copy(slot).start()
+
+        _, slot1, _, guard = stage(1)
+
+        @guard
+        def _():
+            core_copy(slot1).wait()
+            for line in range(4):
+                for side in range(2):
+                    both = r.part[slot1, core, 2 * line + side].astype(F32) + r.recv_c[
+                        slot1, 2 * line + side
+                    ].astype(F32)
+                    both = both.astype(LOW)
+                    r.half_a[slot1, side, line] = both[:32]
+                    r.half_b[slot1, 0, side, line] = both[32:48]
+                    r.half_b[slot1, 1, side, line] = both[48:]
+            col_copy_a(slot1).start()
+            utt_copy_b(slot1).start()
+
+        _, slot2, deep2, guard = stage(2)
+
+        @guard
+        def _():
+            col_copy_a(slot2).wait()
+            r.sum_a[deep2] = (
+                r.half_a[slot2, col].astype(F32) + r.recv_xa[slot2].astype(F32)
+            ).astype(LOW)
+            line_start(slot2, deep2, 1, *line_a)
+            utt_copy_b(slot2).wait()
+            r.sum_b[slot2] = (
+                r.half_b[slot2, utt].astype(F32) + r.recv_yb[slot2].astype(F32)
+            ).astype(LOW)
+            col_copy_b(slot2).start()
+
+        _, slot3, deep3, guard = stage(3)
+
+        @guard
+        def _():
+            line_finish(slot3, deep3, 1, *line_a)
+            line_start(slot3, deep3, 2, *line_a)
+            col_copy_b(slot3).wait()
+            r.line_b[deep3] = (
+                r.sum_b[slot3, col].astype(F32) + r.recv_xb[slot3].astype(F32)
+            ).astype(LOW)
+            line_start(slot3, deep3, 1, *line_bb)
+
+        _, slot4, deep4, guard = stage(4)
+
+        @guard
+        def _():
+            line_finish(slot4, deep4, 2, *line_a)
+            line_start(slot4, deep4, 3, *line_a)
+            line_finish(slot4, deep4, 1, *line_bb)
+            line_start(slot4, deep4, 2, *line_bb)
+
+        _, slot5, deep5, guard = stage(5)
+
+        @guard
+        def _():
+            line_finish(slot5, deep5, 3, *line_a)
+            utt_copy_a(slot5, deep5).start()
+            line_finish(slot5, deep5, 2, *line_bb)
+            line_start(slot5, deep5, 3, *line_bb)
+
+        _, slot6, deep6, guard = stage(6)
+
+        @guard
+        def _():
+            utt_copy_a(slot6, deep6).wait()
+            r.staged[slot6, 0:32] = r.sum_a[deep6, pos].astype(F32) + r.recv_ya[slot6].astype(F32)
+            line_finish(slot6, deep6, 3, *line_bb)
+            utt_copy_b2(slot6, deep6).start()
+
+        slab7, slot7, deep7, guard = stage(7)
+
+        @guard
+        def _():
+            utt_copy_b2(slot7, deep7).wait()
+            mine = r.line_b[deep7, pos].astype(F32)
+            theirs = r.recv_yb2[slot7].astype(F32)
+            r.staged[slot7, 32:48] = jnp.where(utt == 0, mine, theirs)
+            r.staged[slot7, 48:64] = jnp.where(utt == 0, theirs, mine)
+            for ref, spec in zip(outs, PLAN):
+
+                @pl.when((slab7 >= spec[0]) & (slab7 < spec[0] + spec[1]))
+                def _():
+                    pltpu.make_async_copy(
+                        r.staged.at[slot7], window(ref, spec, slab7, ()), r.out_sem.at[slot7]
+                    ).start()
+
+        _, slot8, _, guard = stage(8)
+
+        @guard
+        def _():
+            pltpu.make_async_copy(
+                r.staged.at[slot8], outs[0].at[pl.ds(0, SROWS), pl.ds(0, SCOLS)], r.out_sem.at[slot8]
+            ).wait()
+
+    def cols_of(index):
+        return pl.ds(pl.multiple_of(index * SCOLS, SCOLS), SCOLS)
+
+    def put(slot, dest, rows):
+        r.part[slot, dest % 2, dest // 2] = rows.astype(LOW)
+
+    def put_product(slot, left_of, right):
+        for quarter in range(4):
+            rows = mul(left_of(quarter), right)
+            for index in range(4):
+                put(slot, 4 * quarter + index, rows[64 * index : 64 * index + 64])
+
+    def quarter_rows(ref, lead=()):
+        return lambda quarter: ref[lead + (slice(256 * quarter, 256 * quarter + 256),)]
+
+    def produce(slab):
+        slot = slab % SLOTS
+
+        def among(first, number):
+            return pl.when((slab >= first) & (slab < first + number))
+
+        @among(16, 8)
+        def _():
+            local = slab - 16
+            put_product(slot, quarter_rows(r.l_x_t), r.l_g[local // 2, :, cols_of(local % 2)])
+
+        @among(24, 6)
+        def _():
+            local = slab - 24
+            for dest in range(16):
+                place = 3 * dest + local // 2
+                book = place // 16
+                first = (place % 16) * SROWS
+                ids = first + lax.broadcasted_iota(jnp.int32, (SROWS, LANES), 0)
+                picked = (ids == r.codes[book][0:1]).astype(LOW)
+                put(slot, dest, mul(picked, r.table_g[book, :, cols_of(local % 2)]))
+
+        @among(30, 8)
+        def _():
+            local = slab - 30
+            inner = local // 2
+
+            def rows(quarter):
+                return jnp.concatenate(
+                    [
+                        r.act_t[pl.ds(pl.multiple_of(256 * dest + 64 * inner, 64), 64)]
+                        for dest in range(4 * quarter, 4 * quarter + 4)
+                    ],
+                    axis=0,
+                )
+
+            put_product(slot, rows, r.dout_low[:, cols_of(local % 2)])
+
+        @among(38, 8)
+        def _():
+            put_product(slot, quarter_rows(r.g_hn_t), r.du[:, cols_of(slab - 38)])
+
+        @among(46, 8)
+        def _():
+            local = slab - 46
+            kind = local // 2
+            put_product(
+                slot,
+                quarter_rows(r.g_x_t, (jnp.minimum(kind, 1),)),
+                r.g_g[kind, :, cols_of(local % 2)],
+            )
+
+        @pl.when(slab == 54)
+        def _():
+            b_down = jnp.sum(r.dout_low[...].astype(F32), axis=0, keepdims=True)
+            for dest in range(16):
+                shared = slice(LANES * (dest // 2), LANES * (dest // 2) + LANES)
+                rows = [r.dn1[:, shared], r.dn2[:, shared], b_down[:, shared]]
+                for index in range(2):
+                    first = 256 * (dest % 2) + LANES * index
+                    rows.append(r.db1[dest // 2 : dest // 2 + 1, first : first + LANES])
+                rows += [r.l_dn1[:, shared], r.l_dn2[:, shared], r.l_db2[:, shared]]
+                for index in range(2):
+                    first = 256 * dest + LANES * index
+                    rows.append(r.l_db1[:, first : first + LANES])
+                rows.append(jnp.zeros((6, LANES), F32))
+                r.part[slot, dest % 2, dest // 2, 0:16, 0:LANES] = jnp.concatenate(
+                    rows, axis=0
+                ).astype(LOW)
+
+    own_utt, own_pair = seq // 8, seq % 8
+    own_cols = pl.ds(pl.multiple_of(own_pair * LANES, LANES), LANES)
+
+    def pair_cols(other):
+        return pl.ds(pl.multiple_of((other % 8) * LANES, LANES), LANES)
+
+    def hand_out(other):
+        return remote(
+            r.dmix.at[other // 8, :, pair_cols(other)], r.grads.at[seq], r.send_one.at[other],
+            r.recv_one.at[seq], other,
+        )
+
+    def hand_back(block):
+        return remote(
+            r.pieces.at[block], r.landed.at[:, own_utt, :, own_cols], r.send_two.at[block],
+            r.recv_two.at[seq], block,
+        )
+
+    def others(body):
+        @pl.loop(1, count)
+        def _(step):
+            body(lax.rem(seq + step, count))
+
+    def compute(tick):
+        def at(*ticks):
+            hit = tick == ticks[0]
+            for item in ticks[1:]:
+                hit = hit | (tick == item)
+            return pl.when(hit)
+
+        @pl.when(tick < 8)
+        def _():
+            slot = tick % 2
+            for copy in weights(tick, slot):
+                copy.wait()
+
+            @pl.when(tick < 7)
+            def _():
+                for copy in weights(tick + 1, 1 - slot):
+                    copy.start()
+
+            @pl.when(tick == 0)
+            def _():
+                r.dout_low[...] = r.dout[...].astype(LOW)
+                r.dhn[...] = jnp.zeros_like(r.dhn)
+
+            cols = cols_of(tick)
+            _, slope = gelu_parts(r.u[:, cols])
+            du = (mul_t(r.dout_low[...], r.down_buf[slot]) * slope).astype(LOW)
+            r.du[:, cols] = du
+            r.db1[pl.ds(tick, 1), :] = jnp.sum(du.astype(F32), axis=0, keepdims=True)
+            r.dhn[...] += mul_t(du, r.up_buf[slot])
+
+        @at(3)
+        def _():
+            for copy in fetch(4, 5, 6, 7, 8, 9, 10):
+                copy.start()
+
+        @at(12)
+        def _():
+            for copy in fetch(1, 2, 3, 11, 12, 13, 14):
+                copy.start()
+
+        @at(AT_BACK)
+        def _():
+            for copy in fetch(0):
+                copy.wait()
+            dmid, gain = scale_back(r.mid[...], r.n2[...], r.dhn[...])
+            r.dn2[...] = jnp.sum(gain, axis=0, keepdims=True)
+            dmid = dmid + r.dout[...]
+            r.dmid[...] = dmid
+            dattn = dmid.astype(LOW)
+            r.g_g[0] = dattn
+            r.dmix[...] = mul_t(dattn, r.square[0]).astype(LOW).reshape(r.dmix.shape)
+            others(lambda other: hand_out(other).start())
+            r.grads[seq] = r.dmix[own_utt, :, own_cols]
+
+        @at(AT_BACK + 1)
+        def _():
+            for copy in fetch(4, 5, 6, 7, 8, 9, 10):
+                copy.wait()
+            r.k_t[...] = r.held[:, 64:128].reshape(count * HD, LANES).T
+            fill_bias(r.bias, r.held[:, 192:208])
+            r.dk_acc[...] = jnp.zeros_like(r.dk_acc)
+            r.dv_acc[...] = jnp.zeros_like(r.dv_acc)
+            r.l_x_t[...] = r.l_x[0].T
+
+        @at(AT_ATTEND)
+        def _():
+            def arrived(other):
+                here = r.grads.at[other]
+                remote(here, here, r.send_one.at[other], r.recv_one.at[other], other).wait_recv()
+
+            others(arrived)
+
+        for order, group in enumerate(reversed(range(4))):
+            below = group * 256
+            here = below + 256
+            begin = AT_ATTEND + 2 * order
+
+            @at(begin, begin + 1)
+            def _():
+                @pl.loop(0, 2)
+                def _(index):
+                    block = 4 * group + 2 * (tick - begin) + index
+                    attend_back_block(r, group, below, here, block)
+
+            @at(begin + 1)
+            def _():
+                for block in range(4 * group, 4 * group + 4):
+                    rows = slice(block * HD, (block + 1) * HD)
+                    r.pieces[block, 1] = r.dk_acc[rows].astype(LOW)
+                    r.pieces[block, 2] = r.dv_acc[rows].astype(LOW)
+
+                    @pl.when(block != seq)
+                    def _():
+                        hand_back(block).start()
+
+                    @pl.when(block == seq)
+                    def _():
+                        r.landed[:, own_utt, :, own_cols] = r.pieces[block]
+
+        @at(AT_LANDED)
+        def _():
+            def arrived(other):
+                here = r.landed.at[:, other // 8, :, pair_cols(other)]
+                remote(here, here, r.send_two.at[other], r.recv_two.at[other], other).wait_recv()
+
+            others(arrived)
+            others(lambda other: hand_out(other).wait_send())
+            others(lambda other: hand_back(other).wait_send())
+            for index in range(3):
+                r.g_g[1 + index] = r.landed[index].reshape(r.g_g.shape[1:])
+
+        @at(AT_LANDED + 1)
+        def _():
+            for copy in fetch(1, 2, 3, 11, 12, 13, 14):
+                copy.wait()
+            r.l_x_t[...] = r.l_x[1].T
+            r.dhn[...] = mul_t(r.g_g[1], r.square[1])
+
+        @at(AT_LANDED + 2)
+        def _():
+            r.dhn[...] += mul_t(r.g_g[2], r.square[2])
+
+        @at(AT_LANDED + 3)
+        def _():
+            dnormed = r.dhn[...] + mul_t(r.g_g[3], r.square[3])
+            dx, gain = scale_back(r.x[...].astype(F32), r.n1[...], dnormed)
+            r.dn1[...] = jnp.sum(gain, axis=0, keepdims=True)
+            r.dx[...] = dx + r.dmid[...]
+
+        @at(AT_LANDED + 4)
+        def _():
+            r.act_t[...] = r.act_buf[...].T
+
+        @at(AT_LANDED + 5)
+        def _():
+            r.g_hn_t[...] = r.hn[...].T
+            r.g_x_t[0] = r.g_x[0].T
+            r.g_x_t[1] = r.g_x[1].T
+
+    pl.semaphore_wait(barrier, count)
+
+    @pl.loop(0, SLABS + DRAIN)
+    def _(tick):
+        advance(tick)
+        compute(tick)
+        produce(tick + 1)
+
+
+def attend_back_block(r, group, below, here, block):
+    query = two_heads(r.held[block, 0:64] * LOW(HD ** (-0.5)))
+    grad = two_heads(r.grads[block])
+    log_total = r.log_total[block][0:1]
+    near_v = r.held[4 * group : 4 * group + 4, 128:192].reshape(256, LANES)
+    near_k = r.held[4 * group : 4 * group + 4, 64:128].reshape(256, LANES)
+    near = masked_scores(mul_t(near_k, query), r.bias[below:here], below, block)
+    near = jnp.exp(near - log_total)
+    near_dp = mul_t(near_v, grad)
+    delta = jnp.sum(near * near_dp, axis=0, keepdims=True)
+    if group:
+        far_v = r.held[0 : 4 * group, 128:192].reshape(below, LANES)
+        far_k = r.held[0 : 4 * group, 64:128].reshape(below, LANES)
+        far = jnp.exp(mul_t(far_k, query) + r.bias[0:below] - log_total)
+        far_dp = mul_t(far_v, grad)
+        delta = delta + jnp.sum(far * far_dp, axis=0, keepdims=True)
+        far_ds = (far * (far_dp - delta)).astype(LOW)
+        r.dk_acc[0:below] += mul(far_ds, query)
+        r.dv_acc[0:below] += mul(far.astype(LOW), grad)
+    near_ds = (near * (near_dp - delta)).astype(LOW)
+    r.dk_acc[below:here] += mul(near_ds, query)
+    r.dv_acc[below:here] += mul(near.astype(LOW), grad)
+    dq = mul(r.k_t[:, below:here], near_ds)
+    if group:
+        dq = dq + mul(r.k_t[:, 0:below], far_ds)
+    r.pieces[block, 0] = (join_heads(dq) * HD ** (-0.5)).astype(LOW)
+
+
+def finish_on_slice(far, near):
+    vmem = pl.BlockSpec(memory_space=pltpu.VMEM)
+    hbm = pl.BlockSpec(memory_space=pl.ANY)
+    rows, width = near["x"].shape
+    wide = near["u"].shape[1]
+    utts = rows // HD
+    shapes = [
+        (width // 16, wide), (wide // 16, width), (width // 16, width), (width // 16, width),
+        (width // 16, width), (width // 16, width), (3 * 1024 // 16, width), (wide // 16, width),
+        (width // 16, wide), (width // 16, width), (width // 16, width), (width // 16, width),
+        (width // 16, width), (SROWS, SCOLS),
+    ]
+    out_names = ["dx"] + ["out_%d" % index for index in range(len(shapes))]
+    rows_l = far["l_normed"].shape[0]
+    buffers = dict(
+        part=((SLOTS, 2, 8, 64, SCOLS), LOW),
+        recv_c=((SLOTS, 8, 64, SCOLS), LOW),
+        half_a=((SLOTS, 2, 4, 32, SCOLS), LOW),
+        half_b=((SLOTS, 2, 2, 4, 16, SCOLS), LOW),
+        recv_xa=((SLOTS, 4, 32, SCOLS), LOW),
+        recv_yb=((SLOTS, 2, 4, 16, SCOLS), LOW),
+        sum_a=((DEEP, 4, 32, SCOLS), LOW),
+        sum_b=((SLOTS, 2, 4, 16, SCOLS), LOW),
+        recv_xb=((SLOTS, 4, 16, SCOLS), LOW),
+        line_b=((DEEP, 4, 16, SCOLS), LOW),
+        right_a=((SLOTS, 3, 32, SCOLS), LOW),
+        left_a=((SLOTS, 3, 32, SCOLS), LOW),
+        right_b=((SLOTS, 3, 16, SCOLS), LOW),
+        left_b=((SLOTS, 3, 16, SCOLS), LOW),
+        recv_ya=((SLOTS, 32, SCOLS), LOW),
+        recv_yb2=((SLOTS, 16, SCOLS), LOW),
+        staged=((SLOTS, 64, SCOLS), F32),
+        up_buf=((2, width, SCOLS), LOW),
+        down_buf=((2, SCOLS, width), LOW),
+        square=((4, width, width), LOW),
+        held=(far["saved"].shape, LOW),
+        l_x=((2, rows_l, width), LOW),
+        l_g=((4, rows_l, width), LOW),
+        l_x_t=((width, rows_l), LOW),
+        table_g=(far["rest"].shape, LOW),
+        act_buf=((rows, wide), LOW),
+        act_t=((wide, rows), LOW),
+        g_x=((2, rows, width), LOW),
+        g_x_t=((2, width, rows), LOW),
+        g_hn_t=((width, rows), LOW),
+        g_g=((4, rows, width), LOW),
+        dout_low=((rows, width), LOW),
+        du=((rows, wide), LOW),
+        db1=((8, SCOLS), F32),
+        dn1=((1, width), F32),
+        dn2=((1, width), F32),
+        dhn=((rows, width), F32),
+        dmid=((rows, width), F32),
+        dmix=((utts, HD, width), LOW),
+        grads=((16, HD, LANES), LOW),
+        landed=((3, utts, HD, width), LOW),
+        pieces=((16, 3, HD, LANES), LOW),
+        dk_acc=((16 * HD, LANES), F32),
+        dv_acc=((16 * HD, LANES), F32),
+        bias=((16 * HD, LANES), F32),
+        k_t=((LANES, 16 * HD), LOW),
+    )
+    semaphores = dict(
+        load_sem=(SLOTS, 2), out_sem=(SLOTS,), send_sem=(18, SLOTS), recv_sem=(18, SLOTS),
+        weight_sem=(2, 2), fetch_sem=(15,), send_one=(16,), recv_one=(16,), send_two=(16,),
+        recv_two=(16,),
+    )
+    names = list(far) + list(near) + out_names + list(buffers) + list(semaphores)
+    return pl.pallas_call(
+        functools.partial(tail_kernel, names, len(shapes)),
+        in_specs=[hbm] * len(far) + [vmem] * len(near),
+        out_specs=[vmem] + [hbm] * len(shapes),
+        out_shape=[jax.ShapeDtypeStruct((rows, width), F32)]
+        + [jax.ShapeDtypeStruct(shape, F32) for shape in shapes],
+        scratch_shapes=[pltpu.VMEM(*item) for item in buffers.values()]
+        + [pltpu.SemaphoreType.DMA(item) for item in semaphores.values()],
+        compiler_params=pltpu.CompilerParams(
+            collective_id=1, has_side_effects=True, vmem_limit_bytes=60 << 20
+        ),
+    )(*far.values(), *near.values())
 
 
 def normalize(values, gain_vec):
@@ -1155,27 +1475,105 @@
         local_params,
     )
     normed = normed.reshape(flat_shape)
+    mixed = mixed.reshape(flat_shape)
+    grad_b_down = jnp.sum(local_cotan.astype(F32), axis=(0, 1))
+    grad_first = grad_first.reshape(utter_count, frame_count, model_width)
+    glob_cotan = jnp.where(
+        valid[:, :, None], cotan_global.astype(jnp.float32) + grad_first, 0.0
+    )
+    glob_cotan = glob_cotan.reshape(row_count, model_width)
+    outputs = (global_rows.reshape(utter_count, frame_count, model_width), local_rows)
+
+    if lax.axis_size("seq") == 16 and lax.axis_size("utt") == 2:
+        glob_middle, glob_middle_norm, pre_active, active = glob_kept
+        far = dict(
+            l_up=grad_w_up.reshape(8, 2, -1, grad_w_up.shape[1]),
+            l_down=grad_w_down.reshape(8, 2, -1, grad_w_down.shape[1]),
+            g_w_up=glob_w_up,
+            g_w_down=glob_w_down,
+            g_w_o=glob_w_output,
+            g_w_q=glob_w_query,
+            g_w_k=glob_w_key,
+            g_w_v=glob_w_value,
+            saved=saved,
+            l_normed=normed,
+            l_mixed=mixed,
+            l_dq=grad_q.reshape(flat_shape),
+            l_dk=grad_k.reshape(flat_shape),
+            l_dv=grad_v.reshape(flat_shape),
+            l_dattn=grad_attn.reshape(flat_shape),
+            rest=grad_rest,
+            g_act=active,
+            g_mixed=glob_mixed,
+            g_normed=glob_normed,
+        )
+        near = dict(
+            u=pre_active,
+            dout=glob_cotan,
+            mid=glob_middle,
+            hn=glob_middle_norm,
+            x=frames.reshape(row_count, model_width),
+            n1=glob_norm_one.reshape(1, -1),
+            n2=glob_norm_two.reshape(1, -1),
+            log_total=log_total,
+            codes=jnp.broadcast_to(code_rows[:, None, :], (CB, 8, row_count)),
+            l_dn1=grad_n1,
+            l_dn2=grad_n2,
+            l_db1=grad_b_up,
+            l_db2=grad_b_down.reshape(1, -1),
+        )
+        grad_inputs, *sums = finish_on_slice(far, near)
+        wide = dict(zip("12qkvot76pabc", sums[:-1]))
+        half = lax.axis_index("seq") % 2
+        rest = sums[-1]
+
+        def piece(row):
+            return jnp.where(half == 0, rest[row, : LANES // 2], rest[row, LANES // 2 : LANES])
+
+        def piece_wide(row):
+            return rest[row : row + 2, :LANES].reshape(-1)
+
+        return outputs + (
+            grad_inputs.reshape(utter_count, frame_count, model_width),
+            wide["t"],
+            piece(0),
+            wide["a"],
+            wide["b"],
+            wide["c"],
+            wide["p"],
+            piece(1),
+            wide["6"],
+            piece_wide(3),
+            wide["7"],
+            piece(2),
+            piece(5),
+            wide["q"],
+            wide["k"],
+            wide["v"],
+            wide["o"],
+            piece(6),
+            wide["1"],
+            piece_wide(8),
+            wide["2"],
+            piece(7),
+        )
+
     local_grads = (
         grad_n1[0],
         weight_grad(normed, grad_q.reshape(flat_shape)),
         weight_grad(normed, grad_k.reshape(flat_shape)),
         weight_grad(normed, grad_v.reshape(flat_shape)),
-        weight_grad(mixed.reshape(flat_shape), grad_attn.reshape(flat_shape)),
+        weight_grad(mixed, grad_attn.reshape(flat_shape)),
         grad_n2[0],
         grad_w_up,
         grad_b_up[0],
         grad_w_down,
-        jnp.sum(local_cotan.astype(F32), axis=(0, 1)),
+        grad_b_down,
     )
     picked = code_rows[:, None, :] == jnp.arange(VOCAB, dtype=jnp.int32)[None, :, None]
     grad_tab = jnp.einsum(
         "cvn,cnd->cvd", picked.astype(LOW), grad_rest, preferred_element_type=F32
     ).reshape(CB * VOCAB, model_width)
-    grad_first = grad_first.reshape(utter_count, frame_count, model_width)
-    glob_cotan = jnp.where(
-        valid[:, :, None], cotan_global.astype(jnp.float32) + grad_first, 0.0
-    )
-    glob_cotan = glob_cotan.reshape(row_count, model_width)
 
     def global_back(grad_mixed):
         grads = global_attend_back(
@@ -1187,11 +1585,7 @@
         global_in, glob_normed, glob_mixed, glob_kept, glob_params, glob_cotan, global_back
     )
     reduced = reduce_all((grad_tab,) + glob_grads + local_grads)
-    return (
-        global_rows.reshape(utter_count, frame_count, model_width),
-        local_rows,
-        grad_inputs.reshape(utter_count, frame_count, model_width),
-    ) + reduced
+    return outputs + (grad_inputs.reshape(utter_count, frame_count, model_width),) + reduced
 
 
 def solution(mesh):

time: 510 us -> 442 us (0.87); the launches traced: 500 us -> 442 us
  matrix products: 59.4 us -> 12.1 us
  Pallas kernels: 398 us -> 389 us
    dot_general x17 -> x0, matrix products: 51.9 us -> none  [the longest x10 27.8 us: weight_grad(): lax.dot_general(left_side, gradient, (((0,), (0,)), ((), ())), preferred_...]
    pallas_call x2 -> x1, Pallas kernels: 296 us -> 288 us  [finish_on_slice(): pl.pallas_call(functools.partial(tail_kernel, names, len(shapes)), in_spe...]
    reduce_sum x3 -> x1, other arithmetic: 6.81 us -> 1.22 us  [on_device(): grad_b_down = jnp.sum(local_cotan.astype(F32), axis=(0, 1))]
    unnamed x99 -> x78, local copies, waits for them, and re-layouts: 14 us -> 18.7 us
where the time goes in v4:
time: 442 us
  Pallas kernels  389 us (88%)
  local copies, waits for them, and re-layouts  27.6 us (6%)
  matrix products  12.1 us (3%)
  other arithmetic  11.7 us (3%)
    pallas_call x1, Pallas kernels, finish_on_slice(): pl.pallas_call(functools.partial(tail_kernel, names, len(shapes)), in_spe...  288 us
    pallas_call x1, Pallas kernels, local_ffn(): pl.pallas_call(ffn_kernel, grid=(wide // step,), in_specs=[whole, whole,...  35.4 us
    pallas_call x1, Pallas kernels, global_attend(): pl.pallas_call(functools.partial(attend_kernel, count), in_specs=[vmem] *...  33.5 us
    unnamed x78, local copies, waits for them, and re-layouts  18.7 us
    pallas_call x1, Pallas kernels, local_back(): pl.pallas_call(back_kernel, grid=(frames // step,), in_specs=[rows] * 7 +...  17.8 us
    pallas_call x1, Pallas kernels, local_front(): pl.pallas_call(front_kernel, grid=(frames // step,), in_specs=[rows] + [w...  15 us
    dot_general x3, matrix products, project(): return jnp.dot(left_side, weight, preferred_element_type=jnp.float32)  12.1 us

profile of v4, /device:TPU:0, one launch (start us, length us, event | category | flops | bytes accessed | tf_op | source)
XLA Modules:
  0.0 441.6 jit_solution(11882934065983687919)
XLA Ops:
  0.7 0.7 convert_element_type.25
  1.4 1.6 copy-done
  3.0 1.6 copy-done.1
  4.5 0.9 copy-done.2
  5.5 0.7 copy-done.7
  6.2 33.5 %shard_map.442 = (bf16[128,1024]{1,0:T(8,128)(2,1)S(1)}, bf16[2,64,1024]{2,1,0:T(8,128)(2,1)S(1)}, bf16[16,208,128]{2,1,0:T(8,128)(2,1)S(1)}, f32[16,8,128]{2,1,0:T(8,128)S(1)}) custom-call(bf16[2,64,1024]{2,1,0:T(8,128)(2,1)S(1)} %copy-done.2, bf16[2,16,128]{2,1,0:T(8,128)(2,1)S(1)} %broadcast_in_dim.80.mask_ref, f32[1,1024]{1,0:T(1,128)S(1)} %bitcast.67, ...), custom_call_target="tpu_custom_call" | custom-call | tf_op jit(solution)/shard_map/pallas_call | solution.py:484
  39.7 0.0 copy-start.6
  39.7 0.0 copy-start.27
  39.8 0.5 multiply_reduce_fusion
  40.3 0.1 copy-done.27
  40.5 0.1 multiply_convert_fusion.refs_22_
  40.6 0.0 copy-start.13
  40.6 6.7 %fusion.7 = (bf16[128,4096]{1,0:T(8,128)(2,1)S(1)}, f32[128,4096]{1,0:T(8,128)}) fusion(f32[4096]{0:T(1024)S(1)} %copy-done.30, bf16[128,1024]{1,0:T(8,128)(2,1)S(1)} %multiply_convert_fusion.refs_22_, bf16[1024,4096]{1,0:T(8,128)(2,1)} %refs_2_.1), kind=kOutput, calls=%fused_computation.10 | convolution fusion | flops 1078984704 | bytes 11812864 | tf_op jit(solution)/shard_map/dot_general | solution.py:1318
  47.4 0.1 broadcast_compare_fusion
  47.5 0.1 lt.51
  47.6 4.8 %fusion.10 = bf16[128,1024]{1,0:T(8,128)(2,1)S(1)} fusion(f32[128,1024]{1,0:T(8,128)S(1)} %get-tuple-element.113.refs_21_, bf16[128,4096]{1,0:T(8,128)(2,1)S(1)} %get-tuple-element.114.refs_16_, bf16[4096,1024]{1,0:T(8,128)(2,1)} %refs_3_.1, f32[1024]{0:T(1024)S(1)} %copy-done.29, pred[128]{0:T(512)(128)(4,1)S(1)} %lt.51), kind=kOutput, calls=%fused_computation.16 | convolution fusion | flops 1074266112 | bytes 10227840 | tf_op jit(solution)/shard_map/dot_general | solution.py:1318
  52.4 0.0 copy-start.12
  52.5 0.1 reshape.286
  52.6 0.1 fusion.12
  52.6 6.4 %gather_fusion = bf16[384,1024]{1,0:T(8,128)(2,1)S(1)} fusion(bf16[3072,1024]{1,0:T(8,128)(2,1)} %param.31, s32[1024]{0:T(1024)S(1)} %pad_clamp_fusion), kind=kCustom, calls=%fused_computation | custom fusion | bytes 1574400 | tf_op jit(solution)/shard_map/gather | solution.py:1447
  59.1 0.3 copy.54
  59.4 1.5 pad_maximum_fusion
  61.0 15.0 %shard_map.443 = (bf16[4,128,1024]{2,1,0:T(8,128)(2,1)}, bf16[4,128,1024]{2,1,0:T(8,128)(2,1)}, bf16[4,128,1024]{2,1,0:T(8,128)(2,1)}, bf16[4,128,1024]{2,1,0:T(...) custom-call(bf16[4,128,1024]{2,1,0:T(8,128)(2,1)} %get-tuple-element, ...), custom_call_target="tpu_custom_call" | custom-call | tf_op jit(solution)/shard_map/pallas_call | solution.py:129
  76.0 1.2 bitcast_select_fusion.1.dout_ref
  77.2 35.4 %shard_map.444 = (bf16[512,1024]{1,0:T(8,128)(2,1)}, f32[512,1024]{1,0:T(8,128)}, bf16[1024,4096]{1,0:T(8,128)(2,1)}, bf16[4096,1024]{1,0:T(8,128)(2,1)}, f32[1,4096]{1,0:T(1,128)}) custom-call(bf16[512,1024]{1,0:T(8,128)(2,1)} %bitcast.83, bf16[512,1024]{1,0:T(8,128)(2,1)} %bitcast_select_fusion.1.dout_ref, f32[512,1024]{1,0:T(8,128)} %bitcast.70, ...), custom_call_target="tpu_custom_call" | custom-call | tf_op jit(solution)/shard_map/pallas_call | solution.py:188
  112.6 3.1 fusion.11
  115.6 17.8 %shard_map.445 = (bf16[4,128,1024]{2,1,0:T(8,128)(2,1)}, bf16[4,128,1024]{2,1,0:T(8,128)(2,1)}, bf16[4,128,1024]{2,1,0:T(8,128)(2,1)}, bf16[4,128,1024]{2,1,0:T(...) custom-call(bf16[4,128,1024]{2,1,0:T(8,128)(2,1)} %get-tuple-element.1, ...), custom_call_target="tpu_custom_call" | custom-call | tf_op jit(solution)/shard_map/pallas_call | solution.py:284
  133.4 1.9 add_select_fusion
  135.3 0.1 broadcast_in_dim.94
  135.4 0.6 broadcast_in_dim.95.refs_27_
  136.0 1.2 convert_reduce_fusion
  137.3 287.7 %shard_map.446 = (f32[128,1024]{1,0:T(8,128)}, f32[64,4096]{1,0:T(8,128)}, f32[256,1024]{1,0:T(8,128)}, f32[64,1024]{1,0:T(8,128)}, f32[64,1024]{1,0:T(8,128)}, ...) custom-call(bf16[8,2,64,4096]{3,2,1,0:T(8,128)(2,1)} %bitcast.68, ...), custom_call_target="tpu_custom_call" | custom-call | tf_op jit(solution)/shard_map/pallas_call | solution.py:1293
  425.0 1.7 fusion.18
  426.7 1.2 slice_bitcast_fusion
  428.0 1.9 copy.74
  429.9 2.2 copy.75
  432.1 0.7 copy.76
  432.8 0.7 copy.77
  433.5 0.7 copy.78
  434.2 0.7 copy.79
  434.9 1.0 copy.80
  435.9 1.0 copy.81
  436.9 0.7 copy.82
  437.6 0.7 copy.83
  438.3 0.7 copy.84
  439.0 0.7 copy.85
  439.7 1.0 copy.86
  440.7 1.0 copy.87
  (62 shorter events, 0.2 us)
Async XLA Ops:
  1.4 1.6 copy-start
  2.9 1.6 copy-start.1
  4.5 0.9 copy-start.2
  5.5 0.7 copy-start.7
  6.2 33.6 %copy-start.9 = (bf16[1024,1024]{1,0:T(8,128)(2,1)S(1)}, bf16[1024,1024]{1,0:T(8,128)(2,1)}, u32[]{:S(2)}) copy-start(bf16[1024,1024]{1,0:T(8,128)(2,1)} %refs_4_.1) | copy-start | bytes 6291460
  39.7 7.7 %copy-start.3 = (bf16[2,64,1024]{2,1,0:T(8,128)(2,1)}, bf16[2,64,1024]{2,1,0:T(8,128)(2,1)S(1)}, u32[]{:S(2)}) copy-start(bf16[2,64,1024]{2,1,0:T(8,128)(2,1)S(1)} %get-tuple-element.64) | copy-start | bytes 786436
  39.7 7.6 %copy-start.4 = (bf16[16,208,128]{2,1,0:T(8,128)(2,1)}, bf16[16,208,128]{2,1,0:T(8,128)(2,1)S(1)}, u32[]{:S(2)}) copy-start(bf16[16,208,128]{2,1,0:T(8,128)(2,1)S(1)} %get-tuple-element.70.refs_8_) | copy-start | bytes 2555908
  39.7 7.6 %copy-start.5 = (bf16[128,1024]{1,0:T(8,128)(2,1)}, bf16[128,1024]{1,0:T(8,128)(2,1)S(1)}, u32[]{:S(2)}) copy-start(bf16[128,1024]{1,0:T(8,128)(2,1)S(1)} %get-tuple-element.83.refs_18_) | copy-start | bytes 786436
  39.7 7.6 %copy-start.6 = (f32[16,8,128]{2,1,0:T(8,128)}, f32[16,8,128]{2,1,0:T(8,128)S(1)}, u32[]{:S(2)}) copy-start(f32[16,8,128]{2,1,0:T(8,128)S(1)} %get-tuple-element.85.refs_26_) | copy-start | bytes 196612
  39.7 0.7 copy-start.27
  39.8 0.8 copy-start.30
  40.3 7.3 %copy-start.8 = (f32[128,1024]{1,0:T(8,128)}, f32[128,1024]{1,0:T(8,128)S(1)}, u32[]{:S(2)}) copy-start(f32[128,1024]{1,0:T(8,128)S(1)} %get-tuple-element.113.refs_21_) | copy-start | bytes 1572868
  40.6 6.8 %copy-start.13 = (bf16[128,1024]{1,0:T(8,128)(2,1)}, bf16[128,1024]{1,0:T(8,128)(2,1)S(1)}, u32[]{:S(2)}) copy-start(bf16[128,1024]{1,0:T(8,128)(2,1)S(1)} %multiply_convert_fusion.refs_22_) | copy-start | bytes 786436
  40.6 6.8 %copy-start.31 = (s32[2]{0:T(128)S(1)}, s32[2]{0:T(128)}, u32[]{:S(2)}) copy-start(s32[2]{0:T(128)} %param.29) | copy-start | bytes 28
  40.6 7.0 %copy-start.29 = (f32[1024]{0:T(1024)S(1)}, f32[1024]{0:T(1024)}, u32[]{:S(2)}) copy-start(f32[1024]{0:T(1024)} %param.41) | copy-start | bytes 12292
  47.4 5.1 %copy-start.10 = (bf16[128,4096]{1,0:T(8,128)(2,1)}, bf16[128,4096]{1,0:T(8,128)(2,1)S(1)}, u32[]{:S(2)}) copy-start(bf16[128,4096]{1,0:T(8,128)(2,1)S(1)} %get-tuple-element.114.refs_16_) | copy-start | bytes 3145732
  47.6 4.9 %copy-start.28 = (s32[2,64,3]{1,0,2:T(2,128)S(1)}, s32[2,64,3]{1,0,2:T(2,128)}, u32[]{:S(2)}) copy-start(s32[2,64,3]{1,0,2:T(2,128)} %param.28) | copy-start | bytes 4612
  52.4 7.0 %copy-start.12 = (bf16[128,1024]{1,0:T(8,128)(2,1)}, bf16[128,1024]{1,0:T(8,128)(2,1)S(1)}, u32[]{:S(2)}) copy-start(bf16[128,1024]{1,0:T(8,128)(2,1)S(1)} %fusion.10) | copy-start | bytes 786436
  52.6 6.5 %copy-start.11 = (bf16[2,64,4,1024]{3,2,1,0:T(4,128)(2,1)S(1)}, bf16[2,64,4,1024]{3,2,1,0:T(4,128)(2,1)}, u32[]{:S(2)}) copy-start(bf16[2,64,4,1024]{3,2,1,0:T(4,128)(2,1)} %param.53) | copy-start | bytes 3145732
  115.6 17.8 %copy-start.18 = (bf16[2,64,1024]{2,1,0:T(8,128)(2,1)S(1)}, bf16[2,64,1024]{2,1,0:T(8,128)(2,1)}, u32[]{:S(2)}) copy-start(bf16[2,64,1024]{2,1,0:T(8,128)(2,1)} %param.52) | copy-start | bytes 786436
  425.0 7.1 %copy-start.26 = (f32[64,1024]{1,0:T(8,128)S(1)}, f32[64,1024]{1,0:T(8,128)}, u32[]{:S(2)}) copy-start(f32[64,1024]{1,0:T(8,128)} %get-tuple-element.147) | copy-start | bytes 786436
  425.0 7.8 %copy-start.25 = (f32[64,1024]{1,0:T(8,128)S(1)}, f32[64,1024]{1,0:T(8,128)}, u32[]{:S(2)}) copy-start(f32[64,1024]{1,0:T(8,128)} %get-tuple-element.148) | copy-start | bytes 786436
  425.0 8.5 %copy-start.24 = (f32[64,1024]{1,0:T(8,128)S(1)}, f32[64,1024]{1,0:T(8,128)}, u32[]{:S(2)}) copy-start(f32[64,1024]{1,0:T(8,128)} %get-tuple-element.149) | copy-start | bytes 786436
  428.0 6.2 %copy-start.23 = (f32[64,1024]{1,0:T(8,128)S(1)}, f32[64,1024]{1,0:T(8,128)}, u32[]{:S(2)}) copy-start(f32[64,1024]{1,0:T(8,128)} %get-tuple-element.150) | copy-start | bytes 786436
  429.9 5.0 %copy-start.17 = (f32[64,4096]{1,0:T(8,128)S(1)}, f32[64,4096]{1,0:T(8,128)}, u32[]{:S(2)}) copy-start(f32[64,4096]{1,0:T(8,128)} %get-tuple-element.152) | copy-start | bytes 3145732
  432.1 3.8 copy-start.16
  434.9 2.0 copy-start.22
  434.9 2.7 copy-start.21
  435.9 2.4 copy-start.20
  435.9 3.1 copy-start.19
  435.9 3.8 copy-start.15
  436.9 3.8 copy-start.14

commit v5 on v4

--- a/solution.py
+++ b/solution.py
@@ -663,6 +663,7 @@
 DEEP = 8
 SROWS = 64
 SCOLS = 512
+ACOLS = 384
 DRAIN = 8
 PLAN = (
     (0, 8, 8), (8, 8, 2), (16, 2, 2), (18, 2, 2), (20, 2, 2), (22, 2, 2), (24, 6, 2),
@@ -671,8 +672,9 @@
 SLABS = 55
 LOADED = 16
 AT_BACK = 8
-AT_ATTEND = 10
-AT_LANDED = 20
+AT_ATTEND = 15
+AT_RETURN = 23
+AT_LANDED = 40
 
 
 def tail_kernel(names, out_count, *refs):
@@ -776,6 +778,12 @@
     def utt_copy_b2(slot, deep):
         return send(5, slot, r.line_b.at[deep, pos], r.recv_yb2.at[slot], utt_id)
 
+    def col_copy_c(slot, deep):
+        return send(24, slot, r.line_c.at[deep, pos, 1 - col], r.recv_xc.at[slot], col_id)
+
+    def utt_copy_c(slot):
+        return send(25, slot, r.sum_c.at[slot], r.recv_yc.at[slot], utt_id)
+
     def line_right(kind, slot, deep, step, source, target):
         dest = jnp.minimum(4 - step + pos, 3)
         return send(kind + step - 1, slot, source.at[deep, dest], target.at[slot, step - 1], right_id)
@@ -820,6 +828,7 @@
 
     line_a = (r.sum_a, r.right_a, r.left_a, 6)
     line_bb = (r.line_b, r.right_b, r.left_b, 12)
+    line_cc = (r.line_c, r.right_c, r.left_c, 18)
 
     def advance(tick):
         def stage(offset):
@@ -829,9 +838,10 @@
                 lax.rem(slab + SLOTS * 4, SLOTS),
                 lax.rem(slab + DEEP, DEEP),
                 pl.when((slab >= 0) & (slab < SLABS)),
+                pl.when((slab >= 0) & (slab < SLABS - 1)),
             )
 
-        slab, slot, _, guard = stage(0)
+        slab, slot, _, guard, _ = stage(0)
         load_start(slab + 1)
 
         @pl.when(slab < LOADED)
@@ -842,7 +852,7 @@
         def _():
             core_copy(slot).start()
 
-        _, slot1, _, guard = stage(1)
+        _, slot1, deep1, guard, most = stage(1)
 
         @guard
         def _():
@@ -853,15 +863,25 @@
                         slot1, 2 * line + side
                     ].astype(F32)
                     both = both.astype(LOW)
-                    r.half_a[slot1, side, line] = both[:32]
+                    r.half_a[slot1, side, line] = both[:32, :ACOLS]
+                    r.line_c[deep1, line, side] = both[:32, ACOLS:]
                     r.half_b[slot1, 0, side, line] = both[32:48]
                     r.half_b[slot1, 1, side, line] = both[48:]
+            line_start(slot1, deep1, 1, *line_cc)
+
+        @most
+        def _():
             col_copy_a(slot1).start()
             utt_copy_b(slot1).start()
 
-        _, slot2, deep2, guard = stage(2)
+        _, slot2, deep2, guard, most = stage(2)
 
         @guard
+        def _():
+            line_finish(slot2, deep2, 1, *line_cc)
+            line_start(slot2, deep2, 2, *line_cc)
+
+        @most
         def _():
             col_copy_a(slot2).wait()
             r.sum_a[deep2] = (
@@ -874,9 +894,14 @@
             ).astype(LOW)
             col_copy_b(slot2).start()
 
-        _, slot3, deep3, guard = stage(3)
+        _, slot3, deep3, guard, most = stage(3)
 
         @guard
+        def _():
+            line_finish(slot3, deep3, 2, *line_cc)
+            line_start(slot3, deep3, 3, *line_cc)
+
+        @most
         def _():
             line_finish(slot3, deep3, 1, *line_a)
             line_start(slot3, deep3, 2, *line_a)
@@ -886,51 +911,72 @@
             ).astype(LOW)
             line_start(slot3, deep3, 1, *line_bb)
 
-        _, slot4, deep4, guard = stage(4)
+        _, slot4, deep4, guard, most = stage(4)
 
         @guard
+        def _():
+            line_finish(slot4, deep4, 3, *line_cc)
+            col_copy_c(slot4, deep4).start()
+
+        @most
         def _():
             line_finish(slot4, deep4, 2, *line_a)
             line_start(slot4, deep4, 3, *line_a)
             line_finish(slot4, deep4, 1, *line_bb)
             line_start(slot4, deep4, 2, *line_bb)
 
-        _, slot5, deep5, guard = stage(5)
+        _, slot5, deep5, guard, most = stage(5)
 
         @guard
+        def _():
+            col_copy_c(slot5, deep5).wait()
+            r.sum_c[slot5] = (
+                r.line_c[deep5, pos, col].astype(F32) + r.recv_xc[slot5].astype(F32)
+            ).astype(LOW)
+            utt_copy_c(slot5).start()
+
+        @most
         def _():
             line_finish(slot5, deep5, 3, *line_a)
             utt_copy_a(slot5, deep5).start()
             line_finish(slot5, deep5, 2, *line_bb)
             line_start(slot5, deep5, 3, *line_bb)
 
-        _, slot6, deep6, guard = stage(6)
+        _, slot6, deep6, guard, most = stage(6)
 
         @guard
         def _():
+            utt_copy_c(slot6).wait()
+            r.staged[slot6, 0:32, ACOLS:] = r.sum_c[slot6].astype(F32) + r.recv_yc[slot6].astype(F32)
+
+        @most
+        def _():
             utt_copy_a(slot6, deep6).wait()
-            r.staged[slot6, 0:32] = r.sum_a[deep6, pos].astype(F32) + r.recv_ya[slot6].astype(F32)
+            r.staged[slot6, 0:32, :ACOLS] = r.sum_a[deep6, pos].astype(F32) + r.recv_ya[
+                slot6
+            ].astype(F32)
             line_finish(slot6, deep6, 3, *line_bb)
             utt_copy_b2(slot6, deep6).start()
 
-        slab7, slot7, deep7, guard = stage(7)
-
-        @guard
+        slab7, slot7, deep7, guard, most = stage(7)
+
+        @most
         def _():
             utt_copy_b2(slot7, deep7).wait()
             mine = r.line_b[deep7, pos].astype(F32)
             theirs = r.recv_yb2[slot7].astype(F32)
             r.staged[slot7, 32:48] = jnp.where(utt == 0, mine, theirs)
             r.staged[slot7, 48:64] = jnp.where(utt == 0, theirs, mine)
-            for ref, spec in zip(outs, PLAN):
-
-                @pl.when((slab7 >= spec[0]) & (slab7 < spec[0] + spec[1]))
-                def _():
-                    pltpu.make_async_copy(
-                        r.staged.at[slot7], window(ref, spec, slab7, ()), r.out_sem.at[slot7]
-                    ).start()
-
-        _, slot8, _, guard = stage(8)
+
+        for ref, spec in zip(outs, PLAN):
+
+            @pl.when((slab7 >= spec[0]) & (slab7 < spec[0] + spec[1]))
+            def _():
+                pltpu.make_async_copy(
+                    r.staged.at[slot7], window(ref, spec, slab7, ()), r.out_sem.at[slot7]
+                ).start()
+
+        _, slot8, _, guard, _ = stage(8)
 
         @guard
         def _():
@@ -1019,7 +1065,7 @@
                     first = 256 * dest + LANES * index
                     rows.append(r.l_db1[:, first : first + LANES])
                 rows.append(jnp.zeros((6, LANES), F32))
-                r.part[slot, dest % 2, dest // 2, 0:16, 0:LANES] = jnp.concatenate(
+                r.part[slot, dest % 2, dest // 2, 0:16, ACOLS:] = jnp.concatenate(
                     rows, axis=0
                 ).astype(LOW)
 
@@ -1097,8 +1143,13 @@
             dattn = dmid.astype(LOW)
             r.g_g[0] = dattn
             r.dmix[...] = mul_t(dattn, r.square[0]).astype(LOW).reshape(r.dmix.shape)
-            others(lambda other: hand_out(other).start())
             r.grads[seq] = r.dmix[own_utt, :, own_cols]
+
+        @pl.when((tick >= AT_BACK) & (tick < AT_BACK + 5))
+        def _():
+            @pl.loop(0, 3)
+            def _(index):
+                hand_out(lax.rem(seq + 3 * (tick - AT_BACK) + index + 1, count)).start()
 
         @at(AT_BACK + 1)
         def _():
@@ -1127,8 +1178,9 @@
             def _():
                 @pl.loop(0, 2)
                 def _(index):
-                    block = 4 * group + 2 * (tick - begin) + index
-                    attend_back_block(r, group, below, here, block)
+                    attend_back_block(
+                        r, group, below, here, 4 * group + 2 * (tick - begin) + index
+                    )
 
             @at(begin + 1)
             def _():
@@ -1137,13 +1189,13 @@
                     r.pieces[block, 1] = r.dk_acc[rows].astype(LOW)
                     r.pieces[block, 2] = r.dv_acc[rows].astype(LOW)
 
-                    @pl.when(block != seq)
-                    def _():
-                        hand_back(block).start()
-
-                    @pl.when(block == seq)
-                    def _():
-                        r.landed[:, own_utt, :, own_cols] = r.pieces[block]
+        @at(AT_RETURN)
+        def _():
+            r.landed[:, own_utt, :, own_cols] = r.pieces[seq]
+
+        @pl.when((tick >= AT_RETURN) & (tick < AT_RETURN + 15))
+        def _():
+            hand_back(lax.rem(seq + tick - AT_RETURN + 1, count)).start()
 
         @at(AT_LANDED)
         def _():
@@ -1159,9 +1211,8 @@
 
         @at(AT_LANDED + 1)
         def _():
-            for copy in fetch(1, 2, 3, 11, 12, 13, 14):
+            for copy in fetch(1, 2, 3):
                 copy.wait()
-            r.l_x_t[...] = r.l_x[1].T
             r.dhn[...] = mul_t(r.g_g[1], r.square[1])
 
         @at(AT_LANDED + 2)
@@ -1175,15 +1226,27 @@
             r.dn1[...] = jnp.sum(gain, axis=0, keepdims=True)
             r.dx[...] = dx + r.dmid[...]
 
-        @at(AT_LANDED + 4)
-        def _():
-            r.act_t[...] = r.act_buf[...].T
-
-        @at(AT_LANDED + 5)
+        @at(21)
+        def _():
+            r.l_x_t[...] = r.l_x[1].T
+
+        @at(22)
+        def _():
+            for copy in fetch(11, 12, 13, 14):
+                copy.wait()
+
+        @pl.when((tick >= 24) & (tick < 28))
+        def _():
+            cols = pl.ds(pl.multiple_of((tick - 24) * 1024, 1024), 1024)
+            r.act_t[cols] = r.act_buf[:, cols].T
+
+        @at(29)
         def _():
             r.g_hn_t[...] = r.hn[...].T
-            r.g_x_t[0] = r.g_x[0].T
-            r.g_x_t[1] = r.g_x[1].T
+
+        @at(31, 32)
+        def _():
+            r.g_x_t[tick - 31] = r.g_x[tick - 31].T
 
     pl.semaphore_wait(barrier, count)
 
@@ -1239,20 +1302,26 @@
     buffers = dict(
         part=((SLOTS, 2, 8, 64, SCOLS), LOW),
         recv_c=((SLOTS, 8, 64, SCOLS), LOW),
-        half_a=((SLOTS, 2, 4, 32, SCOLS), LOW),
+        half_a=((SLOTS, 2, 4, 32, ACOLS), LOW),
         half_b=((SLOTS, 2, 2, 4, 16, SCOLS), LOW),
-        recv_xa=((SLOTS, 4, 32, SCOLS), LOW),
+        recv_xa=((SLOTS, 4, 32, ACOLS), LOW),
         recv_yb=((SLOTS, 2, 4, 16, SCOLS), LOW),
-        sum_a=((DEEP, 4, 32, SCOLS), LOW),
+        sum_a=((DEEP, 4, 32, ACOLS), LOW),
         sum_b=((SLOTS, 2, 4, 16, SCOLS), LOW),
         recv_xb=((SLOTS, 4, 16, SCOLS), LOW),
         line_b=((DEEP, 4, 16, SCOLS), LOW),
-        right_a=((SLOTS, 3, 32, SCOLS), LOW),
-        left_a=((SLOTS, 3, 32, SCOLS), LOW),
+        right_a=((SLOTS, 3, 32, ACOLS), LOW),
+        left_a=((SLOTS, 3, 32, ACOLS), LOW),
         right_b=((SLOTS, 3, 16, SCOLS), LOW),
         left_b=((SLOTS, 3, 16, SCOLS), LOW),
-        recv_ya=((SLOTS, 32, SCOLS), LOW),
+        recv_ya=((SLOTS, 32, ACOLS), LOW),
         recv_yb2=((SLOTS, 16, SCOLS), LOW),
+        line_c=((DEEP, 4, 2, 32, LANES), LOW),
+        right_c=((SLOTS, 3, 2, 32, LANES), LOW),
+        left_c=((SLOTS, 3, 2, 32, LANES), LOW),
+        recv_xc=((SLOTS, 32, LANES), LOW),
+        sum_c=((SLOTS, 32, LANES), LOW),
+        recv_yc=((SLOTS, 32, LANES), LOW),
         staged=((SLOTS, 64, SCOLS), F32),
         up_buf=((2, width, SCOLS), LOW),
         down_buf=((2, SCOLS, width), LOW),
@@ -1285,7 +1354,7 @@
         k_t=((LANES, 16 * HD), LOW),
     )
     semaphores = dict(
-        load_sem=(SLOTS, 2), out_sem=(SLOTS,), send_sem=(18, SLOTS), recv_sem=(18, SLOTS),
+        load_sem=(SLOTS, 2), out_sem=(SLOTS,), send_sem=(26, SLOTS), recv_sem=(26, SLOTS),
         weight_sem=(2, 2), fetch_sem=(15,), send_one=(16,), recv_one=(16,), send_two=(16,),
         recv_two=(16,),
     )
@@ -1528,10 +1597,10 @@
         rest = sums[-1]
 
         def piece(row):
-            return jnp.where(half == 0, rest[row, : LANES // 2], rest[row, LANES // 2 : LANES])
+            return jnp.where(half == 0, rest[row, ACOLS : ACOLS + LANES // 2], rest[row, ACOLS + LANES // 2 :])
 
         def piece_wide(row):
-            return rest[row : row + 2, :LANES].reshape(-1)
+            return rest[row : row + 2, ACOLS:].reshape(-1)
 
         return outputs + (
             grad_inputs.reshape(utter_count, frame_count, model_width),

time: 442 us -> 410 us (0.928)
  Pallas kernels: 389 us -> 357 us
    pallas_call x1, Pallas kernels: 288 us -> 256 us  [finish_on_slice(): pl.pallas_call(functools.partial(tail_kernel, names, len(shapes)), in_spe...]
where the time goes in v5:
time: 410 us
  Pallas kernels  357 us (87%)
  local copies, waits for them, and re-layouts  27.6 us (7%)
  matrix products  12.1 us (3%)
  other arithmetic  11.7 us (3%)
    pallas_call x1, Pallas kernels, finish_on_slice(): pl.pallas_call(functools.partial(tail_kernel, names, len(shapes)), in_spe...  256 us
    pallas_call x1, Pallas kernels, local_ffn(): pl.pallas_call(ffn_kernel, grid=(wide // step,), in_specs=[whole, whole,...  35.4 us
    pallas_call x1, Pallas kernels, global_attend(): pl.pallas_call(functools.partial(attend_kernel, count), in_specs=[vmem] *...  33.5 us
    unnamed x78, local copies, waits for them, and re-layouts  18.7 us
    pallas_call x1, Pallas kernels, local_back(): pl.pallas_call(back_kernel, grid=(frames // step,), in_specs=[rows] * 7 +...  17.8 us
    pallas_call x1, Pallas kernels, local_front(): pl.pallas_call(front_kernel, grid=(frames // step,), in_specs=[rows] + [w...  15 us
    dot_general x3, matrix products, project(): return jnp.dot(left_side, weight, preferred_element_type=jnp.float32)  12.1 us

profile of v5, /device:TPU:0, one launch (start us, length us, event | category | flops | bytes accessed | tf_op | source)
XLA Modules:
  0.0 409.6 jit_solution(15034073868644446039)
XLA Ops:
  0.7 0.7 convert_element_type.25
  1.4 1.6 copy-done
  3.0 1.6 copy-done.1
  4.5 0.9 copy-done.2
  5.5 0.7 copy-done.7
  6.2 33.5 %shard_map.442 = (bf16[128,1024]{1,0:T(8,128)(2,1)S(1)}, bf16[2,64,1024]{2,1,0:T(8,128)(2,1)S(1)}, bf16[16,208,128]{2,1,0:T(8,128)(2,1)S(1)}, f32[16,8,128]{2,1,0:T(8,128)S(1)}) custom-call(bf16[2,64,1024]{2,1,0:T(8,128)(2,1)S(1)} %copy-done.2, bf16[2,16,128]{2,1,0:T(8,128)(2,1)S(1)} %broadcast_in_dim.80.mask_ref, f32[1,1024]{1,0:T(1,128)S(1)} %bitcast.67, ...), custom_call_target="tpu_custom_call" | custom-call | tf_op jit(solution)/shard_map/pallas_call | solution.py:484
  39.7 0.0 copy-start.3
  39.7 0.0 copy-start.5
  39.8 0.0 copy-start.30
  39.8 0.5 multiply_reduce_fusion
  40.3 0.1 copy-done.27
  40.5 0.1 multiply_convert_fusion.refs_22_
  40.6 6.7 %fusion.7 = (bf16[128,4096]{1,0:T(8,128)(2,1)S(1)}, f32[128,4096]{1,0:T(8,128)}) fusion(f32[4096]{0:T(1024)S(1)} %copy-done.30, bf16[128,1024]{1,0:T(8,128)(2,1)S(1)} %multiply_convert_fusion.refs_22_, bf16[1024,4096]{1,0:T(8,128)(2,1)} %refs_2_.1), kind=kOutput, calls=%fused_computation.10 | convolution fusion | flops 1078984704 | bytes 11812864 | tf_op jit(solution)/shard_map/dot_general | solution.py:1387
  47.4 0.1 broadcast_compare_fusion
  47.5 0.1 lt.51
  47.6 4.8 %fusion.10 = bf16[128,1024]{1,0:T(8,128)(2,1)S(1)} fusion(f32[128,1024]{1,0:T(8,128)S(1)} %get-tuple-element.113.refs_21_, bf16[128,4096]{1,0:T(8,128)(2,1)S(1)} %get-tuple-element.114.refs_16_, bf16[4096,1024]{1,0:T(8,128)(2,1)} %refs_3_.1, f32[1024]{0:T(1024)S(1)} %copy-done.29, pred[128]{0:T(512)(128)(4,1)S(1)} %lt.51), kind=kOutput, calls=%fused_computation.16 | convolution fusion | flops 1074266112 | bytes 10227840 | tf_op jit(solution)/shard_map/dot_general | solution.py:1387
  52.4 0.0 copy-start.12
  52.5 0.1 reshape.286
  52.6 0.1 fusion.12
  52.6 6.4 %gather_fusion = bf16[384,1024]{1,0:T(8,128)(2,1)S(1)} fusion(bf16[3072,1024]{1,0:T(8,128)(2,1)} %param.31, s32[1024]{0:T(1024)S(1)} %pad_clamp_fusion), kind=kCustom, calls=%fused_computation | custom fusion | bytes 1574400 | tf_op jit(solution)/shard_map/gather | solution.py:1516
  59.1 0.3 copy.54
  59.4 1.5 pad_maximum_fusion
  61.0 15.0 %shard_map.443 = (bf16[4,128,1024]{2,1,0:T(8,128)(2,1)}, bf16[4,128,1024]{2,1,0:T(8,128)(2,1)}, bf16[4,128,1024]{2,1,0:T(8,128)(2,1)}, bf16[4,128,1024]{2,1,0:T(...) custom-call(bf16[4,128,1024]{2,1,0:T(8,128)(2,1)} %get-tuple-element, ...), custom_call_target="tpu_custom_call" | custom-call | tf_op jit(solution)/shard_map/pallas_call | solution.py:129
  76.0 1.2 bitcast_select_fusion.1.dout_ref
  77.2 35.4 %shard_map.444 = (bf16[512,1024]{1,0:T(8,128)(2,1)}, f32[512,1024]{1,0:T(8,128)}, bf16[1024,4096]{1,0:T(8,128)(2,1)}, bf16[4096,1024]{1,0:T(8,128)(2,1)}, f32[1,4096]{1,0:T(1,128)}) custom-call(bf16[512,1024]{1,0:T(8,128)(2,1)} %bitcast.83, bf16[512,1024]{1,0:T(8,128)(2,1)} %bitcast_select_fusion.1.dout_ref, f32[512,1024]{1,0:T(8,128)} %bitcast.70, ...), custom_call_target="tpu_custom_call" | custom-call | tf_op jit(solution)/shard_map/pallas_call | solution.py:188
  112.6 3.1 fusion.11
  115.6 17.8 %shard_map.445 = (bf16[4,128,1024]{2,1,0:T(8,128)(2,1)}, bf16[4,128,1024]{2,1,0:T(8,128)(2,1)}, bf16[4,128,1024]{2,1,0:T(8,128)(2,1)}, bf16[4,128,1024]{2,1,0:T(...) custom-call(bf16[4,128,1024]{2,1,0:T(8,128)(2,1)} %get-tuple-element.1, ...), custom_call_target="tpu_custom_call" | custom-call | tf_op jit(solution)/shard_map/pallas_call | solution.py:284
  133.4 1.9 add_select_fusion
  135.3 0.1 broadcast_in_dim.94
  135.4 0.6 broadcast_in_dim.95.refs_27_
  136.0 1.2 convert_reduce_fusion
  137.3 255.7 %shard_map.446 = (f32[128,1024]{1,0:T(8,128)}, f32[64,4096]{1,0:T(8,128)}, f32[256,1024]{1,0:T(8,128)}, f32[64,1024]{1,0:T(8,128)}, f32[64,1024]{1,0:T(8,128)}, ...) custom-call(bf16[8,2,64,4096]{3,2,1,0:T(8,128)(2,1)} %bitcast.68, ...), custom_call_target="tpu_custom_call" | custom-call | tf_op jit(solution)/shard_map/pallas_call | solution.py:1362
  393.0 1.7 fusion.18
  394.7 1.3 slice_bitcast_fusion
  396.0 1.9 copy.74
  397.9 2.2 copy.75
  400.1 0.7 copy.76
  400.8 0.7 copy.77
  401.5 0.7 copy.78
  402.2 0.7 copy.79
  402.9 1.0 copy.80
  403.9 1.0 copy.81
  404.9 0.7 copy.82
  405.6 0.7 copy.83
  406.3 0.7 copy.84
  407.0 0.7 copy.85
  407.7 1.0 copy.86
  408.7 1.0 copy.87
  (62 shorter events, 0.2 us)
Async XLA Ops:
  1.4 1.6 copy-start
  2.9 1.6 copy-start.1
  4.5 0.9 copy-start.2
  5.5 0.7 copy-start.7
  6.2 33.6 %copy-start.9 = (bf16[1024,1024]{1,0:T(8,128)(2,1)S(1)}, bf16[1024,1024]{1,0:T(8,128)(2,1)}, u32[]{:S(2)}) copy-start(bf16[1024,1024]{1,0:T(8,128)(2,1)} %refs_4_.1) | copy-start | bytes 6291460
  39.7 7.7 %copy-start.3 = (bf16[2,64,1024]{2,1,0:T(8,128)(2,1)}, bf16[2,64,1024]{2,1,0:T(8,128)(2,1)S(1)}, u32[]{:S(2)}) copy-start(bf16[2,64,1024]{2,1,0:T(8,128)(2,1)S(1)} %get-tuple-element.64) | copy-start | bytes 786436
  39.7 7.6 %copy-start.4 = (bf16[16,208,128]{2,1,0:T(8,128)(2,1)}, bf16[16,208,128]{2,1,0:T(8,128)(2,1)S(1)}, u32[]{:S(2)}) copy-start(bf16[16,208,128]{2,1,0:T(8,128)(2,1)S(1)} %get-tuple-element.70.refs_8_) | copy-start | bytes 2555908
  39.7 7.6 %copy-start.5 = (bf16[128,1024]{1,0:T(8,128)(2,1)}, bf16[128,1024]{1,0:T(8,128)(2,1)S(1)}, u32[]{:S(2)}) copy-start(bf16[128,1024]{1,0:T(8,128)(2,1)S(1)} %get-tuple-element.83.refs_18_) | copy-start | bytes 786436
  39.7 7.6 %copy-start.6 = (f32[16,8,128]{2,1,0:T(8,128)}, f32[16,8,128]{2,1,0:T(8,128)S(1)}, u32[]{:S(2)}) copy-start(f32[16,8,128]{2,1,0:T(8,128)S(1)} %get-tuple-element.85.refs_26_) | copy-start | bytes 196612
  39.7 0.7 copy-start.27
  39.8 0.8 copy-start.30
  40.3 7.3 %copy-start.8 = (f32[128,1024]{1,0:T(8,128)}, f32[128,1024]{1,0:T(8,128)S(1)}, u32[]{:S(2)}) copy-start(f32[128,1024]{1,0:T(8,128)S(1)} %get-tuple-element.113.refs_21_) | copy-start | bytes 1572868
  40.6 6.8 %copy-start.13 = (bf16[128,1024]{1,0:T(8,128)(2,1)}, bf16[128,1024]{1,0:T(8,128)(2,1)S(1)}, u32[]{:S(2)}) copy-start(bf16[128,1024]{1,0:T(8,128)(2,1)S(1)} %multiply_convert_fusion.refs_22_) | copy-start | bytes 786436
  40.6 6.8 %copy-start.31 = (s32[2]{0:T(128)S(1)}, s32[2]{0:T(128)}, u32[]{:S(2)}) copy-start(s32[2]{0:T(128)} %param.29) | copy-start | bytes 28
  40.6 7.0 %copy-start.29 = (f32[1024]{0:T(1024)S(1)}, f32[1024]{0:T(1024)}, u32[]{:S(2)}) copy-start(f32[1024]{0:T(1024)} %param.41) | copy-start | bytes 12292
  47.4 5.1 %copy-start.10 = (bf16[128,4096]{1,0:T(8,128)(2,1)}, bf16[128,4096]{1,0:T(8,128)(2,1)S(1)}, u32[]{:S(2)}) copy-start(bf16[128,4096]{1,0:T(8,128)(2,1)S(1)} %get-tuple-element.114.refs_16_) | copy-start | bytes 3145732
  47.6 4.9 %copy-start.28 = (s32[2,64,3]{1,0,2:T(2,128)S(1)}, s32[2,64,3]{1,0,2:T(2,128)}, u32[]{:S(2)}) copy-start(s32[2,64,3]{1,0,2:T(2,128)} %param.28) | copy-start | bytes 4612
  52.4 7.0 %copy-start.12 = (bf16[128,1024]{1,0:T(8,128)(2,1)}, bf16[128,1024]{1,0:T(8,128)(2,1)S(1)}, u32[]{:S(2)}) copy-start(bf16[128,1024]{1,0:T(8,128)(2,1)S(1)} %fusion.10) | copy-start | bytes 786436
  52.6 6.5 %copy-start.11 = (bf16[2,64,4,1024]{3,2,1,0:T(4,128)(2,1)S(1)}, bf16[2,64,4,1024]{3,2,1,0:T(4,128)(2,1)}, u32[]{:S(2)}) copy-start(bf16[2,64,4,1024]{3,2,1,0:T(4,128)(2,1)} %param.53) | copy-start | bytes 3145732
  115.6 17.8 %copy-start.18 = (bf16[2,64,1024]{2,1,0:T(8,128)(2,1)S(1)}, bf16[2,64,1024]{2,1,0:T(8,128)(2,1)}, u32[]{:S(2)}) copy-start(bf16[2,64,1024]{2,1,0:T(8,128)(2,1)} %param.52) | copy-start | bytes 786436
  392.9 7.2 %copy-start.26 = (f32[64,1024]{1,0:T(8,128)S(1)}, f32[64,1024]{1,0:T(8,128)}, u32[]{:S(2)}) copy-start(f32[64,1024]{1,0:T(8,128)} %get-tuple-element.147) | copy-start | bytes 786436
  392.9 7.9 %copy-start.25 = (f32[64,1024]{1,0:T(8,128)S(1)}, f32[64,1024]{1,0:T(8,128)}, u32[]{:S(2)}) copy-start(f32[64,1024]{1,0:T(8,128)} %get-tuple-element.148) | copy-start | bytes 786436
  392.9 8.6 %copy-start.24 = (f32[64,1024]{1,0:T(8,128)S(1)}, f32[64,1024]{1,0:T(8,128)}, u32[]{:S(2)}) copy-start(f32[64,1024]{1,0:T(8,128)} %get-tuple-element.149) | copy-start | bytes 786436
  396.0 6.2 %copy-start.23 = (f32[64,1024]{1,0:T(8,128)S(1)}, f32[64,1024]{1,0:T(8,128)}, u32[]{:S(2)}) copy-start(f32[64,1024]{1,0:T(8,128)} %get-tuple-element.150) | copy-start | bytes 786436
  397.9 5.0 %copy-start.17 = (f32[64,4096]{1,0:T(8,128)S(1)}, f32[64,4096]{1,0:T(8,128)}, u32[]{:S(2)}) copy-start(f32[64,4096]{1,0:T(8,128)} %get-tuple-element.152) | copy-start | bytes 3145732
  400.1 3.8 copy-start.16
  402.9 2.0 copy-start.22
  402.9 2.7 copy-start.21
  403.9 2.4 copy-start.20
  403.9 3.1 copy-start.19
  403.9 3.8 copy-start.15
  404.9 3.8 copy-start.14

commit v6 on v5

--- a/solution.py
+++ b/solution.py
@@ -358,9 +358,11 @@
 
 
 def attend_kernel(
-    count, x_ref, mask_ref, n1_ref, wq_ref, wk_ref, wv_ref,
-    normed_ref, mixed_ref, saved_ref, log_ref,
-    packed, held, mixed_all, pieces, bias, v_t, send_sem, recv_sem, send_two, recv_two, save_sem,
+    count, x_ref, mask_ref, n1_ref, wq_ref, wk_ref, wv_ref, codes_ref, valid_ref, n2_ref, b1_ref,
+    b2_ref, table_ref, wo_ref, w1_ref, w2_ref,
+    normed_ref, mixed_ref, saved_ref, log_ref, local_ref, mid_ref, hn_ref, u_ref, act_ref,
+    packed, held, mixed_all, pieces, bias, v_t, table, wo, w1, w2,
+    send_sem, recv_sem, send_two, recv_two, save_sem, fetch_sem,
 ):
     share = count // 16
     me = lax.axis_index("seq")
@@ -368,9 +370,18 @@
     own_utt, own_pair = unit // 8, unit % 8
     own_cols = pl.ds(pl.multiple_of(own_pair * LANES, LANES), LANES)
     utts, frames, width = x_ref.shape
+    rows = utts * frames
     barrier = greet(count)
-
-    x = x_ref[...].astype(F32).reshape(utts * frames, width)
+    fetches = [
+        pltpu.make_async_copy(source, target, fetch_sem.at[index])
+        for index, (source, target) in enumerate(
+            ((table_ref, table), (wo_ref, wo), (w1_ref, w1), (w2_ref, w2))
+        )
+    ]
+    for copy in fetches:
+        copy.start()
+
+    x = x_ref[...].astype(F32).reshape(rows, width)
     normed = (x * scale_of(x) * n1_ref[...]).astype(LOW)
     normed_ref[...] = normed
     packed[:, 0:64] = (mul(normed, wq_ref[...]).astype(LOW)).reshape(utts, frames, width)
@@ -396,15 +407,14 @@
 
     held[me] = packed[own_utt, :, own_cols]
 
-    @pl.loop(1, count)
-    def _(step):
-        place = lax.rem(me + count - step, count)
-        remote(held.at[place], held.at[place], send_sem.at[step], recv_sem.at[step], place).wait_recv()
+    fetches[0].wait()
+    vocab = table.shape[0] // CB
+    for book in range(CB):
+        ids = jnp.broadcast_to(codes_ref[book][:, 0:1], (rows, vocab))
+        picked = (ids == lax.broadcasted_iota(jnp.int32, (rows, vocab), 1)).astype(LOW)
+        local_ref[1 + book] = mul(picked, table[book * vocab : (book + 1) * vocab]).astype(LOW)
 
     save = pltpu.make_async_copy(held, saved_ref, save_sem)
-    save.start()
-    v_t[...] = held[:, 128:192].reshape(count * HD, LANES).T
-    fill_bias(bias, held[:, 192:208])
 
     def returning(block):
         return remote(
@@ -418,6 +428,17 @@
     for group in range(count // 4):
         below = group * 256
         here = below + 256
+        for place in range(4 * group, 4 * group + 4):
+
+            @pl.when(place != me)
+            def _():
+                step = lax.rem(me + count - place, count)
+                remote(
+                    held.at[place], held.at[place], send_sem.at[step], recv_sem.at[step], place
+                ).wait_recv()
+
+        v_t[:, below:here] = held[4 * group : 4 * group + 4, 128:192].reshape(256, LANES).T
+        fill_bias(bias.at[below:here], held[4 * group : 4 * group + 4, 192:208])
 
         @pl.loop(0, 4 // share)
         def _(index):
@@ -450,6 +471,8 @@
             def _():
                 mixed_all[own_utt, :, own_cols] = pieces[block]
 
+    save.start()
+
     @pl.loop(0, 16)
     def _(other):
         place = other * share + me % share
@@ -460,6 +483,25 @@
             here = mixed_all.at[other // 8, :, cols]
             remote(here, here, send_two.at[0], recv_two.at[other], place).wait_recv()
 
+    mixed = mixed_all[...].reshape(rows, width)
+    mixed_ref[...] = mixed
+    fetches[1].wait()
+    mid = x_ref[...].astype(F32).reshape(rows, width) + mul(mixed, wo[...])
+    hn = (mid * scale_of(mid) * n2_ref[...]).astype(LOW)
+    mid_ref[...] = mid
+    hn_ref[...] = hn
+    fetches[2].wait()
+    fetches[3].wait()
+    result = mid + b2_ref[...]
+    for first in range(0, u_ref.shape[1], 512):
+        cols = slice(first, first + 512)
+        u = mul(hn, w1[:, cols]) + b1_ref[:, cols]
+        act = gelu_parts(u)[0].astype(LOW)
+        u_ref[:, cols] = u
+        act_ref[:, cols] = act
+        result = result + mul(act, w2[cols])
+    local_ref[0] = jnp.where(valid_ref[...] > 0, result, 0.0).astype(LOW)
+
     @pl.loop(1, count)
     def _(step):
         outgoing(step).wait_send()
@@ -472,24 +514,29 @@
         def _():
             returning(block).wait_send()
 
-    mixed_ref[...] = mixed_all[...]
     save.wait()
 
 
-def global_attend(x, mask, params):
+def global_forward(x, mask, codes, valid, table, params):
     count = lax.axis_size("seq")
     utts, frames, width = x.shape
+    rows, wide = utts * frames, params[6].shape[1]
     vmem = pl.BlockSpec(memory_space=pltpu.VMEM)
     hbm = pl.BlockSpec(memory_space=pl.ANY)
     return pl.pallas_call(
         functools.partial(attend_kernel, count),
-        in_specs=[vmem] * 6,
-        out_specs=[vmem, vmem, hbm, vmem],
+        in_specs=[vmem] * 11 + [hbm] * 4,
+        out_specs=[vmem, vmem, hbm] + [vmem] * 6,
         out_shape=[
-            jax.ShapeDtypeStruct((utts * frames, width), LOW),
-            jax.ShapeDtypeStruct((utts, frames, width), LOW),
+            jax.ShapeDtypeStruct((rows, width), LOW),
+            jax.ShapeDtypeStruct((rows, width), LOW),
             jax.ShapeDtypeStruct((count, 208, LANES), LOW),
             jax.ShapeDtypeStruct((count, 8, LANES), F32),
+            jax.ShapeDtypeStruct((1 + CB, rows, width), LOW),
+            jax.ShapeDtypeStruct((rows, width), F32),
+            jax.ShapeDtypeStruct((rows, width), LOW),
+            jax.ShapeDtypeStruct((rows, wide), F32),
+            jax.ShapeDtypeStruct((rows, wide), LOW),
         ],
         scratch_shapes=[
             pltpu.VMEM((utts, 208, width), LOW),
@@ -498,16 +545,57 @@
             pltpu.VMEM((count, HD, LANES), LOW),
             pltpu.VMEM((count * HD, LANES), F32),
             pltpu.VMEM((LANES, count * HD), LOW),
+            pltpu.VMEM(table.shape, LOW),
+            pltpu.VMEM(params[4].shape, LOW),
+            pltpu.VMEM(params[6].shape, LOW),
+            pltpu.VMEM(params[8].shape, LOW),
             pltpu.SemaphoreType.DMA((count,)),
             pltpu.SemaphoreType.DMA((count,)),
             pltpu.SemaphoreType.DMA((count,)),
             pltpu.SemaphoreType.DMA((16,)),
             pltpu.SemaphoreType.DMA,
+            pltpu.SemaphoreType.DMA((4,)),
         ],
         compiler_params=pltpu.CompilerParams(
-            collective_id=2, has_side_effects=True, vmem_limit_bytes=48 << 20
+            collective_id=2, has_side_effects=True, vmem_limit_bytes=58 << 20
         ),
-    )(x, mask, params[0].reshape(1, -1), params[1], params[2], params[3])
+    )(
+        x, mask, params[0].reshape(1, -1), params[1], params[2], params[3], codes, valid,
+        params[5].reshape(1, -1), params[7].reshape(1, -1), params[9].reshape(1, -1), table,
+        params[4], params[6], params[8],
+    )
+
+
+def settle_kernel(number, *refs):
+    sources, targets, held = (refs[index * number : (index + 1) * number] for index in range(3))
+    into = [
+        pltpu.make_async_copy(sources[index], held[index], refs[-1].at[0, index])
+        for index in range(number)
+    ]
+    out = [
+        pltpu.make_async_copy(held[index], targets[index], refs[-1].at[1, index])
+        for index in range(number)
+    ]
+    for copy in into:
+        copy.start()
+    for first, second in zip(into, out):
+        first.wait()
+        second.start()
+    for copy in out:
+        copy.wait()
+
+
+def settle(arrays):
+    hbm = pl.BlockSpec(memory_space=pl.ANY)
+    return pl.pallas_call(
+        functools.partial(settle_kernel, len(arrays)),
+        in_specs=[hbm] * len(arrays),
+        out_specs=[hbm] * len(arrays),
+        out_shape=[jax.ShapeDtypeStruct(item.shape, item.dtype) for item in arrays],
+        scratch_shapes=[pltpu.VMEM(item.shape, item.dtype) for item in arrays]
+        + [pltpu.SemaphoreType.DMA((2, len(arrays)))],
+        compiler_params=pltpu.CompilerParams(vmem_limit_bytes=62 << 20),
+    )(*arrays)
 
 
 def attend_back_kernel(
@@ -1383,10 +1471,6 @@
     return jax.nn.gelu(values, approximate=True)
 
 
-def project(left_side, weight):
-    return jnp.dot(left_side, weight, preferred_element_type=jnp.float32)
-
-
 def project_back(gradient, weight):
     return lax.dot_general(
         gradient, weight, (((1,), (1,)), ((), ())), preferred_element_type=jnp.float32
@@ -1397,15 +1481,6 @@
     return lax.dot_general(
         left_side, gradient, (((0,), (0,)), ((), ())), preferred_element_type=jnp.float32
     )
-
-
-def block_outputs(inputs, mixed_rows, params):
-    middle = inputs + project(mixed_rows, params[4])
-    middle_norm = normalize(middle, params[5]).astype(jnp.bfloat16)
-    pre_active = project(middle_norm, params[6]) + params[7]
-    active = gelu_fn(pre_active).astype(jnp.bfloat16)
-    result = middle + project(active, params[8]) + params[9]
-    return (result, (middle, middle_norm, pre_active, active))
 
 
 def block_back(inputs, normed, mixed_rows, kept_parts, params, grad_out, attention_back):
@@ -1506,15 +1581,19 @@
         local_w_down,
         local_b_down,
     )
-    global_in = frames.astype(jnp.float32).reshape(row_count, model_width)
-    glob_normed, glob_mixed, saved, log_total = global_attend(frames, usable, glob_params)
-    glob_mixed = glob_mixed.reshape(row_count, model_width)
-    glob_result, glob_kept = block_outputs(global_in, glob_mixed, glob_params)
-    global_rows = jnp.where(valid.reshape(row_count, 1), glob_result, 0.0).astype(jnp.bfloat16)
     code_rows = codes.transpose(2, 0, 1).reshape(CB, row_count)
-    table_ids = code_rows + VOCAB * jnp.arange(CB, dtype=jnp.int32)[:, None]
-    embedded = table.at[table_ids].get(mode="promise_in_bounds")
-    local_in = jnp.concatenate([global_rows[None], embedded], axis=0)
+    (
+        glob_normed, glob_mixed, saved, log_total, local_in,
+        glob_middle, glob_middle_norm, pre_active, active,
+    ) = global_forward(
+        frames,
+        usable,
+        jnp.broadcast_to(code_rows[:, :, None], (CB, row_count, LANES)),
+        valid.reshape(row_count, 1).astype(F32),
+        table,
+        glob_params,
+    )
+    global_rows = local_in[0]
     local_shape = (local_len, row_count, model_width)
     flat_shape = (local_len * row_count, model_width)
     normed, local_q, local_k, local_v, local_probs, mixed, middle, middle_norm = local_front(
@@ -1554,7 +1633,6 @@
     outputs = (global_rows.reshape(utter_count, frame_count, model_width), local_rows)
 
     if lax.axis_size("seq") == 16 and lax.axis_size("utt") == 2:
-        glob_middle, glob_middle_norm, pre_active, active = glob_kept
         far = dict(
             l_up=grad_w_up.reshape(8, 2, -1, grad_w_up.shape[1]),
             l_down=grad_w_down.reshape(8, 2, -1, grad_w_down.shape[1]),
@@ -1591,7 +1669,7 @@
             l_db1=grad_b_up,
             l_db2=grad_b_down.reshape(1, -1),
         )
-        grad_inputs, *sums = finish_on_slice(far, near)
+        grad_inputs, *sums = settle(finish_on_slice(far, near))
         wide = dict(zip("12qkvot76pabc", sums[:-1]))
         half = lax.axis_index("seq") % 2
         rest = sums[-1]
@@ -1650,6 +1728,8 @@
         )
         return tuple(grads.reshape(3, row_count, model_width))
 
+    global_in = frames.astype(F32).reshape(row_count, model_width)
+    glob_kept = (glob_middle, glob_middle_norm, pre_active, active)
     grad_inputs, glob_grads = block_back(
         global_in, glob_normed, glob_mixed, glob_kept, glob_params, glob_cotan, global_back
     )

time: 410 us -> 389 us (0.949)
  local copies, waits for them, and re-layouts: 27.6 us -> 6.9 us
  Pallas kernels: 357 us -> 371 us
  matrix products: 12.1 us -> 0 us
    unnamed x78 -> x6, local copies, waits for them, and re-layouts: 18.7 us -> 0.01 us
    dot_general x3 -> x0, matrix products: 12.1 us -> none  [project(): return jnp.dot(left_side, weight, preferred_element_type=jnp.float32)]
    pallas_call x1 -> x2, Pallas kernels: 33.5 us -> 44.5 us  [the longest x1 38.3 us: global_forward(): pl.pallas_call(functools.partial(attend_kernel, count), in_specs=[vmem] *...]
    gather x1 -> x0, local copies, waits for them, and re-layouts: 6.45 us -> none  [on_device(): embedded = table.at[table_ids].get(mode='promise_in_bounds')]
where the time goes in v6:
time: 389 us
  Pallas kernels  371 us (95%)
  other arithmetic  10.5 us (3%)
  local copies, waits for them, and re-layouts  6.9 us (2%)
    pallas_call x1, Pallas kernels, finish_on_slice(): pl.pallas_call(functools.partial(tail_kernel, names, len(shapes)), in_spe...  258 us
    pallas_call x1, Pallas kernels, global_forward(): pl.pallas_call(functools.partial(attend_kernel, count), in_specs=[vmem] *...  38.3 us
    pallas_call x1, Pallas kernels, local_ffn(): pl.pallas_call(ffn_kernel, grid=(wide // step,), in_specs=[whole, whole,...  35.4 us
    pallas_call x1, Pallas kernels, local_back(): pl.pallas_call(back_kernel, grid=(frames // step,), in_specs=[rows] * 7 +...  17.6 us
    pallas_call x1, Pallas kernels, local_front(): pl.pallas_call(front_kernel, grid=(frames // step,), in_specs=[rows] + [w...  14.9 us

profile of v6, /device:TPU:0, one launch (start us, length us, event | category | flops | bytes accessed | tf_op | source)
XLA Modules:
  0.0 389.0 jit_solution(11255250292498644873)
XLA Ops:
  0.7 0.7 fusion.7
  1.4 0.8 reshape.266.valid_ref
  2.2 0.8 broadcast_in_dim.62
  2.9 0.8 broadcast_in_dim.63.codes_ref
  3.7 0.7 convert_element_type.20
  4.4 0.6 broadcast_in_dim.61.mask_ref
  5.0 38.3 %shard_map.442 = (bf16[128,1024]{1,0:T(8,128)(2,1)}, bf16[128,1024]{1,0:T(8,128)(2,1)}, bf16[16,208,128]{2,1,0:T(8,128)(2,1)}, f32[16,8,128]{2,1,0:T(8,128)}, bf...) custom-call(bf16[2,64,1024]{2,1,0:T(8,128)(2,1)} %x_ref.1, ...), custom_call_target="tpu_custom_call" | custom-call | tf_op jit(solution)/shard_map/pallas_call | solution.py:526
  43.4 0.0 copy-start
  43.4 14.9 %shard_map.443 = (bf16[4,128,1024]{2,1,0:T(8,128)(2,1)}, bf16[4,128,1024]{2,1,0:T(8,128)(2,1)}, bf16[4,128,1024]{2,1,0:T(8,128)(2,1)}, bf16[4,128,1024]{2,1,0:T(...) custom-call(bf16[4,128,1024]{2,1,0:T(8,128)(2,1)} %get-tuple-element, ...), custom_call_target="tpu_custom_call" | custom-call | tf_op jit(solution)/shard_map/pallas_call | solution.py:129
  58.3 0.1 lt.43
  58.4 0.0 copy-done
  58.4 0.3 copy.52
  58.7 1.2 bitcast_select_fusion.1.dout_ref
  59.9 35.4 %shard_map.444 = (bf16[512,1024]{1,0:T(8,128)(2,1)}, f32[512,1024]{1,0:T(8,128)}, bf16[1024,4096]{1,0:T(8,128)(2,1)}, bf16[4096,1024]{1,0:T(8,128)(2,1)}, f32[1,4096]{1,0:T(1,128)}) custom-call(bf16[512,1024]{1,0:T(8,128)(2,1)} %bitcast.66, bf16[512,1024]{1,0:T(8,128)(2,1)} %bitcast_select_fusion.1.dout_ref, f32[512,1024]{1,0:T(8,128)} %bitcast.55, ...), custom_call_target="tpu_custom_call" | custom-call | tf_op jit(solution)/shard_map/pallas_call | solution.py:188
  95.2 1.2 bitcast_select_fusion.dout_ref
  96.4 0.0 copy-start.2
  96.4 17.6 %shard_map.445 = (bf16[4,128,1024]{2,1,0:T(8,128)(2,1)}, bf16[4,128,1024]{2,1,0:T(8,128)(2,1)}, bf16[4,128,1024]{2,1,0:T(8,128)(2,1)}, bf16[4,128,1024]{2,1,0:T(...) custom-call(bf16[4,128,1024]{2,1,0:T(8,128)(2,1)} %get-tuple-element.8, ...), custom_call_target="tpu_custom_call" | custom-call | tf_op jit(solution)/shard_map/pallas_call | solution.py:284
  114.0 0.0 copy-done.2
  114.0 1.9 add_select_fusion
  116.0 1.2 convert_reduce_fusion
  117.2 0.6 broadcast_in_dim.74.refs_27_
  117.8 258.5 %shard_map.446 = (f32[128,1024]{1,0:T(8,128)}, f32[64,4096]{1,0:T(8,128)}, f32[256,1024]{1,0:T(8,128)}, f32[64,1024]{1,0:T(8,128)}, f32[64,1024]{1,0:T(8,128)}, ...) custom-call(bf16[8,2,64,4096]{3,2,1,0:T(8,128)(2,1)} %bitcast.53, ...), custom_call_target="tpu_custom_call" | custom-call | tf_op jit(solution)/shard_map/pallas_call | solution.py:1450
  376.2 0.0 copy-start.1
  376.3 6.2 %shard_map.447 = (f32[128,1024]{1,0:T(8,128)}, f32[64,4096]{1,0:T(8,128)}, f32[256,1024]{1,0:T(8,128)}, f32[64,1024]{1,0:T(8,128)}, f32[64,1024]{1,0:T(8,128)}, ...) custom-call(f32[128,1024]{1,0:T(8,128)} %get-tuple-element.114.refs_, ...), custom_call_target="tpu_custom_call" | custom-call | tf_op jit(solution)/shard_map/pallas_call | solution.py:590
  382.5 1.7 fusion.6
  384.2 1.3 slice_bitcast_fusion
  385.5 0.0 copy-done.1
  385.5 1.8 fusion
  387.3 1.7 slice.45
  (3 shorter events, 0.0 us)
Async XLA Ops:
  43.4 15.0 %copy-start = (bf16[2,64,4,1024]{3,2,1,0:T(4,128)(2,1)S(1)}, bf16[2,64,4,1024]{3,2,1,0:T(4,128)(2,1)}, u32[]{:S(2)}) copy-start(bf16[2,64,4,1024]{3,2,1,0:T(4,128)(2,1)} %param.53) | copy-start | bytes 3145732
  96.4 17.6 %copy-start.2 = (bf16[2,64,1024]{2,1,0:T(8,128)(2,1)S(1)}, bf16[2,64,1024]{2,1,0:T(8,128)(2,1)}, u32[]{:S(2)}) copy-start(bf16[2,64,1024]{2,1,0:T(8,128)(2,1)} %param.52) | copy-start | bytes 786436
  376.2 9.2 %copy-start.1 = (bf16[512,1024]{1,0:T(8,128)(2,1)S(1)}, bf16[512,1024]{1,0:T(8,128)(2,1)}, u32[]{:S(2)}) copy-start(bf16[512,1024]{1,0:T(8,128)(2,1)} %get-tuple-element.87) | copy-start | bytes 3145732

commit v7 on v6

--- a/solution.py
+++ b/solution.py
@@ -152,7 +152,7 @@
 
 def ffn_kernel(
     hn_ref, dout_ref, mid_ref, w1_ref, b1_ref, w2_ref, b2_ref,
-    y_ref, dhn_ref, dw1_ref, dw2_ref, db1_ref, acc_ref, hn_t_ref,
+    y_ref, dhn_ref, dw1_ref, dw2_ref, db1_ref, db2_ref, acc_ref, hn_t_ref,
 ):
     at = pl.program_id(0)
     last = pl.num_programs(0) - 1
@@ -162,6 +162,7 @@
         hn_t_ref[...] = hn_ref[...].T
         acc_ref[...] = mid_ref[...] + b2_ref[...]
         dhn_ref[...] = jnp.zeros_like(dhn_ref)
+        db2_ref[...] = jnp.sum(dout_ref[...].astype(F32), axis=0, keepdims=True)
 
     hn, dout = hn_ref[...], dout_ref[...]
     u = mul(hn, w1_ref[...]) + b1_ref[...]
@@ -200,6 +201,7 @@
             pl.BlockSpec((width, step), lambda i: (0, i)),
             pl.BlockSpec((step, width), lambda i: (i, 0)),
             pl.BlockSpec((1, step), lambda i: (0, i)),
+            pl.BlockSpec((1, width), lambda i: (0, 0)),
         ],
         out_shape=[
             jax.ShapeDtypeStruct((rows, width), LOW),
@@ -207,6 +209,7 @@
             jax.ShapeDtypeStruct((width, wide), LOW),
             jax.ShapeDtypeStruct((wide, width), LOW),
             jax.ShapeDtypeStruct((1, wide), F32),
+            jax.ShapeDtypeStruct((1, width), F32),
         ],
         scratch_shapes=[pltpu.VMEM((rows, width), F32), pltpu.VMEM((width, rows), LOW)],
         compiler_params=pltpu.CompilerParams(vmem_limit_bytes=56 << 20),
@@ -759,10 +762,12 @@
 )
 SLABS = 55
 LOADED = 16
-AT_BACK = 8
-AT_ATTEND = 15
-AT_RETURN = 23
-AT_LANDED = 40
+AT_HIDDEN = 8
+AT_BACK = 16
+AT_ATTEND = 23
+AT_RETURN = 31
+AT_LANDED = 47
+PART = 32
 
 
 def tail_kernel(names, out_count, *refs):
@@ -824,9 +829,9 @@
     fetches = (
         (r.g_w_o, r.square.at[0]), (r.g_w_q, r.square.at[1]), (r.g_w_k, r.square.at[2]),
         (r.g_w_v, r.square.at[3]), (r.saved, r.held), (r.l_normed, r.l_x.at[0]),
-        (r.l_mixed, r.l_x.at[1]), (r.l_dq, r.l_g.at[0]), (r.l_dk, r.l_g.at[1]),
-        (r.l_dv, r.l_g.at[2]), (r.l_dattn, r.l_g.at[3]), (r.rest, r.table_g),
-        (r.g_act, r.act_buf), (r.g_mixed, r.g_x.at[0]), (r.g_normed, r.g_x.at[1]),
+        (r.l_mixed, r.l_x.at[1]), (r.g_act, r.act_buf), (r.g_mixed, r.g_x.at[0]),
+        (r.g_normed, r.g_x.at[1]), (r.l_w_o, r.square.at[0]), (r.l_w_q, r.square.at[1]),
+        (r.l_w_k, r.square.at[2]), (r.l_w_v, r.square.at[3]),
     )
 
     def fetch(*which):
@@ -834,9 +839,21 @@
             pltpu.make_async_copy(*fetches[index], r.fetch_sem.at[index]) for index in which
         ]
 
-    for copy in weights(0, 0) + tuple(fetch(0)):
+    def local_rows(step, slot):
+        rows = pl.ds(step * PART if isinstance(step, int) else pl.multiple_of(step * PART, PART), PART)
+        pairs = (
+            (r.l_in, r.l_in_buf), (r.l_mid, r.l_mid_buf), (r.l_dhn, r.l_dhn_buf),
+            (r.l_dout, r.l_dout_buf), (r.l_q, r.l_q_buf), (r.l_k, r.l_k_buf), (r.l_v, r.l_v_buf),
+            (r.l_probs, r.l_probs_buf),
+        )
+        return [
+            pltpu.make_async_copy(ref.at[:, rows], buffer.at[slot], r.local_sem.at[slot, index])
+            for index, (ref, buffer) in enumerate(pairs)
+        ]
+
+    load_start(0)
+    for copy in local_rows(0, 0) + fetch(10, 11, 12, 13):
         copy.start()
-    load_start(0)
 
     def send(kind, slot, source, target, device):
         return pltpu.make_async_remote_copy(
@@ -1187,37 +1204,76 @@
                 hit = hit | (tick == item)
             return pl.when(hit)
 
-        @pl.when(tick < 8)
-        def _():
-            slot = tick % 2
-            for copy in weights(tick, slot):
+        @pl.when((tick < 8) & (tick % 2 == 0))
+        def _():
+            step = tick // 2
+            slot = step % 2
+            for copy in local_rows(step, slot):
                 copy.wait()
-
-            @pl.when(tick < 7)
-            def _():
-                for copy in weights(tick + 1, 1 - slot):
-                    copy.start()
 
             @pl.when(tick == 0)
             def _():
-                r.dout_low[...] = r.dout[...].astype(LOW)
-                r.dhn[...] = jnp.zeros_like(r.dhn)
-
-            cols = cols_of(tick)
+                for copy in fetch(10):
+                    copy.wait()
+                r.l_dn1[...] = jnp.zeros_like(r.l_dn1)
+                r.l_dn2[...] = jnp.zeros_like(r.l_dn2)
+
+            @pl.when(step < 3)
+            def _():
+                for copy in local_rows(step + 1, 1 - slot):
+                    copy.start()
+
+            local_attend_back(r, step, slot)
+
+        @pl.when((tick < 8) & (tick % 2 == 1))
+        def _():
+            @pl.when(tick == 1)
+            def _():
+                for copy in fetch(11, 12, 13):
+                    copy.wait()
+
+            local_project_back(r, tick // 2, (tick // 2) % 2)
+
+        @at(6)
+        def _():
+            for copy in weights(0, 0) + tuple(fetch(4, 5, 6)):
+                copy.start()
+
+        @at(AT_HIDDEN)
+        def _():
+            for copy in fetch(0, 1, 2, 3):
+                copy.start()
+            r.dout_low[...] = r.dout[...].astype(LOW)
+            r.dhn[...] = jnp.zeros_like(r.dhn)
+
+        @pl.when((tick >= AT_HIDDEN) & (tick < AT_HIDDEN + 8))
+        def _():
+            block = tick - AT_HIDDEN
+            slot = block % 2
+            for copy in weights(block, slot):
+                copy.wait()
+
+            @pl.when(block < 7)
+            def _():
+                for copy in weights(block + 1, 1 - slot):
+                    copy.start()
+
+            cols = cols_of(block)
             _, slope = gelu_parts(r.u[:, cols])
             du = (mul_t(r.dout_low[...], r.down_buf[slot]) * slope).astype(LOW)
             r.du[:, cols] = du
-            r.db1[pl.ds(tick, 1), :] = jnp.sum(du.astype(F32), axis=0, keepdims=True)
+            r.db1[pl.ds(block, 1), :] = jnp.sum(du.astype(F32), axis=0, keepdims=True)
             r.dhn[...] += mul_t(du, r.up_buf[slot])
 
-        @at(3)
-        def _():
-            for copy in fetch(4, 5, 6, 7, 8, 9, 10):
-                copy.start()
-
-        @at(12)
-        def _():
-            for copy in fetch(1, 2, 3, 11, 12, 13, 14):
+        @at(13)
+        def _():
+            for copy in fetch(4, 5, 6):
+                copy.wait()
+            r.l_x_t[...] = r.l_x[0].T
+
+        @at(18)
+        def _():
+            for copy in fetch(7, 8, 9):
                 copy.start()
 
         @at(AT_BACK)
@@ -1241,13 +1297,10 @@
 
         @at(AT_BACK + 1)
         def _():
-            for copy in fetch(4, 5, 6, 7, 8, 9, 10):
-                copy.wait()
             r.k_t[...] = r.held[:, 64:128].reshape(count * HD, LANES).T
             fill_bias(r.bias, r.held[:, 192:208])
             r.dk_acc[...] = jnp.zeros_like(r.dk_acc)
             r.dv_acc[...] = jnp.zeros_like(r.dv_acc)
-            r.l_x_t[...] = r.l_x[0].T
 
         @at(AT_ATTEND)
         def _():
@@ -1320,7 +1373,7 @@
 
         @at(22)
         def _():
-            for copy in fetch(11, 12, 13, 14):
+            for copy in fetch(7, 8, 9):
                 copy.wait()
 
         @pl.when((tick >= 24) & (tick < 28))
@@ -1328,7 +1381,7 @@
             cols = pl.ds(pl.multiple_of((tick - 24) * 1024, 1024), 1024)
             r.act_t[cols] = r.act_buf[:, cols].T
 
-        @at(29)
+        @at(28)
         def _():
             r.g_hn_t[...] = r.hn[...].T
 
@@ -1343,6 +1396,74 @@
         advance(tick)
         compute(tick)
         produce(tick + 1)
+
+
+def local_attend_back(r, step, slot):
+    places, width = r.l_in_buf.shape[1], r.l_in_buf.shape[3]
+    frames = r.l_in.shape[1]
+    rows = places * PART
+
+    def rows_of(place):
+        return pl.ds(pl.multiple_of(place * frames + step * PART, PART), PART)
+
+    mid = r.l_mid_buf[slot].reshape(rows, width)
+    dmid, gain = scale_back(mid, r.l_n2[...], r.l_dhn_buf[slot].reshape(rows, width))
+    r.l_dn2[...] += jnp.sum(gain, axis=0, keepdims=True)
+    dmid = dmid + r.l_dout_buf[slot].astype(F32).reshape(rows, width)
+    r.l_dmid[...] = dmid
+    dattn = dmid.astype(LOW)
+    for place in range(places):
+        r.l_g[3, rows_of(place)] = dattn[place * PART : (place + 1) * PART]
+    r.l_dmix[...] = mul_t(dattn, r.square[0]).astype(LOW).reshape(places, PART, width)
+    sums, spread = head_sums(width), head_spread(width)
+    add = lambda old, term: term if old is None else old + term
+    pair = 0
+    dk, dv = [None] * places, [None] * places
+    for i in range(places):
+        grad = r.l_dmix[i].astype(F32)
+        query = r.l_q_buf[slot, i].astype(F32)
+        dp = [sum_heads(grad * r.l_v_buf[slot, j].astype(F32), sums) for j in range(i + 1)]
+        delta = None
+        for j in range(i + 1):
+            delta = add(delta, r.l_probs_buf[slot, pair + j] * dp[j])
+        dq = None
+        for j in range(i + 1):
+            probs = r.l_probs_buf[slot, pair + j]
+            ds = mul((probs * (dp[j] - delta)).astype(LOW), spread)
+            dq = add(dq, ds * r.l_k_buf[slot, j].astype(F32))
+            dk[j] = add(dk[j], ds * query)
+            dv[j] = add(dv[j], mul(probs.astype(LOW), spread) * grad)
+        pair += i + 1
+        r.l_g[0, rows_of(i)] = (dq * HD ** (-0.5)).astype(LOW)
+    for j in range(places):
+        r.l_g[1, rows_of(j)] = (dk[j] * HD ** (-0.5)).astype(LOW)
+        r.l_g[2, rows_of(j)] = dv[j].astype(LOW)
+
+
+def local_project_back(r, step, slot):
+    places, width = r.l_in_buf.shape[1], r.l_in_buf.shape[3]
+    frames = r.l_in.shape[1]
+    rows = places * PART
+    dnormed = None
+    for kind in range(3):
+        grad = jnp.concatenate(
+            [
+                r.l_g[kind, pl.ds(pl.multiple_of(place * frames + step * PART, PART), PART)]
+                for place in range(places)
+            ],
+            axis=0,
+        )
+        term = mul_t(grad, r.square[1 + kind])
+        dnormed = term if dnormed is None else dnormed + term
+    x = r.l_in_buf[slot].astype(F32).reshape(rows, width)
+    dx, gain = scale_back(x, r.l_n1[...], dnormed)
+    r.l_dn1[...] += jnp.sum(gain, axis=0, keepdims=True)
+    dx = dx + r.l_dmid[...]
+    here = pl.ds(pl.multiple_of(step * PART, PART), PART)
+    total = r.cotan[here].astype(F32) + dx[:PART]
+    r.dout[here] = jnp.where(r.valid[here] > 0, total, 0.0)
+    for place in range(1, places):
+        r.table_g[place - 1, here] = dx[place * PART : (place + 1) * PART].astype(LOW)
 
 
 def attend_back_block(r, group, below, here, block):
@@ -1387,6 +1508,7 @@
     ]
     out_names = ["dx"] + ["out_%d" % index for index in range(len(shapes))]
     rows_l = far["l_normed"].shape[0]
+    places, pairs = far["l_in"].shape[0], far["l_probs"].shape[0]
     buffers = dict(
         part=((SLOTS, 2, 8, 64, SCOLS), LOW),
         recv_c=((SLOTS, 8, 64, SCOLS), LOW),
@@ -1418,7 +1540,20 @@
         l_x=((2, rows_l, width), LOW),
         l_g=((4, rows_l, width), LOW),
         l_x_t=((width, rows_l), LOW),
-        table_g=(far["rest"].shape, LOW),
+        l_in_buf=((2, places, PART, width), LOW),
+        l_mid_buf=((2, places, PART, width), F32),
+        l_dhn_buf=((2, places, PART, width), F32),
+        l_dout_buf=((2, places, PART, width), LOW),
+        l_q_buf=((2, places, PART, width), LOW),
+        l_k_buf=((2, places, PART, width), LOW),
+        l_v_buf=((2, places, PART, width), LOW),
+        l_probs_buf=((2, pairs, PART, LANES), F32),
+        l_dmid=((places * PART, width), F32),
+        l_dmix=((places, PART, width), LOW),
+        l_dn1=((1, width), F32),
+        l_dn2=((1, width), F32),
+        dout=((rows, width), F32),
+        table_g=((places - 1, rows, width), LOW),
         act_buf=((rows, wide), LOW),
         act_t=((wide, rows), LOW),
         g_x=((2, rows, width), LOW),
@@ -1443,7 +1578,7 @@
     )
     semaphores = dict(
         load_sem=(SLOTS, 2), out_sem=(SLOTS,), send_sem=(26, SLOTS), recv_sem=(26, SLOTS),
-        weight_sem=(2, 2), fetch_sem=(15,), send_one=(16,), recv_one=(16,), send_two=(16,),
+        weight_sem=(2, 2), fetch_sem=(14,), local_sem=(2, 8), send_one=(16,), recv_one=(16,), send_two=(16,),
         recv_two=(16,),
     )
     names = list(far) + list(near) + out_names + list(buffers) + list(semaphores)
@@ -1456,7 +1591,7 @@
         scratch_shapes=[pltpu.VMEM(*item) for item in buffers.values()]
         + [pltpu.SemaphoreType.DMA(item) for item in semaphores.values()],
         compiler_params=pltpu.CompilerParams(
-            collective_id=1, has_side_effects=True, vmem_limit_bytes=60 << 20
+            collective_id=1, has_side_effects=True, vmem_limit_bytes=62 << 20
         ),
     )(*far.values(), *near.values())
 
@@ -1602,7 +1737,7 @@
     row_valid = valid.reshape(1, row_count, 1)
     local_cotan = cotan_local.transpose(2, 0, 1, 3).reshape(local_shape)
     local_cotan = jnp.where(row_valid, local_cotan, 0)
-    local_result, grad_hidden, grad_w_up, grad_w_down, grad_b_up = local_ffn(
+    local_result, grad_hidden, grad_w_up, grad_w_down, grad_b_up, grad_b_down = local_ffn(
         middle_norm.reshape(flat_shape),
         local_cotan.reshape(flat_shape),
         middle.reshape(flat_shape),
@@ -1611,25 +1746,8 @@
     local_rows = jnp.where(row_valid, local_result.reshape(local_shape), 0)
     local_rows = local_rows.reshape(local_len, utter_count, frame_count, model_width)
     local_rows = local_rows.transpose(1, 2, 0, 3)
-    grad_attn, grad_q, grad_k, grad_v, grad_first, grad_rest, grad_n1, grad_n2 = local_back(
-        local_in,
-        middle,
-        grad_hidden.reshape(local_shape),
-        local_cotan,
-        local_q,
-        local_k,
-        local_v,
-        local_probs,
-        local_params,
-    )
     normed = normed.reshape(flat_shape)
     mixed = mixed.reshape(flat_shape)
-    grad_b_down = jnp.sum(local_cotan.astype(F32), axis=(0, 1))
-    grad_first = grad_first.reshape(utter_count, frame_count, model_width)
-    glob_cotan = jnp.where(
-        valid[:, :, None], cotan_global.astype(jnp.float32) + grad_first, 0.0
-    )
-    glob_cotan = glob_cotan.reshape(row_count, model_width)
     outputs = (global_rows.reshape(utter_count, frame_count, model_width), local_rows)
 
     if lax.axis_size("seq") == 16 and lax.axis_size("utt") == 2:
@@ -1645,18 +1763,26 @@
             saved=saved,
             l_normed=normed,
             l_mixed=mixed,
-            l_dq=grad_q.reshape(flat_shape),
-            l_dk=grad_k.reshape(flat_shape),
-            l_dv=grad_v.reshape(flat_shape),
-            l_dattn=grad_attn.reshape(flat_shape),
-            rest=grad_rest,
+            l_in=local_in,
+            l_mid=middle,
+            l_dhn=grad_hidden.reshape(local_shape),
+            l_dout=local_cotan,
+            l_q=local_q,
+            l_k=local_k,
+            l_v=local_v,
+            l_probs=local_probs,
+            l_w_o=local_w_output,
+            l_w_q=local_w_query,
+            l_w_k=local_w_key,
+            l_w_v=local_w_value,
             g_act=active,
             g_mixed=glob_mixed,
             g_normed=glob_normed,
         )
         near = dict(
             u=pre_active,
-            dout=glob_cotan,
+            cotan=cotan_global.reshape(row_count, model_width),
+            valid=valid.reshape(row_count, 1).astype(F32),
             mid=glob_middle,
             hn=glob_middle_norm,
             x=frames.reshape(row_count, model_width),
@@ -1664,10 +1790,10 @@
             n2=glob_norm_two.reshape(1, -1),
             log_total=log_total,
             codes=jnp.broadcast_to(code_rows[:, None, :], (CB, 8, row_count)),
-            l_dn1=grad_n1,
-            l_dn2=grad_n2,
+            l_n1=local_norm_one.reshape(1, -1),
+            l_n2=local_norm_two.reshape(1, -1),
             l_db1=grad_b_up,
-            l_db2=grad_b_down.reshape(1, -1),
+            l_db2=grad_b_down,
         )
         grad_inputs, *sums = settle(finish_on_slice(far, near))
         wide = dict(zip("12qkvot76pabc", sums[:-1]))
@@ -1705,6 +1831,22 @@
             piece(7),
         )
 
+    grad_attn, grad_q, grad_k, grad_v, grad_first, grad_rest, grad_n1, grad_n2 = local_back(
+        local_in,
+        middle,
+        grad_hidden.reshape(local_shape),
+        local_cotan,
+        local_q,
+        local_k,
+        local_v,
+        local_probs,
+        local_params,
+    )
+    grad_first = grad_first.reshape(utter_count, frame_count, model_width)
+    glob_cotan = jnp.where(
+        valid[:, :, None], cotan_global.astype(jnp.float32) + grad_first, 0.0
+    )
+    glob_cotan = glob_cotan.reshape(row_count, model_width)
     local_grads = (
         grad_n1[0],
         weight_grad(normed, grad_q.reshape(flat_shape)),
@@ -1715,7 +1857,7 @@
         grad_w_up,
         grad_b_up[0],
         grad_w_down,
-        grad_b_down,
+        grad_b_down[0],
     )
     picked = code_rows[:, None, :] == jnp.arange(VOCAB, dtype=jnp.int32)[None, :, None]
     grad_tab = jnp.einsum(

time: 389 us -> 375 us (0.964)
  Pallas kernels: 371 us -> 360 us
    pallas_call x1 -> x0, Pallas kernels: 17.6 us -> none  [local_back(): pl.pallas_call(back_kernel, grid=(frames // step,), in_specs=[rows] * 7 +...]
    pallas_call x1, Pallas kernels: 258 us -> 265 us  [finish_on_slice(): pl.pallas_call(functools.partial(tail_kernel, names, len(shapes)), in_spe...]
where the time goes in v7:
time: 375 us
  Pallas kernels  360 us (96%)
  other arithmetic  7.31 us (2%)
  local copies, waits for them, and re-layouts  6.89 us (2%)
    pallas_call x1, Pallas kernels, finish_on_slice(): pl.pallas_call(functools.partial(tail_kernel, names, len(shapes)), in_spe...  265 us
    pallas_call x1, Pallas kernels, global_forward(): pl.pallas_call(functools.partial(attend_kernel, count), in_specs=[vmem] *...  38.3 us
    pallas_call x1, Pallas kernels, local_ffn(): pl.pallas_call(ffn_kernel, grid=(wide // step,), in_specs=[whole, whole,...  35.6 us
    pallas_call x1, Pallas kernels, local_front(): pl.pallas_call(front_kernel, grid=(frames // step,), in_specs=[rows] + [w...  14.9 us

profile of v7, /device:TPU:0, one launch (start us, length us, event | category | flops | bytes accessed | tf_op | source)
XLA Modules:
  0.0 375.0 jit_solution(1100481934049496880)
XLA Ops:
  0.7 0.7 fusion.7
  1.4 0.8 reshape.215.valid_ref.refs_28_
  2.2 0.8 broadcast_in_dim.49
  2.9 0.8 broadcast_in_dim.50.codes_ref
  3.7 0.7 convert_element_type.14
  4.4 0.6 broadcast_in_dim.48.mask_ref
  5.0 38.3 %shard_map.442 = (bf16[128,1024]{1,0:T(8,128)(2,1)}, bf16[128,1024]{1,0:T(8,128)(2,1)}, bf16[16,208,128]{2,1,0:T(8,128)(2,1)}, f32[16,8,128]{2,1,0:T(8,128)}, bf...) custom-call(bf16[2,64,1024]{2,1,0:T(8,128)(2,1)} %x_ref.1, ...), custom_call_target="tpu_custom_call" | custom-call | tf_op jit(solution)/shard_map/pallas_call | solution.py:529
  43.4 0.0 copy-start.1
  43.4 14.9 %shard_map.443 = (bf16[4,128,1024]{2,1,0:T(8,128)(2,1)}, bf16[4,128,1024]{2,1,0:T(8,128)(2,1)}, bf16[4,128,1024]{2,1,0:T(8,128)(2,1)}, bf16[4,128,1024]{2,1,0:T(...) custom-call(bf16[4,128,1024]{2,1,0:T(8,128)(2,1)} %get-tuple-element, ...), custom_call_target="tpu_custom_call" | custom-call | tf_op jit(solution)/shard_map/pallas_call | solution.py:129
  58.3 0.1 lt.39
  58.4 0.0 copy-done.1
  58.4 0.3 copy.52
  58.7 1.2 bitcast_select_fusion.1.dout_ref
  59.9 35.6 %shard_map.444 = (bf16[512,1024]{1,0:T(8,128)(2,1)}, f32[512,1024]{1,0:T(8,128)}, bf16[1024,4096]{1,0:T(8,128)(2,1)}, bf16[4096,1024]{1,0:T(8,128)(2,1)}, f32[1,4096]{1,0:T(1,128)}, /*index=5*/f32[1,1024]{1,0:T(1,128)}) custom-call(bf16[512,1024]{1,0:T(8,128)(2,1)} %bitcast.53, bf16[512,1024]{1,0:T(8,128)(2,1)} %bitcast_select_fusion.1.dout_ref, ...), custom_call_target="tpu_custom_call" | custom-call | tf_op jit(solution)/shard_map/pallas_call | solution.py:189
  95.5 1.2 bitcast_select_fusion.refs_14_
  96.6 0.6 broadcast_in_dim.59.refs_35_
  97.2 265.0 %shard_map.445 = (f32[128,1024]{1,0:T(8,128)}, f32[64,4096]{1,0:T(8,128)}, f32[256,1024]{1,0:T(8,128)}, f32[64,1024]{1,0:T(8,128)}, f32[64,1024]{1,0:T(8,128)}, ...) custom-call(bf16[8,2,64,4096]{3,2,1,0:T(8,128)(2,1)} %bitcast.46, ...), custom_call_target="tpu_custom_call" | custom-call | tf_op jit(solution)/shard_map/pallas_call | solution.py:1585
  362.3 0.0 copy-start
  362.3 6.2 %shard_map.446 = (f32[128,1024]{1,0:T(8,128)}, f32[64,4096]{1,0:T(8,128)}, f32[256,1024]{1,0:T(8,128)}, f32[64,1024]{1,0:T(8,128)}, f32[64,1024]{1,0:T(8,128)}, ...) custom-call(f32[128,1024]{1,0:T(8,128)} %get-tuple-element.100.refs_, ...), custom_call_target="tpu_custom_call" | custom-call | tf_op jit(solution)/shard_map/pallas_call | solution.py:593
  368.5 1.7 fusion.6
  370.2 1.3 slice_bitcast_fusion
  371.5 0.0 copy-done
  371.5 1.8 fusion
  373.3 1.7 slice.45
  (3 shorter events, 0.0 us)
Async XLA Ops:
  43.4 15.0 %copy-start.1 = (bf16[2,64,4,1024]{3,2,1,0:T(4,128)(2,1)S(1)}, bf16[2,64,4,1024]{3,2,1,0:T(4,128)(2,1)}, u32[]{:S(2)}) copy-start(bf16[2,64,4,1024]{3,2,1,0:T(4,128)(2,1)} %param.53) | copy-start | bytes 3145732
  362.3 9.2 %copy-start = (bf16[512,1024]{1,0:T(8,128)(2,1)S(1)}, bf16[512,1024]{1,0:T(8,128)(2,1)}, u32[]{:S(2)}) copy-start(bf16[512,1024]{1,0:T(8,128)(2,1)} %get-tuple-element.80) | copy-start | bytes 3145732

commit v8 on v7

--- a/solution.py
+++ b/solution.py
@@ -120,7 +120,7 @@
 def local_front(x, params):
     places, frames, width = x.shape
     pairs = places * (places + 1) // 2
-    step = 64
+    step = frames
     rows = pl.BlockSpec((places, step, width), lambda i: (0, i, 0))
     whole = lambda item: pl.BlockSpec(item.shape, lambda i: (0, 0), pipeline_mode=pl.Buffered(1))
     n1, n2 = params[0].reshape(1, -1), params[5].reshape(1, -1)
@@ -363,7 +363,7 @@
 def attend_kernel(
     count, x_ref, mask_ref, n1_ref, wq_ref, wk_ref, wv_ref, codes_ref, valid_ref, n2_ref, b1_ref,
     b2_ref, table_ref, wo_ref, w1_ref, w2_ref,
-    normed_ref, mixed_ref, saved_ref, log_ref, local_ref, mid_ref, hn_ref, u_ref, act_ref,
+    normed_ref, mixed_ref, saved_ref, log_ref, local_ref, mid_ref, hn_ref, u_ref, act_ref, out_ref,
     packed, held, mixed_all, pieces, bias, v_t, table, wo, w1, w2,
     send_sem, recv_sem, send_two, recv_two, save_sem, fetch_sem,
 ):
@@ -413,7 +413,7 @@
     fetches[0].wait()
     vocab = table.shape[0] // CB
     for book in range(CB):
-        ids = jnp.broadcast_to(codes_ref[book][:, 0:1], (rows, vocab))
+        ids = jnp.broadcast_to(codes_ref[:, book : book + 1], (rows, vocab))
         picked = (ids == lax.broadcasted_iota(jnp.int32, (rows, vocab), 1)).astype(LOW)
         local_ref[1 + book] = mul(picked, table[book * vocab : (book + 1) * vocab]).astype(LOW)
 
@@ -503,7 +503,9 @@
         u_ref[:, cols] = u
         act_ref[:, cols] = act
         result = result + mul(act, w2[cols])
-    local_ref[0] = jnp.where(valid_ref[...] > 0, result, 0.0).astype(LOW)
+    result = jnp.where(valid_ref[...] > 0, result, 0.0).astype(LOW)
+    local_ref[0] = result
+    out_ref[...] = result
 
     @pl.loop(1, count)
     def _(step):
@@ -529,7 +531,7 @@
     return pl.pallas_call(
         functools.partial(attend_kernel, count),
         in_specs=[vmem] * 11 + [hbm] * 4,
-        out_specs=[vmem, vmem, hbm] + [vmem] * 6,
+        out_specs=[vmem, vmem, hbm] + [vmem] * 7,
         out_shape=[
             jax.ShapeDtypeStruct((rows, width), LOW),
             jax.ShapeDtypeStruct((rows, width), LOW),
@@ -540,6 +542,7 @@
             jax.ShapeDtypeStruct((rows, width), LOW),
             jax.ShapeDtypeStruct((rows, wide), F32),
             jax.ShapeDtypeStruct((rows, wide), LOW),
+            jax.ShapeDtypeStruct((rows, width), LOW),
         ],
         scratch_shapes=[
             pltpu.VMEM((utts, 208, width), LOW),
@@ -762,11 +765,12 @@
 )
 SLABS = 55
 LOADED = 16
-AT_HIDDEN = 8
-AT_BACK = 16
-AT_ATTEND = 23
-AT_RETURN = 31
-AT_LANDED = 47
+AT_LOCAL = 7
+AT_HIDDEN = 16
+AT_BACK = 20
+AT_ATTEND = 27
+AT_RETURN = 35
+AT_LANDED = 45
 PART = 32
 
 
@@ -796,33 +800,32 @@
 
     def load_start(slab):
         slot = slab % SLOTS
-        for ref, spec in ((r.l_up, PLAN[0]), (r.l_down, PLAN[1])):
-
-            @pl.when((slab >= spec[0]) & (slab < spec[0] + spec[1]))
-            def _():
-                for side in range(2):
-                    pltpu.make_async_copy(
-                        window(ref, spec, slab, (slice(None), side)),
-                        r.part.at[slot, side],
-                        r.load_sem.at[slot, side],
-                    ).start()
+
+        @pl.when((slab >= PLAN[1][0]) & (slab < LOADED))
+        def _():
+            for side in range(2):
+                pltpu.make_async_copy(
+                    window(r.l_down, PLAN[1], slab, (slice(None), side)),
+                    r.part.at[slot, side],
+                    r.load_sem.at[slot, side],
+                ).start()
 
     def load_wait(slot):
         for side in range(2):
             pltpu.make_async_copy(
-                r.l_up.at[:, side, pl.ds(0, SROWS), pl.ds(0, SCOLS)],
+                r.l_down.at[:, side, pl.ds(0, SROWS), pl.ds(0, SCOLS)],
                 r.part.at[slot, side],
                 r.load_sem.at[slot, side],
             ).wait()
 
-    def weights(block, slot):
+    def weights(block, slot, up=r.g_w_up, down=r.g_w_down):
         start = block * SCOLS if isinstance(block, int) else pl.multiple_of(block * SCOLS, SCOLS)
         return (
             pltpu.make_async_copy(
-                r.g_w_up.at[:, pl.ds(start, SCOLS)], r.up_buf.at[slot], r.weight_sem.at[slot, 0]
+                up.at[:, pl.ds(start, SCOLS)], r.up_buf.at[slot], r.weight_sem.at[slot, 0]
             ),
             pltpu.make_async_copy(
-                r.g_w_down.at[pl.ds(start, SCOLS)], r.down_buf.at[slot], r.weight_sem.at[slot, 1]
+                down.at[pl.ds(start, SCOLS)], r.down_buf.at[slot], r.weight_sem.at[slot, 1]
             ),
         )
 
@@ -831,7 +834,8 @@
         (r.g_w_v, r.square.at[3]), (r.saved, r.held), (r.l_normed, r.l_x.at[0]),
         (r.l_mixed, r.l_x.at[1]), (r.g_act, r.act_buf), (r.g_mixed, r.g_x.at[0]),
         (r.g_normed, r.g_x.at[1]), (r.l_w_o, r.square.at[0]), (r.l_w_q, r.square.at[1]),
-        (r.l_w_k, r.square.at[2]), (r.l_w_v, r.square.at[3]),
+        (r.l_w_k, r.square.at[2]), (r.l_w_v, r.square.at[3]), (r.l_hn, r.l_x.at[0]),
+        (r.l_dout_flat, r.l_x.at[1]), (r.l_mid_flat, r.l_acc),
     )
 
     def fetch(*which):
@@ -842,7 +846,7 @@
     def local_rows(step, slot):
         rows = pl.ds(step * PART if isinstance(step, int) else pl.multiple_of(step * PART, PART), PART)
         pairs = (
-            (r.l_in, r.l_in_buf), (r.l_mid, r.l_mid_buf), (r.l_dhn, r.l_dhn_buf),
+            (r.l_in, r.l_in_buf), (r.l_mid, r.l_mid_buf),
             (r.l_dout, r.l_dout_buf), (r.l_q, r.l_q_buf), (r.l_k, r.l_k_buf), (r.l_v, r.l_v_buf),
             (r.l_probs, r.l_probs_buf),
         )
@@ -851,8 +855,14 @@
             for index, (ref, buffer) in enumerate(pairs)
         ]
 
-    load_start(0)
-    for copy in local_rows(0, 0) + fetch(10, 11, 12, 13):
+    def local_weights(block, slot):
+        return weights(block, slot, r.l_w_up, r.l_w_down)
+
+    def kept(block, slot):
+        return pltpu.make_async_copy(r.l_kept.at[slot], r.l_down.at[block], r.kept_sem.at[slot])
+
+    result = pltpu.make_async_copy(r.l_x.at[0], r.y, r.result_sem.at[0])
+    for copy in tuple(fetch(14, 15, 16)) + local_weights(0, 0):
         copy.start()
 
     def send(kind, slot, source, target, device):
@@ -949,7 +959,7 @@
         slab, slot, _, guard, _ = stage(0)
         load_start(slab + 1)
 
-        @pl.when(slab < LOADED)
+        @pl.when((slab >= PLAN[1][0]) & (slab < LOADED))
         def _():
             load_wait(slot)
 
@@ -1204,14 +1214,65 @@
                 hit = hit | (tick == item)
             return pl.when(hit)
 
-        @pl.when((tick < 8) & (tick % 2 == 0))
-        def _():
-            step = tick // 2
-            slot = step % 2
+        @at(-1)
+        def _():
+            for copy in fetch(14, 15, 16):
+                copy.wait()
+            r.l_x_t[...] = r.l_x[0].T
+            r.l_acc[...] += r.l_b2[...]
+            r.l_dhn[...] = jnp.zeros_like(r.l_dhn)
+
+        @pl.when(tick < AT_LOCAL)
+        def _():
+            block = tick + 1
+            slot = block % 2
+            for copy in local_weights(block, slot):
+                copy.wait()
+
+            @pl.when(block < 7)
+            def _():
+                for copy in local_weights(block + 1, 1 - slot):
+                    copy.start()
+
+            @pl.when(block >= 2)
+            def _():
+                kept(block - 2, slot).wait()
+
+            cols = cols_of(block)
+            u = mul(r.l_x[0], r.up_buf[slot]) + r.l_b1[:, cols]
+            act, slope = gelu_parts(u)
+            act = act.astype(LOW)
+            r.l_acc[...] += mul(act, r.down_buf[slot])
+            du = (mul_t(r.l_x[1], r.down_buf[slot]) * slope).astype(LOW)
+            r.l_db1[:, cols] = jnp.sum(du.astype(F32), axis=0, keepdims=True)
+            r.l_dhn[...] += mul_t(du, r.up_buf[slot])
+            put_product(block % SLOTS, quarter_rows(r.l_x_t), du)
+            r.l_kept[slot] = t_mul(act, r.l_x[1]).astype(LOW).reshape(r.l_kept.shape[1:])
+            kept(block, slot).start()
+
+        @at(1)
+        def _():
+            for copy in local_rows(0, 0) + fetch(10, 11, 12, 13):
+                copy.start()
+
+        @at(AT_LOCAL - 1)
+        def _():
+            kept(6, 0).wait()
+            kept(7, 1).wait()
+            r.l_db2[...] = jnp.sum(r.l_x[1].astype(F32), axis=0, keepdims=True)
+            r.l_x[0] = r.l_acc[...].astype(LOW)
+            result.start()
+
+        since = tick - AT_LOCAL
+        step = since // 2
+        slot = step % 2
+
+        @pl.when((since >= 0) & (since < 8) & (since % 2 == 0))
+        def _():
             for copy in local_rows(step, slot):
                 copy.wait()
 
-            @pl.when(tick == 0)
+            @pl.when(since == 0)
             def _():
                 for copy in fetch(10):
                     copy.wait()
@@ -1223,18 +1284,24 @@
                 for copy in local_rows(step + 1, 1 - slot):
                     copy.start()
 
+            local_hidden_back(r, step, slot)
             local_attend_back(r, step, slot)
 
-        @pl.when((tick < 8) & (tick % 2 == 1))
-        def _():
-            @pl.when(tick == 1)
+        @pl.when((since >= 0) & (since < 8) & (since % 2 == 1))
+        def _():
+            @pl.when(since == 1)
             def _():
                 for copy in fetch(11, 12, 13):
                     copy.wait()
 
-            local_project_back(r, tick // 2, (tick // 2) % 2)
-
-        @at(6)
+            local_project_back(r, step)
+            local_input_back(r, step, slot)
+
+        @at(9)
+        def _():
+            result.wait()
+
+        @at(10)
         def _():
             for copy in weights(0, 0) + tuple(fetch(4, 5, 6)):
                 copy.start()
@@ -1246,26 +1313,28 @@
             r.dout_low[...] = r.dout[...].astype(LOW)
             r.dhn[...] = jnp.zeros_like(r.dhn)
 
-        @pl.when((tick >= AT_HIDDEN) & (tick < AT_HIDDEN + 8))
-        def _():
-            block = tick - AT_HIDDEN
-            slot = block % 2
-            for copy in weights(block, slot):
-                copy.wait()
-
-            @pl.when(block < 7)
-            def _():
-                for copy in weights(block + 1, 1 - slot):
-                    copy.start()
-
-            cols = cols_of(block)
-            _, slope = gelu_parts(r.u[:, cols])
-            du = (mul_t(r.dout_low[...], r.down_buf[slot]) * slope).astype(LOW)
-            r.du[:, cols] = du
-            r.db1[pl.ds(block, 1), :] = jnp.sum(du.astype(F32), axis=0, keepdims=True)
-            r.dhn[...] += mul_t(du, r.up_buf[slot])
-
-        @at(13)
+        @pl.when((tick >= AT_HIDDEN) & (tick < AT_HIDDEN + 4))
+        def _():
+            @pl.loop(0, 2)
+            def _(index):
+                block = 2 * (tick - AT_HIDDEN) + index
+                slot = block % 2
+                for copy in weights(block, slot):
+                    copy.wait()
+
+                @pl.when(block < 7)
+                def _():
+                    for copy in weights(block + 1, 1 - slot):
+                        copy.start()
+
+                cols = cols_of(block)
+                _, slope = gelu_parts(r.u[:, cols])
+                du = (mul_t(r.dout_low[...], r.down_buf[slot]) * slope).astype(LOW)
+                r.du[:, cols] = du
+                r.db1[pl.ds(block, 1), :] = jnp.sum(du.astype(F32), axis=0, keepdims=True)
+                r.dhn[...] += mul_t(du, r.up_buf[slot])
+
+        @at(15)
         def _():
             for copy in fetch(4, 5, 6):
                 copy.wait()
@@ -1334,9 +1403,13 @@
         def _():
             r.landed[:, own_utt, :, own_cols] = r.pieces[seq]
 
-        @pl.when((tick >= AT_RETURN) & (tick < AT_RETURN + 15))
-        def _():
-            hand_back(lax.rem(seq + tick - AT_RETURN + 1, count)).start()
+        @pl.when((tick >= AT_RETURN) & (tick < AT_RETURN + 8))
+        def _():
+            hand_back(lax.rem(seq + 2 * (tick - AT_RETURN) + 1, count)).start()
+
+        @pl.when((tick >= AT_RETURN) & (tick < AT_RETURN + 7))
+        def _():
+            hand_back(lax.rem(seq + 2 * (tick - AT_RETURN) + 2, count)).start()
 
         @at(AT_LANDED)
         def _():
@@ -1391,14 +1464,15 @@
 
     pl.semaphore_wait(barrier, count)
 
-    @pl.loop(0, SLABS + DRAIN)
-    def _(tick):
+    @pl.loop(0, SLABS + DRAIN + 1)
+    def _(index):
+        tick = index - 1
         advance(tick)
         compute(tick)
         produce(tick + 1)
 
 
-def local_attend_back(r, step, slot):
+def local_hidden_back(r, step, slot):
     places, width = r.l_in_buf.shape[1], r.l_in_buf.shape[3]
     frames = r.l_in.shape[1]
     rows = places * PART
@@ -1407,7 +1481,17 @@
         return pl.ds(pl.multiple_of(place * frames + step * PART, PART), PART)
 
     mid = r.l_mid_buf[slot].reshape(rows, width)
-    dmid, gain = scale_back(mid, r.l_n2[...], r.l_dhn_buf[slot].reshape(rows, width))
+    dmid, gain = scale_back(
+        mid,
+        r.l_n2[...],
+        jnp.concatenate(
+            [
+                r.l_dhn[pl.ds(pl.multiple_of(place * frames + step * PART, PART), PART)]
+                for place in range(places)
+            ],
+            axis=0,
+        ),
+    )
     r.l_dn2[...] += jnp.sum(gain, axis=0, keepdims=True)
     dmid = dmid + r.l_dout_buf[slot].astype(F32).reshape(rows, width)
     r.l_dmid[...] = dmid
@@ -1415,6 +1499,15 @@
     for place in range(places):
         r.l_g[3, rows_of(place)] = dattn[place * PART : (place + 1) * PART]
     r.l_dmix[...] = mul_t(dattn, r.square[0]).astype(LOW).reshape(places, PART, width)
+
+
+def local_attend_back(r, step, slot):
+    places, width = r.l_in_buf.shape[1], r.l_in_buf.shape[3]
+    frames = r.l_in.shape[1]
+
+    def rows_of(place):
+        return pl.ds(pl.multiple_of(place * frames + step * PART, PART), PART)
+
     sums, spread = head_sums(width), head_spread(width)
     add = lambda old, term: term if old is None else old + term
     pair = 0
@@ -1440,10 +1533,9 @@
         r.l_g[2, rows_of(j)] = dv[j].astype(LOW)
 
 
-def local_project_back(r, step, slot):
-    places, width = r.l_in_buf.shape[1], r.l_in_buf.shape[3]
+def local_project_back(r, step):
+    places = r.l_in_buf.shape[1]
     frames = r.l_in.shape[1]
-    rows = places * PART
     dnormed = None
     for kind in range(3):
         grad = jnp.concatenate(
@@ -1455,8 +1547,14 @@
         )
         term = mul_t(grad, r.square[1 + kind])
         dnormed = term if dnormed is None else dnormed + term
+    r.l_dnormed[...] = dnormed
+
+
+def local_input_back(r, step, slot):
+    places, width = r.l_in_buf.shape[1], r.l_in_buf.shape[3]
+    rows = places * PART
     x = r.l_in_buf[slot].astype(F32).reshape(rows, width)
-    dx, gain = scale_back(x, r.l_n1[...], dnormed)
+    dx, gain = scale_back(x, r.l_n1[...], r.l_dnormed[...])
     r.l_dn1[...] += jnp.sum(gain, axis=0, keepdims=True)
     dx = dx + r.l_dmid[...]
     here = pl.ds(pl.multiple_of(step * PART, PART), PART)
@@ -1506,7 +1604,7 @@
         (width // 16, wide), (width // 16, width), (width // 16, width), (width // 16, width),
         (width // 16, width), (SROWS, SCOLS),
     ]
-    out_names = ["dx"] + ["out_%d" % index for index in range(len(shapes))]
+    out_names = ["dx", "y", "l_down"] + ["out_%d" % index for index in range(len(shapes))]
     rows_l = far["l_normed"].shape[0]
     places, pairs = far["l_in"].shape[0], far["l_probs"].shape[0]
     buffers = dict(
@@ -1542,13 +1640,18 @@
         l_x_t=((width, rows_l), LOW),
         l_in_buf=((2, places, PART, width), LOW),
         l_mid_buf=((2, places, PART, width), F32),
-        l_dhn_buf=((2, places, PART, width), F32),
+        l_acc=((rows_l, width), F32),
+        l_dhn=((rows_l, width), F32),
+        l_kept=((2, 2, wide // 16, width), LOW),
+        l_db1=((1, wide), F32),
+        l_db2=((1, width), F32),
         l_dout_buf=((2, places, PART, width), LOW),
         l_q_buf=((2, places, PART, width), LOW),
         l_k_buf=((2, places, PART, width), LOW),
         l_v_buf=((2, places, PART, width), LOW),
         l_probs_buf=((2, pairs, PART, LANES), F32),
         l_dmid=((places * PART, width), F32),
+        l_dnormed=((places * PART, width), F32),
         l_dmix=((places, PART, width), LOW),
         l_dn1=((1, width), F32),
         l_dn2=((1, width), F32),
@@ -1578,20 +1681,24 @@
     )
     semaphores = dict(
         load_sem=(SLOTS, 2), out_sem=(SLOTS,), send_sem=(26, SLOTS), recv_sem=(26, SLOTS),
-        weight_sem=(2, 2), fetch_sem=(14,), local_sem=(2, 8), send_one=(16,), recv_one=(16,), send_two=(16,),
+        weight_sem=(2, 2), fetch_sem=(17,), local_sem=(2, 7), kept_sem=(2,), result_sem=(1,), send_one=(16,), recv_one=(16,), send_two=(16,),
         recv_two=(16,),
     )
     names = list(far) + list(near) + out_names + list(buffers) + list(semaphores)
     return pl.pallas_call(
         functools.partial(tail_kernel, names, len(shapes)),
         in_specs=[hbm] * len(far) + [vmem] * len(near),
-        out_specs=[vmem] + [hbm] * len(shapes),
-        out_shape=[jax.ShapeDtypeStruct((rows, width), F32)]
+        out_specs=[vmem] + [hbm] * (2 + len(shapes)),
+        out_shape=[
+            jax.ShapeDtypeStruct((rows, width), F32),
+            jax.ShapeDtypeStruct((rows_l, width), LOW),
+            jax.ShapeDtypeStruct((8, 2, wide // 16, width), LOW),
+        ]
         + [jax.ShapeDtypeStruct(shape, F32) for shape in shapes],
         scratch_shapes=[pltpu.VMEM(*item) for item in buffers.values()]
         + [pltpu.SemaphoreType.DMA(item) for item in semaphores.values()],
         compiler_params=pltpu.CompilerParams(
-            collective_id=1, has_side_effects=True, vmem_limit_bytes=62 << 20
+            collective_id=1, has_side_effects=True, vmem_limit_bytes=63 << 20
         ),
     )(*far.values(), *near.values())
 
@@ -1719,16 +1826,15 @@
     code_rows = codes.transpose(2, 0, 1).reshape(CB, row_count)
     (
         glob_normed, glob_mixed, saved, log_total, local_in,
-        glob_middle, glob_middle_norm, pre_active, active,
+        glob_middle, glob_middle_norm, pre_active, active, global_rows,
     ) = global_forward(
         frames,
         usable,
-        jnp.broadcast_to(code_rows[:, :, None], (CB, row_count, LANES)),
+        codes.reshape(row_count, CB),
         valid.reshape(row_count, 1).astype(F32),
         table,
         glob_params,
     )
-    global_rows = local_in[0]
     local_shape = (local_len, row_count, model_width)
     flat_shape = (local_len * row_count, model_width)
     normed, local_q, local_k, local_v, local_probs, mixed, middle, middle_norm = local_front(
@@ -1737,23 +1843,21 @@
     row_valid = valid.reshape(1, row_count, 1)
     local_cotan = cotan_local.transpose(2, 0, 1, 3).reshape(local_shape)
     local_cotan = jnp.where(row_valid, local_cotan, 0)
-    local_result, grad_hidden, grad_w_up, grad_w_down, grad_b_up, grad_b_down = local_ffn(
-        middle_norm.reshape(flat_shape),
-        local_cotan.reshape(flat_shape),
-        middle.reshape(flat_shape),
-        local_params,
-    )
-    local_rows = jnp.where(row_valid, local_result.reshape(local_shape), 0)
-    local_rows = local_rows.reshape(local_len, utter_count, frame_count, model_width)
-    local_rows = local_rows.transpose(1, 2, 0, 3)
+
+    def by_frame(result):
+        result = jnp.where(row_valid, result.reshape(local_shape), 0)
+        result = result.reshape(local_len, utter_count, frame_count, model_width)
+        return result.transpose(1, 2, 0, 3)
+
     normed = normed.reshape(flat_shape)
     mixed = mixed.reshape(flat_shape)
-    outputs = (global_rows.reshape(utter_count, frame_count, model_width), local_rows)
-
     if lax.axis_size("seq") == 16 and lax.axis_size("utt") == 2:
         far = dict(
-            l_up=grad_w_up.reshape(8, 2, -1, grad_w_up.shape[1]),
-            l_down=grad_w_down.reshape(8, 2, -1, grad_w_down.shape[1]),
+            l_w_up=local_w_up,
+            l_w_down=local_w_down,
+            l_hn=middle_norm.reshape(flat_shape),
+            l_dout_flat=local_cotan.reshape(flat_shape),
+            l_mid_flat=middle.reshape(flat_shape),
             g_w_up=glob_w_up,
             g_w_down=glob_w_down,
             g_w_o=glob_w_output,
@@ -1765,7 +1869,6 @@
             l_mixed=mixed,
             l_in=local_in,
             l_mid=middle,
-            l_dhn=grad_hidden.reshape(local_shape),
             l_dout=local_cotan,
             l_q=local_q,
             l_k=local_k,
@@ -1792,10 +1895,11 @@
             codes=jnp.broadcast_to(code_rows[:, None, :], (CB, 8, row_count)),
             l_n1=local_norm_one.reshape(1, -1),
             l_n2=local_norm_two.reshape(1, -1),
-            l_db1=grad_b_up,
-            l_db2=grad_b_down,
+            l_b1=local_b_up.reshape(1, -1),
+            l_b2=local_b_down.reshape(1, -1),
         )
-        grad_inputs, *sums = settle(finish_on_slice(far, near))
+        grad_inputs, local_result, _, *sums = finish_on_slice(far, near)
+        grad_inputs, *sums = settle([grad_inputs] + sums)
         wide = dict(zip("12qkvot76pabc", sums[:-1]))
         half = lax.axis_index("seq") % 2
         rest = sums[-1]
@@ -1806,7 +1910,9 @@
         def piece_wide(row):
             return rest[row : row + 2, ACOLS:].reshape(-1)
 
-        return outputs + (
+        return (
+            global_rows.reshape(utter_count, frame_count, model_width),
+            by_frame(local_result),
             grad_inputs.reshape(utter_count, frame_count, model_width),
             wide["t"],
             piece(0),
@@ -1831,6 +1937,12 @@
             piece(7),
         )
 
+    local_result, grad_hidden, grad_w_up, grad_w_down, grad_b_up, grad_b_down = local_ffn(
+        middle_norm.reshape(flat_shape),
+        local_cotan.reshape(flat_shape),
+        middle.reshape(flat_shape),
+        local_params,
+    )
     grad_attn, grad_q, grad_k, grad_v, grad_first, grad_rest, grad_n1, grad_n2 = local_back(
         local_in,
         middle,
@@ -1876,7 +1988,11 @@
         global_in, glob_normed, glob_mixed, glob_kept, glob_params, glob_cotan, global_back
     )
     reduced = reduce_all((grad_tab,) + glob_grads + local_grads)
-    return outputs + (grad_inputs.reshape(utter_count, frame_count, model_width),) + reduced
+    return (
+        global_rows.reshape(utter_count, frame_count, model_width),
+        by_frame(local_result),
+        grad_inputs.reshape(utter_count, frame_count, model_width),
+    ) + reduced
 
 
 def solution(mesh):

time: 375 us -> 359 us (0.957)
  Pallas kernels: 360 us -> 341 us
    pallas_call x1 -> x0, Pallas kernels: 35.6 us -> none  [local_ffn(): pl.pallas_call(ffn_kernel, grid=(wide // step,), in_specs=[whole, whole,...]
    pallas_call x1, Pallas kernels: 265 us -> 283 us  [finish_on_slice(): pl.pallas_call(functools.partial(tail_kernel, names, len(shapes)), in_spe...]
where the time goes in v8:
time: 359 us; the launch traced here: 358 us
  Pallas kernels  341 us (95%)
  other arithmetic  8.58 us (2%)
  local copies, waits for them, and re-layouts  7.77 us (2%)
    pallas_call x1, Pallas kernels, finish_on_slice(): pl.pallas_call(functools.partial(tail_kernel, names, len(shapes)), in_spe...  283 us
    pallas_call x1, Pallas kernels, global_forward(): pl.pallas_call(functools.partial(attend_kernel, count), in_specs=[vmem] *...  38.7 us
    pallas_call x1, Pallas kernels, local_front(): pl.pallas_call(front_kernel, grid=(frames // step,), in_specs=[rows] + [w...  13.2 us

profile of v8, /device:TPU:0, one launch (start us, length us, event | category | flops | bytes accessed | tf_op | source)
XLA Modules:
  0.0 358.1 jit_solution(11838196139459313839)
XLA Ops:
  0.7 0.7 convert_element_type.14
  1.4 0.7 fusion.7
  2.1 0.1 lt.39
  2.2 0.8 broadcast_in_dim.51
  3.0 0.6 broadcast_in_dim.43.mask_ref
  3.6 0.6 broadcast_in_dim.52.refs_37_
  4.2 0.8 reshape.210.valid_ref.refs_30_
  4.9 1.4 copy.51
  6.4 1.5 copy.53
  7.9 1.2 bitcast_select_fusion.refs_16_
  9.1 1.2 bitcast_select_fusion.1.refs_3_
  10.3 38.7 %shard_map.442 = (bf16[128,1024]{1,0:T(8,128)(2,1)}, bf16[128,1024]{1,0:T(8,128)(2,1)}, bf16[16,208,128]{2,1,0:T(8,128)(2,1)}, f32[16,8,128]{2,1,0:T(8,128)}, bf...) custom-call(bf16[2,64,1024]{2,1,0:T(8,128)(2,1)} %x_ref.1, ...), custom_call_target="tpu_custom_call" | custom-call | tf_op jit(solution)/shard_map/pallas_call | solution.py:531
  49.0 13.2 %shard_map.443 = (bf16[4,128,1024]{2,1,0:T(8,128)(2,1)}, bf16[4,128,1024]{2,1,0:T(8,128)(2,1)}, bf16[4,128,1024]{2,1,0:T(8,128)(2,1)}, bf16[4,128,1024]{2,1,0:T(...) custom-call(bf16[4,128,1024]{2,1,0:T(8,128)(2,1)} %get-tuple-element, ...), custom_call_target="tpu_custom_call" | custom-call | tf_op jit(solution)/shard_map/pallas_call | solution.py:129
  62.2 283.0 %shard_map.444 = (f32[128,1024]{1,0:T(8,128)}, bf16[512,1024]{1,0:T(8,128)(2,1)}, bf16[8,2,256,1024]{3,2,1,0:T(8,128)(2,1)}, f32[64,4096]{1,0:T(8,128)}, f32[256...) custom-call(bf16[1024,4096]{1,0:T(8,128)(2,1)} %refs_0_.1, ...), custom_call_target="tpu_custom_call" | custom-call | tf_op jit(solution)/shard_map/pallas_call | solution.py:1688
  345.2 3.1 fusion
  348.3 0.0 copy-start
  348.3 6.1 %shard_map.445 = (f32[128,1024]{1,0:T(8,128)}, f32[64,4096]{1,0:T(8,128)}, f32[256,1024]{1,0:T(8,128)}, f32[64,1024]{1,0:T(8,128)}, f32[64,1024]{1,0:T(8,128)}, ...) custom-call(f32[128,1024]{1,0:T(8,128)} %get-tuple-element.92.refs_0, ...), custom_call_target="tpu_custom_call" | custom-call | tf_op jit(solution)/shard_map/pallas_call | solution.py:596
  354.4 1.3 slice_bitcast_fusion
  355.7 1.7 fusion.6
  357.4 0.0 copy-done
  357.4 0.7 copy.61
  (3 shorter events, 0.0 us)
Async XLA Ops:
  348.3 9.1 %copy-start = (bf16[128,1024]{1,0:T(8,128)(2,1)S(1)}, bf16[128,1024]{1,0:T(8,128)(2,1)}, u32[]{:S(2)}) copy-start(bf16[128,1024]{1,0:T(8,128)(2,1)} %get-tuple-element.73) | copy-start | bytes 786436

commit v9 on v8

--- a/solution.py
+++ b/solution.py
@@ -1842,7 +1842,7 @@
     )
     row_valid = valid.reshape(1, row_count, 1)
     local_cotan = cotan_local.transpose(2, 0, 1, 3).reshape(local_shape)
-    local_cotan = jnp.where(row_valid, local_cotan, 0)
+    local_cotan = lax.optimization_barrier(jnp.where(row_valid, local_cotan, 0))
 
     def by_frame(result):
         result = jnp.where(row_valid, result.reshape(local_shape), 0)

time: 359 us -> 357 us (level)
  no operation moved by 1% of the time
where the time goes in v9:
time: 357 us
  Pallas kernels  341 us (96%)
  local copies, waits for them, and re-layouts  7.76 us (2%)
  other arithmetic  7.4 us (2%)
    pallas_call x1, Pallas kernels, finish_on_slice(): pl.pallas_call(functools.partial(tail_kernel, names, len(shapes)), in_spe...  283 us
    pallas_call x1, Pallas kernels, global_forward(): pl.pallas_call(functools.partial(attend_kernel, count), in_specs=[vmem] *...  38.7 us
    pallas_call x1, Pallas kernels, local_front(): pl.pallas_call(front_kernel, grid=(frames // step,), in_specs=[rows] + [w...  13.1 us

profile of v9, /device:TPU:0, one launch (start us, length us, event | category | flops | bytes accessed | tf_op | source)
XLA Modules:
  0.0 356.7 jit_solution(12214992468324657041)
XLA Ops:
  0.7 0.7 convert_element_type.14
  1.4 0.7 fusion.7
  2.1 0.1 lt.39
  2.2 0.8 broadcast_in_dim.39
  3.0 0.6 broadcast_in_dim.35.mask_ref
  3.6 0.6 broadcast_in_dim.40.refs_37_
  4.2 0.8 reshape.208.valid_ref.refs_30_
  4.9 1.4 copy.51
  6.3 1.5 copy.53
  7.9 1.2 bitcast_select_fusion.refs_16_
  9.1 38.7 %shard_map.442 = (bf16[128,1024]{1,0:T(8,128)(2,1)}, bf16[128,1024]{1,0:T(8,128)(2,1)}, bf16[16,208,128]{2,1,0:T(8,128)(2,1)}, f32[16,8,128]{2,1,0:T(8,128)}, bf...) custom-call(bf16[2,64,1024]{2,1,0:T(8,128)(2,1)} %x_ref.1, ...), custom_call_target="tpu_custom_call" | custom-call | tf_op jit(solution)/shard_map/pallas_call | solution.py:531
  47.8 13.1 %shard_map.443 = (bf16[4,128,1024]{2,1,0:T(8,128)(2,1)}, bf16[4,128,1024]{2,1,0:T(8,128)(2,1)}, bf16[4,128,1024]{2,1,0:T(8,128)(2,1)}, bf16[4,128,1024]{2,1,0:T(...) custom-call(bf16[4,128,1024]{2,1,0:T(8,128)(2,1)} %get-tuple-element, ...), custom_call_target="tpu_custom_call" | custom-call | tf_op jit(solution)/shard_map/pallas_call | solution.py:129
  60.8 283.0 %shard_map.444 = (f32[128,1024]{1,0:T(8,128)}, bf16[512,1024]{1,0:T(8,128)(2,1)}, bf16[8,2,256,1024]{3,2,1,0:T(8,128)(2,1)}, f32[64,4096]{1,0:T(8,128)}, f32[256...) custom-call(bf16[1024,4096]{1,0:T(8,128)(2,1)} %refs_0_.1, ...), custom_call_target="tpu_custom_call" | custom-call | tf_op jit(solution)/shard_map/pallas_call | solution.py:1688
  343.8 3.1 fusion
  346.9 0.0 copy-start
  346.9 6.1 %shard_map.445 = (f32[128,1024]{1,0:T(8,128)}, f32[64,4096]{1,0:T(8,128)}, f32[256,1024]{1,0:T(8,128)}, f32[64,1024]{1,0:T(8,128)}, f32[64,1024]{1,0:T(8,128)}, ...) custom-call(f32[128,1024]{1,0:T(8,128)} %get-tuple-element.92.refs_0, ...), custom_call_target="tpu_custom_call" | custom-call | tf_op jit(solution)/shard_map/pallas_call | solution.py:596
  353.0 1.3 slice_bitcast_fusion
  354.3 1.7 fusion.6
  356.0 0.0 copy-done
  356.0 0.7 copy.60
  (2 shorter events, 0.0 us)
Async XLA Ops:
  346.9 9.1 %copy-start = (bf16[128,1024]{1,0:T(8,128)(2,1)S(1)}, bf16[128,1024]{1,0:T(8,128)(2,1)}, u32[]{:S(2)}) copy-start(bf16[128,1024]{1,0:T(8,128)(2,1)} %get-tuple-element.73) | copy-start | bytes 786436
